TPU v7x, 32 devices: a whole 2x2x4 slice. The times are simulated.
32 devices in a mesh: grp: 4 (over y, x), dev: 8 (over z, core).
Axes of the slice: x: 2, y: 2, z: 4, core: 2. Of those that a mesh axis runs over, the one named last changes fastest.
Arguments:
- captions: bfloat16 [8, 64, 4096], P('dev', 'grp'), may hold values from -6 to 6
- kv_weight: bfloat16 [4096, 2048], P('grp'), may hold values from -0.09375 to 0.09375
- image_tokens: bfloat16 [128, 256, 2048], P(('grp', 'dev')), may hold values from -28 to 28
- q_weight: bfloat16 [2048, 1024], replicated, may hold values from -0.125 to 0.125
- context_grad: bfloat16 [128, 256, 1024], P(('grp', 'dev')), may hold values from -6 to 6
- sample_prompt: int32 [128], replicated, may hold values from 0 to 7
- caption_len: int32 [8], replicated, may hold values from 8 to 64
Outputs:
- context: bfloat16 [128, 256, 1024], P(('grp', 'dev'))
- image_grad: bfloat16 [128, 256, 2048], P(('grp', 'dev'))
- caption_grad: float32 [8, 64, 4096], P('dev', 'grp')
Inputs may be any that keep to these rules, and one draw needn't show every extreme that they name: `sample_prompt`: sample s belongs to the device at position s // 4 of the devices taken with grp slowest; a prompt may have no samples.
All inputs are finite; a program needn't handle non-finite values.
Results may differ from a plain program's by a relative error of at most 0.008.
Values may be sent and summed in bfloat16 or wider, within the bound.
No kernel may reach another device: no remote copies, remote signals or barrier semaphores. Data moves between devices by JAX's collectives and lax.ppermute only.
A program may use at most 128 MiB of HBM per device.

v0:
```python
import math

import jax
import jax.numpy as jnp
from jax import lax
from jax.sharding import PartitionSpec as P

HEADS = 8
HD = 128


NEG_FILL = -1e30


def attend_block(queries, key_rows, value_rows, live, grad_rows, score_scale):
    scores = (
        jnp.einsum("sihd,sjhd->shij", queries, key_rows, preferred_element_type=jnp.float32)
        * score_scale
    )
    scores = jnp.where(live[:, None, None, :], scores, NEG_FILL)
    top_score = jnp.max(scores, axis=-1, keepdims=True)
    expd = jnp.exp(scores - top_score)
    soft = expd / jnp.sum(expd, axis=-1, keepdims=True)
    soft_b = soft.astype(jnp.bfloat16)
    context = jnp.einsum(
        "shij,sjhd->sihd", soft_b, value_rows, preferred_element_type=jnp.float32
    ).astype(jnp.bfloat16)
    d_soft = jnp.einsum(
        "sihd,sjhd->shij", grad_rows, value_rows, preferred_element_type=jnp.float32
    )
    d_values = jnp.einsum("shij,sihd->sjhd", soft_b, grad_rows, preferred_element_type=jnp.float32)
    d_scores = (
        soft * (d_soft - jnp.sum(d_soft * soft, axis=-1, keepdims=True)) * score_scale
    ).astype(jnp.bfloat16)
    d_keys = jnp.einsum("shij,sihd->sjhd", d_scores, queries, preferred_element_type=jnp.float32)
    d_queries = jnp.einsum(
        "shij,sjhd->sihd", d_scores, key_rows, preferred_element_type=jnp.float32
    ).astype(jnp.bfloat16)
    return (context, d_queries, d_keys, d_values)


def shards(captions, kv_weight, image_tokens, q_weight, context_grad, sample_prompt, caption_len):
    n_grp = lax.axis_size("grp")
    n_dev = lax.axis_size("dev")
    grp_at = lax.axis_index("grp")
    dev_at = lax.axis_index("dev")
    samp_dev, img_len, width_img = image_tokens.shape
    prompt_dev, block_len, width_cap = captions.shape
    inner = q_weight.shape[1]
    full_len = block_len * n_grp
    prompts = prompt_dev * n_dev
    score_scale = 1.0 / math.sqrt(HD)
    caption_share = lax.all_to_all(captions, "grp", split_axis=2, concat_axis=1, tiled=True)
    summed = lax.psum_scatter(
        jnp.einsum("ple,ek->lpk", caption_share, kv_weight, preferred_element_type=jnp.float32),
        "grp",
        scatter_dimension=0,
        tiled=True,
    )
    kv_block = jnp.transpose(summed, (1, 0, 2)).astype(jnp.bfloat16)
    placed = sample_prompt.reshape(n_grp, n_dev, samp_dev)
    column = lax.dynamic_index_in_dim(placed, dev_at, 1, keepdims=False)
    own_prompts = lax.dynamic_index_in_dim(column, grp_at, 0, keepdims=False)
    whole_prompts = lax.all_gather(kv_block, "grp", axis=1, tiled=True)
    piece = lax.all_gather(whole_prompts, "dev", axis=0, tiled=True)
    prompt_rows = jnp.arange(piece.shape[0], dtype=jnp.int32)
    match = (own_prompts[:, None] == prompt_rows[None, :]).astype(jnp.bfloat16)
    picked = jnp.einsum("sp,plk->slk", match, piece, preferred_element_type=jnp.float32)
    sample_kv = picked.astype(jnp.bfloat16)
    prompt_ids = jnp.arange(prompts, dtype=jnp.int32)
    own_len = jnp.sum(
        jnp.where(own_prompts[:, None] == prompt_ids[None, :], caption_len[None, :], 0), axis=1
    )
    live = jnp.arange(full_len, dtype=jnp.int32)[None, :] < own_len[:, None]
    queries = jnp.dot(
        image_tokens.reshape(samp_dev * img_len, width_img),
        q_weight,
        preferred_element_type=jnp.float32,
    )
    queries = queries.astype(jnp.bfloat16).reshape(samp_dev, img_len, HEADS, HD)
    key_rows = sample_kv[:, :, :inner].reshape(samp_dev, full_len, HEADS, HD)
    value_rows = sample_kv[:, :, inner:].reshape(samp_dev, full_len, HEADS, HD)
    grad_rows = context_grad.reshape(samp_dev, img_len, HEADS, HD)
    context, d_queries, d_keys, d_values = attend_block(
        queries, key_rows, value_rows, live, grad_rows, score_scale
    )
    image_grad = jnp.dot(
        d_queries.reshape(samp_dev * img_len, inner), q_weight.T, preferred_element_type=jnp.float32
    )
    image_grad = image_grad.astype(jnp.bfloat16).reshape(samp_dev, img_len, width_img)
    grad_kv = jnp.concatenate(
        [d_keys.reshape(samp_dev, full_len, inner), d_values.reshape(samp_dev, full_len, inner)],
        axis=2,
    )
    split_grad = grad_kv.reshape(samp_dev, n_grp, block_len, 2 * inner)
    arrived = lax.all_to_all(split_grad, "grp", split_axis=1, concat_axis=1, tiled=True)
    prompt_rows = jnp.arange(lax.axis_size("dev") * prompt_dev, dtype=jnp.int32)
    match = (column[:, :, None] == prompt_rows[None, None, :]).astype(jnp.float32)
    kv_grad = lax.psum_scatter(
        jnp.einsum("gsp,sglk->plk", match, arrived, precision=lax.Precision.HIGHEST),
        "dev",
        scatter_dimension=0,
        tiled=True,
    )
    kv_grad_b = kv_grad.astype(jnp.bfloat16)
    grad_whole = lax.all_gather(kv_grad_b, "grp", axis=1, tiled=True)
    share_grad = jnp.einsum(
        "plk,ek->ple", grad_whole, kv_weight, preferred_element_type=jnp.float32
    )
    caption_grad = lax.all_to_all(share_grad, "grp", split_axis=1, concat_axis=2, tiled=True)
    return (context.reshape(samp_dev, img_len, inner), image_grad, caption_grad)


def solution(mesh):
    placed = (
        P("dev", "grp", None),
        P("grp", None),
        P(("grp", "dev"), None, None),
        P(),
        P(("grp", "dev"), None, None),
        P(),
        P(),
    )
    return jax.shard_map(
        shards,
        mesh=mesh,
        in_specs=placed,
        out_specs=(
            P(("grp", "dev"), None, None),
            P(("grp", "dev"), None, None),
            P("dev", "grp", None),
        ),
        check_vma=False,
    )
```

profile of v0, /device:TPU:0, one launch (start us, length us, event | category | flops | bytes accessed | tf_op | source)
XLA Modules:
  0.0 253.5 jit_solution(17903702311628979394)
XLA Ops:
  7.2 0.0 copy-start
  7.2 0.0 reduce-scatter.3.cloned.1.call-start
  7.2 5.0 %copy.54 = bf16[1,16,4096]{1,0,2:T(2,128)(2,1)} copy(bf16[1,16,4096]{2,1,0:T(8,128)(2,1)} %param.7) | data formatting | bytes 262144 | tf_op args[0]
  12.3 0.5 broadcast.29
  12.8 23.4 %reduce = bf16[4096,16]{1,0:T(8,128)(2,1)S(1)} reduce(bf16[4096,1,16]{2,1,0:T(2,128)(2,1)} %bitcast.101, bf16[]{:T(256)} %broadcast.29), dimensions={1}, to_apply=%bitcast.86.reduce_sub_computation | reduce | bytes 262146
  36.2 1.1 reshape.105
  37.3 10.0 %all_to_all.38 = bf16[4,2,8192]{2,1,0:T(2,128)(2,1)S(1)} all-to-all(bf16[4,2,8192]{2,1,0:T(2,128)(2,1)S(1)} %reshape.105), channel_id=1, replica_groups=mesh['grp'=4,'dev'=8] {'grp'}, dimensions={0} | all-to-all | bytes 262144 | tf_op jit(solution)/shard_map/all_to_all | solution.py:53
  47.3 2.7 %reshape.106 = bf16[4096,1,16]{2,1,0:T(2,128)(2,1)} reshape(bf16[4,2,8192]{2,1,0:T(2,128)(2,1)S(1)} %all_to_all.38) | data formatting | bytes 262144
  50.0 4.4 %copy.55 = bf16[1,16,4096]{2,1,0:T(8,128)(2,1)S(1)} copy(bf16[1,16,4096]{1,0,2:T(2,128)(2,1)} %bitcast.102) | data formatting | bytes 262144 | tf_op jit(solution)/shard_map/all_to_all | solution.py:53
  54.4 0.1 all_to_all.28
  54.6 0.0 copy-start.5
  54.6 3.8 %convolution_bitcast_fusion.1 = f32[64,1,2048]{2,0,1:T(8,128)} fusion(bf16[64,1024]{1,0:T(8,128)(2,1)S(1)} %bitcast.109, bf16[1024,2048]{1,0:T(8,128)(2,1)} %param.8), kind=kOutput, calls=%fused_computation.5 | convolution fusion | flops 268435456 | bytes 4849664 | tf_op jit(solution)/shard_map/ple,ek->lpk/dot_general | solution.py:55
  58.4 0.0 reduce-scatter.3.cloned.1.call-update
  58.4 0.0 all-gather.4.cloned.1.call-start
  58.5 24.9 %reduce-scatter.3.cloned.1.call-done = f32[16,1,2048]{2,0,1:T(8,128)} async-done(((f32[64,1,2048]{2,0,1:T(8,128)}), f32[16,1,2048]{2,0,1:T(8,128)}) %reduce-scatter.3.cloned.1.call-update) | async-done | bytes 131088 | tf_op jit(solution)/shard_map/reduce_scatter | solution.py:54
  83.4 0.9 convert_element_type.46
  84.3 9.7 %all-gather = bf16[64,1,2048]{2,0,1:T(8,128)(2,1)} all-gather(bf16[16,1,2048]{2,0,1:T(8,128)(2,1)S(1)} %convert_element_type.46), channel_id=2, replica_groups=mesh['grp'=4,'dev'=8] {'grp'}, dimensions={0}, use_global_device_ids=true | all-gather | bytes 327680 | tf_op jit(solution)/shard_map/all_gather | solution.py:64
  94.1 0.0 all-gather.4.cloned.1.call-update
  94.1 0.0 copy-done.5
  94.1 0.1 reshape.89
  94.2 8.0 %convert_bitcast_fusion.1 = bf16[128,8,8,128]{3,1,2,0:T(8,128)(2,1)S(1)} fusion(bf16[1024,2048]{1,0:T(8,128)(2,1)} %bitcast.112, bf16[2048,1024]{1,0:T(8,128)(2,1)} %param.10), kind=kOutput, calls=%fused_computation.22 | convolution fusion | flops 4296015872 | bytes 10485760 | tf_op jit(solution)/shard_map/dot_general | solution.py:75
  102.2 0.0 copy-start.6
  102.2 1.9 copy.77
  104.1 0.0 copy-done.6
  104.1 0.2 select_reduce_fusion
  104.3 0.1 iota_compare_fusion.1
  104.4 19.0 %all-gather.4.cloned.1.call-done = bf16[512,1,2048]{2,0,1:T(8,128)(2,1)} async-done(((bf16[64,1,2048]{2,0,1:T(8,128)(2,1)}), bf16[512,1,2048]{2,0,1:T(8,128)(2,1)}) %all-gather.4.cloned.1.call-update) | async-done | bytes 2097168 | tf_op jit(solution)/shard_map/all_gather | solution.py:65
  123.4 3.1 %convolution_convert_fusion.1 = bf16[4,64,2048]{2,0,1:T(4,128)(2,1)S(1)} fusion(bf16[8,64,2048]{2,1,0:T(8,128)(2,1)} %bitcast.103, s32[4]{0:T(128)S(1)} %dynamic-slice_bitcast_fusion), kind=kOutput, calls=%fused_computation.3 | convolution fusion | flops 8912928 | bytes 3145744 | tf_op jit(solution)/shard_map/sp,plk->slk/dot_general | solution.py:68
  126.5 0.4 fusion.48
  126.9 1.0 reshape.94
  127.9 0.2 reshape.91
  128.1 0.0 copy-done
  128.1 0.0 copy-start.1
  128.1 0.0 copy-start.3
  128.1 2.2 fusion.6
  130.3 4.1 %fusion.49 = (f32[4,8,256]{2,1,0:T(8,128)S(1)}, f32[4,8,256,64]{2,3,1,0:T(8,128)}) fusion(pred[4,64]{1,0:T(4,128)(4,1)S(1)} %iota_compare_fusion.1, bf16[4,256,8,128]{3,2,1,0:T(8,128)(2,1)} %bitcast.104, bf16[4,64,8,128]{3,2,0,1:T(8,128)(2,1)S(1)} %copy-done.3), kind=kOutput, calls=%fused_computation.63 | convolution fusion | flops 136314944 | bytes 4751616 | tf_op jit(solution)/shard_map/sub | solution.py:22
  134.4 3.0 %fusion.22 = f32[4,64,8,128]{3,1,2,0:T(8,128)} fusion(f32[4,8,256,64]{2,3,1,0:T(8,128)} %get-tuple-element.18, f32[4,8,256]{2,1,0:T(8,128)S(1)} %get-tuple-element.17, bf16[4,256,1024]{2,1,0:T(8,128)(2,1)S(1)} %copy-done), kind=kOutput, calls=%fused_computation.32 | convolution fusion | flops 135266304 | bytes 5275648 | tf_op jit(solution)/shard_map/shij,sihd->sjhd/dot_general | solution.py:31
  137.4 6.2 %fusion.19 = f32[4,64,8,128]{3,1,2,0:T(8,128)} fusion(bf16[4,256,8,128]{3,2,1,0:T(8,128)(2,1)} %bitcast.105, f32[4,8,64,256]{3,2,1,0:T(8,128)} %fusion.6, f32[4,8,256,64]{2,3,1,0:T(8,128)} %get-tuple-element.18, f32[4,8,256]{2,1,0:T(8,128)S(1)} %get-tuple-element.17), kind=kOutput, calls=%fused_computation.31 | convolution fusion | flops 137896000 | bytes 7372800 | tf_op jit(solution)/shard_map/shij,sihd->sjhd/dot_general | solution.py:35
  143.6 1.8 copy.66
  145.5 1.1 concatenate.8
  146.6 1.8 copy.68
  148.4 1.1 concatenate.9
  149.6 1.7 pad_maximum_fusion
  151.3 2.9 %copy.69 = f32[4,4,16,2048]{3,0,2,1:T(4,128)} copy(f32[4,4,16,2048]{3,2,1,0:T(8,128)S(1)} %pad_maximum_fusion) | data formatting | bytes 4194304 | tf_op jit(solution)/shard_map/concatenate | solution.py:91
  154.2 4.5 %all-to-all-start.1 = ((f32[4,4,16,2048]{3,0,2,1:T(4,128)}), f32[4,4,16,2048]{3,0,2,1:T(4,128)}, u32[]{:S(2)}, u32[]{:S(2)}) async-start(f32[4,4,16,2048]{3,0,2,1:T(4,128)} %copy.69), calls=%async_computation.2 | async-start | bytes 4194304 | tf_op jit(solution)/shard_map/all_to_all | solution.py:96
  158.6 0.0 reduce-scatter.5.cloned.1.call-start
  158.7 25.5 %all-to-all-done.1 = f32[4,4,16,2048]{3,0,2,1:T(4,128)} async-done(((f32[4,4,16,2048]{3,0,2,1:T(4,128)}), f32[4,4,16,2048]{3,0,2,1:T(4,128)}, u32[]{:S(2)}, u32[]{:S(2)}) %all-to-all-start.1) | async-done | bytes 2097184 | tf_op jit(solution)/shard_map/all_to_all | solution.py:96
  184.2 3.3 %convolution_bitcast_fusion = f32[8,16,2048]{2,0,1:T(8,128)S(1)} fusion(f32[4,4,16,2048]{3,0,2,1:T(4,128)} %all-to-all-done.1, s32[4,4]{1,0:T(4,128)S(1)} %bitcast.111), kind=kOutput, calls=%fused_computation.4 | convolution fusion | flops 50331776 | bytes 3145792 | tf_op jit(solution)/shard_map/gsp,sglk->plk/dot_general | solution.py:100
  187.5 1.6 copy.71
  189.1 0.0 reduce-scatter.5.cloned.1.call-update
  189.2 6.0 %convert_bitcast_fusion = bf16[4,256,8,128]{1,3,2,0:T(8,128)(2,1)} fusion(f32[4,8,64,256]{3,2,1,0:T(8,128)} %fusion.6, bf16[4,64,8,128]{3,2,0,1:T(8,128)(2,1)S(1)} %copy-done.4, f32[4,8,256,64]{2,3,1,0:T(8,128)} %get-tuple-element.18, f32[4,8,256]{2,1,0:T(8,128)S(1)} %get-tuple-element.17), kind=kOutput, calls=%fused_computation.19 | convolution fusion | flops 138944576 | bytes 6848512 | tf_op jit(solution)/shard_map/shij,sjhd->sihd/dot_general | solution.py:36
  195.2 4.3 %copy.64 = bf16[4,256,8,128]{3,2,1,0:T(8,128)(2,1)} copy(bf16[4,256,8,128]{1,3,2,0:T(8,128)(2,1)} %convert_bitcast_fusion) | data formatting | bytes 4194304 | tf_op jit(solution)/shard_map/convert_element_type | solution.py:38
  199.5 9.4 %convolution_convert_fusion = bf16[1024,2048]{1,0:T(8,128)(2,1)} fusion(bf16[2048,1024]{1,0:T(8,128)(2,1)} %param.10, bf16[128,8,8,128]{3,2,1,0:T(8,128)(2,1)} %bitcast.107), kind=kOutput, calls=%fused_computation.2 | convolution fusion | flops 4297064448 | bytes 10485760 | tf_op jit(solution)/shard_map/dot_general | solution.py:87
  208.9 11.5 %reduce-scatter.5.cloned.1.call-done = f32[1,16,2048]{2,1,0:T(8,128)} async-done(((f32[8,16,2048]{2,1,0:T(8,128)}), f32[1,16,2048]{2,1,0:T(8,128)}) %reduce-scatter.5.cloned.1.call-update) | async-done | bytes 131088 | tf_op jit(solution)/shard_map/reduce_scatter | solution.py:99
  220.4 0.9 convert_element_type.57
  221.3 8.9 %all_gather.11 = bf16[1,64,2048]{2,1,0:T(8,128)(2,1)S(1)} all-gather(bf16[1,16,2048]{2,1,0:T(8,128)(2,1)S(1)} %convert_element_type.57), channel_id=1, replica_groups=mesh['grp'=4,'dev'=8] {'grp'}, dimensions={1}, use_global_device_ids=true | all-gather | bytes 327680 | tf_op jit(solution)/shard_map/all_gather | solution.py:106
  230.2 3.6 %convolution_bitcast_fusion.2 = f32[1,64,1024]{2,1,0:T(8,128)S(1)} fusion(bf16[1024,2048]{1,0:T(8,128)(2,1)} %param.8, bf16[1,64,2048]{2,1,0:T(8,128)(2,1)S(1)} %all_gather.11), kind=kOutput, calls=%fused_computation.33 | convolution fusion | flops 268435456 | bytes 4718592 | tf_op jit(solution)/shard_map/plk,ek->ple/dot_general | solution.py:107
  233.9 1.0 copy.72
  234.9 3.4 %all-to-all-start.2 = ((f32[1,64,1024]{2,0,1:T(1,128)}), f32[1,64,1024]{2,0,1:T(1,128)S(1)}, u32[]{:S(2)}, u32[]{:S(2)}) async-start(f32[1,64,1024]{2,0,1:T(1,128)} %copy.72), calls=%async_computation.4 | async-start | bytes 524288 | tf_op jit(solution)/shard_map/all_to_all | solution.py:110
  238.3 3.7 %convolution_convert_fusion.2 = bf16[4,8,128,256]{3,2,1,0:T(8,128)(2,1)} fusion(bf16[4,64,8,128]{3,2,0,1:T(8,128)(2,1)S(1)} %copy-done.2, f32[4,8,256,64]{2,3,1,0:T(8,128)} %get-tuple-element.18, f32[4,8,256]{2,1,0:T(8,128)S(1)} %get-tuple-element.17), kind=kOutput, calls=%fused_computation.23 | convolution fusion | flops 136314880 | bytes 4751360 | tf_op jit(solution)/shard_map/shij,sjhd->sihd/dot_general | solution.py:25
  241.9 3.9 %copy.74 = bf16[4,256,1024]{2,1,0:T(8,128)(2,1)} copy(bf16[4,256,1024]{1,2,0:T(8,128)(2,1)} %bitcast.106) | data formatting | bytes 4194304
  245.9 0.0 all-to-all-done.2
  245.9 0.2 copy.73
  246.1 0.9 all_to_all.34
  (9 shorter events, 0.1 us)
Async XLA Ops:
  7.2 120.9 %copy-start = (bf16[4,256,1024]{2,1,0:T(8,128)(2,1)S(1)}, bf16[4,256,1024]{2,1,0:T(8,128)(2,1)}, u32[]{:S(2)}) copy-start(bf16[4,256,1024]{2,1,0:T(8,128)(2,1)} %param.11) | copy-start | bytes 6291460
  7.2 76.2 %reduce-scatter.3.cloned.1.call-start = ((), (), s32[]{:S(2)}) async-start(), calls=%async_computation.5 | async-start | bytes 655360 | tf_op jit(solution)/shard_map/reduce_scatter | solution.py:54
  54.6 39.5 %copy-start.5 = (s32[128]{0:T(128)S(1)}, s32[128]{0:T(128)}, u32[]{:S(2)}) copy-start(s32[128]{0:T(128)} %param.12) | copy-start | bytes 1540
  58.4 65.0 %all-gather.4.cloned.1.call-start = ((), (), s32[]{:S(2)}) async-start(), calls=%async_computation.7 | async-start | bytes 2359296 | tf_op jit(solution)/shard_map/all_gather | solution.py:65
  102.2 2.0 copy-start.6
  128.1 2.2 copy-start.1
  128.1 2.2 copy-start.3
  154.2 30.1 %all-to-all-start.1 = ((f32[4,4,16,2048]{3,0,2,1:T(4,128)}), f32[4,4,16,2048]{3,0,2,1:T(4,128)}, u32[]{:S(2)}, u32[]{:S(2)}) async-start(f32[4,4,16,2048]{3,0,2,1:T(4,128)} %copy.69), calls=%async_computation.2 | async-start | bytes 4194304 | tf_op jit(solution)/shard_map/all_to_all | solution.py:96
  158.6 61.8 %reduce-scatter.5.cloned.1.call-start = ((), (), s32[]{:S(2)}) async-start(), calls=%async_computation.6 | async-start | bytes 1179648 | tf_op jit(solution)/shard_map/reduce_scatter | solution.py:99
  187.5 1.6 copy-start.4
  230.2 8.0 %copy-start.2 = (bf16[4,64,8,128]{3,2,0,1:T(8,128)(2,1)S(1)}, bf16[4,64,8,128]{3,2,0,1:T(8,128)(2,1)}, u32[]{:S(2)}) copy-start(bf16[4,64,8,128]{3,2,0,1:T(8,128)(2,1)} %copy-done.1) | copy-start | bytes 1572868
  234.9 11.0 %all-to-all-start.2 = ((f32[1,64,1024]{2,0,1:T(1,128)}), f32[1,64,1024]{2,0,1:T(1,128)S(1)}, u32[]{:S(2)}, u32[]{:S(2)}) async-start(f32[1,64,1024]{2,0,1:T(1,128)} %copy.72), calls=%async_computation.4 | async-start | bytes 524288 | tf_op jit(solution)/shard_map/all_to_all | solution.py:110
Sparse Core Ops, SparseCore 0:
  58.6 24.8 reduce-scatter.2
  94.2 29.1 all-gather.3
  189.3 31.0 reduce-scatter.4
where the time goes:
time: 255 us; the launch traced here: 253 us
  waiting for transfers between devices  81 us (32%)
  matrix products  56.4 us (22%)
  local copies, waits for them, and re-layouts  38.2 us (15%)
  blocking collectives  28.7 us (11%)
  other arithmetic  27.2 us (11%)
  between operations  13.9 us (5%)
  starting transfers between devices  7.98 us (3%)
    all_to_all x1, waiting for transfers between devices, shards(): lax.all_to_all(split_grad, 'grp', split_axis=1, concat_axis=1, tiled=True)  25.5 us
    reduce_scatter x1, waiting for transfers between devices, shards(): lax.psum_scatter(jnp.einsum('ple,ek->lpk', caption_share, kv_weight, pref...  24.9 us
    unnamed x1, other arithmetic  23.4 us
    all_gather x1, waiting for transfers between devices, shards(): piece = lax.all_gather(whole_prompts, 'dev', axis=0, tiled=True)  19 us
    unnamed x20, local copies, waits for them, and re-layouts  15.2 us
    reduce_scatter x1, waiting for transfers between devices, shards(): lax.psum_scatter(jnp.einsum('gsp,sglk->plk', match, arrived, precision=la...  11.5 us
    all_to_all x1, blocking collectives, shards(): lax.all_to_all(captions, 'grp', split_axis=2, concat_axis=1, tiled=True)  10 us
    all_gather x1, blocking collectives, shards(): whole_prompts = lax.all_gather(kv_block, 'grp', axis=1, tiled=True)  9.75 us
  transfers between devices with their start and end apart: 5, of which 4 were waited for; matrix products, arithmetic and copies ran while one was open for 15% of the time, Pallas kernels for 0%

commit v1 on v0

v1 whole, which is shorter than its diff:
```python
import functools
import math

import jax
import jax.numpy as jnp
from jax import lax
from jax.experimental import pallas as pl
from jax.experimental.pallas import tpu as pltpu
from jax.sharding import PartitionSpec as P

HEADS = 8
HD = 128
NEG_FILL = -1e30
F32 = jnp.float32
BF16 = jnp.bfloat16


def partner(x, axis, size, k):
    return lax.ppermute(x, axis, [(i, i ^ k) for i in range(size)])


def attend(ids, prompt_of, lens, queries, grads, own_kv, other_kv, shape):
    samp_dev, img_len, inner, n_grp, n_dev, block_len = shape
    full_len = n_grp * block_len
    scale = 1.0 / math.sqrt(HD)

    def prompt_at(s, ids_ref, prompt_ref):
        return prompt_ref[(ids_ref[0] * n_dev + ids_ref[1]) * samp_dev + s]

    def body(ids_ref, prompt_ref, len_ref, q_ref, g_ref, *refs):
        own = refs[:n_grp]
        other = refs[n_grp : 2 * n_grp]
        ctx_ref, dq_ref = refs[2 * n_grp : 2 * n_grp + 2]
        outs = refs[2 * n_grp + 2 : 3 * n_grp + 2]
        kv_ref = refs[3 * n_grp + 2]
        s = pl.program_id(0)
        prompt = prompt_at(s, ids_ref, prompt_ref)
        live_len = len_ref[prompt]
        flip = (prompt ^ ids_ref[1]) & 1

        @pl.when(flip == 0)
        def _():
            for k in range(n_grp):
                kv_ref[k * block_len : (k + 1) * block_len, :] = own[k][0]

        @pl.when(flip == 1)
        def _():
            for k in range(n_grp):
                kv_ref[k * block_len : (k + 1) * block_len, :] = other[k][0]

        row = lax.broadcasted_iota(jnp.int32, (full_len, 1), 0)
        token = ((row // block_len) ^ ids_ref[0]) * block_len + row % block_len
        live = token < live_len
        nt = (((1,), (1,)), ((), ()))
        tn = (((0,), (0,)), ((), ()))
        nn = (((1,), (0,)), ((), ()))

        def dot(a, b, dims):
            return lax.dot_general(a, b, dims, preferred_element_type=F32)

        for h in range(HEADS):
            cols = slice(h * HD, (h + 1) * HD)
            vcols = slice(inner + h * HD, inner + (h + 1) * HD)
            q = q_ref[:, cols]
            g = g_ref[:, cols]
            key = kv_ref[:, cols]
            val = kv_ref[:, vcols]
            scores = jnp.where(live, dot(key, q, nt) * scale, NEG_FILL)
            expd = jnp.exp(scores - jnp.max(scores, axis=0, keepdims=True))
            soft = expd * (1.0 / jnp.sum(expd, axis=0, keepdims=True))
            soft_b = soft.astype(BF16)
            d_soft = dot(val, g, nt)
            mean = jnp.sum(d_soft * soft, axis=0, keepdims=True)
            d_scores = (soft * (d_soft - mean) * scale).astype(BF16)
            ctx_ref[:, cols] = dot(soft_b, val, tn).astype(BF16)
            dq_ref[:, cols] = dot(d_scores, key, tn).astype(BF16)
            d_key = dot(d_scores, q, nn).astype(BF16)
            d_val = dot(soft_b, g, nn).astype(BF16)
            for k in range(n_grp):
                rows = slice(k * block_len, (k + 1) * block_len)
                outs[k][0, :, cols] = d_key[rows]
                outs[k][0, :, vcols] = d_val[rows]

    def kv_map(s, ids_ref, prompt_ref, len_ref):
        return ((prompt_at(s, ids_ref, prompt_ref) >> 1) ^ (ids_ref[1] >> 1), 0, 0)

    rows_spec = pl.BlockSpec((img_len, inner), lambda s, *_: (s, 0))
    kv_spec = pl.BlockSpec((1, block_len, 2 * inner), kv_map)
    out_spec = pl.BlockSpec((1, block_len, 2 * inner), lambda s, *_: (s, 0, 0))
    rows_shape = jax.ShapeDtypeStruct((samp_dev * img_len, inner), BF16)
    out_shape = jax.ShapeDtypeStruct((samp_dev, block_len, 2 * inner), BF16)
    return pl.pallas_call(
        body,
        grid_spec=pltpu.PrefetchScalarGridSpec(
            num_scalar_prefetch=3,
            grid=(samp_dev,),
            in_specs=[rows_spec, rows_spec] + [kv_spec] * (2 * n_grp),
            out_specs=[rows_spec, rows_spec] + [out_spec] * n_grp,
            scratch_shapes=[pltpu.VMEM((full_len, 2 * inner), BF16)],
        ),
        out_shape=[rows_shape, rows_shape] + [out_shape] * n_grp,
        name="attend",
    )(ids, prompt_of, lens, queries, grads, *own_kv, *other_kv)


def combine(ids, prompt_of, arrived, shape):
    samp_dev, n_grp, n_dev, block_len, width = shape
    chips = n_dev // 2

    def body(ids_ref, prompt_ref, *refs):
        same_ref, other_ref, acc_ref = refs[n_grp:]
        acc_ref[...] = jnp.zeros_like(acc_ref)
        for k in range(n_grp):
            base = ((ids_ref[0] ^ k) * n_dev + ids_ref[1]) * samp_dev
            for s in range(samp_dev):
                rel = prompt_ref[base + s] ^ ids_ref[1]
                slot = (rel & 1) * chips + (rel >> 1)
                acc_ref[slot] += refs[k][s].astype(F32)
        same_ref[...] = acc_ref[:chips]
        other_ref[...] = acc_ref[chips:].astype(BF16)

    vmem = pl.BlockSpec(memory_space=pltpu.VMEM)
    smem = pl.BlockSpec(memory_space=pltpu.SMEM)
    return pl.pallas_call(
        body,
        in_specs=[smem, smem] + [vmem] * n_grp,
        out_specs=[vmem, vmem],
        out_shape=[
            jax.ShapeDtypeStruct((chips, block_len, width), F32),
            jax.ShapeDtypeStruct((chips, block_len, width), BF16),
        ],
        scratch_shapes=[pltpu.VMEM((2 * chips, block_len, width), F32)],
        name="combine",
    )(ids, prompt_of, *arrived)


def shards(captions, kv_weight, image_tokens, q_weight, context_grad, sample_prompt, caption_len):
    n_grp = lax.axis_size("grp")
    n_dev = lax.axis_size("dev")
    grp_at = lax.axis_index("grp")
    dev_at = lax.axis_index("dev")
    samp_dev, img_len, width_img = image_tokens.shape
    _, block_len, width_cap = captions.shape
    inner = q_weight.shape[1]
    share = width_cap // n_grp
    chips = n_dev // 2
    ids = jnp.stack([grp_at, dev_at]).astype(jnp.int32)

    def over_grp(blocks):
        return [blocks[0]] + [partner(blocks[k], "grp", n_grp, k) for k in range(1, n_grp)]

    rows = captions.reshape(block_len, width_cap)
    pieces = [lax.dynamic_slice_in_dim(rows, (grp_at ^ k) * share, share, 1) for k in range(n_grp)]
    caption_share = jnp.concatenate(over_grp(pieces), axis=0)
    partial = jnp.dot(caption_share, kv_weight, preferred_element_type=F32)
    summed = over_grp([partial[k * block_len : (k + 1) * block_len] for k in range(n_grp)])
    kv_block = sum(summed[1:], summed[0]).astype(BF16)

    column = jnp.stack(
        [kv_block] + [partner(kv_block, "dev", n_dev, 2 * k) for k in range(1, chips)]
    )
    own_kv = over_grp([column] * n_grp)
    other_kv = [partner(x, "dev", n_dev, 1) for x in own_kv]

    queries = jnp.dot(
        image_tokens.reshape(samp_dev * img_len, width_img), q_weight, preferred_element_type=F32
    ).astype(BF16)
    context, d_queries, *d_kv = attend(
        ids,
        sample_prompt,
        caption_len,
        queries,
        context_grad.reshape(samp_dev * img_len, inner),
        own_kv,
        other_kv,
        (samp_dev, img_len, inner, n_grp, n_dev, block_len),
    )

    arrived = over_grp(d_kv)
    same, other = combine(
        ids, sample_prompt, arrived, (samp_dev, n_grp, n_dev, block_len, 2 * inner)
    )
    both = same + partner(other, "dev", n_dev, 1).astype(F32)
    kv_grad = both[0]
    for k in range(1, chips):
        kv_grad = kv_grad + partner(both[k].astype(BF16), "dev", n_dev, 2 * k).astype(F32)
    kv_grad_b = kv_grad.astype(BF16)
    grad_whole = jnp.concatenate(over_grp([kv_grad_b] * n_grp), axis=0)
    share_grad = lax.dot_general(
        grad_whole, kv_weight, (((1,), (1,)), ((), ())), preferred_element_type=F32
    )
    shares = over_grp([share_grad[k * block_len : (k + 1) * block_len] for k in range(n_grp)])
    caption_grad = jnp.zeros((block_len, width_cap), F32)
    for k in range(n_grp):
        caption_grad = lax.dynamic_update_slice_in_dim(
            caption_grad, shares[k], (grp_at ^ k) * share, 1
        )

    image_grad = lax.dot_general(
        d_queries, q_weight, (((1,), (1,)), ((), ())), preferred_element_type=F32
    ).astype(BF16)
    return (
        context.reshape(samp_dev, img_len, inner),
        image_grad.reshape(samp_dev, img_len, width_img),
        caption_grad[None],
    )


def solution(mesh):
    placed = (
        P("dev", "grp", None),
        P("grp", None),
        P(("grp", "dev"), None, None),
        P(),
        P(("grp", "dev"), None, None),
        P(),
        P(),
    )
    return jax.shard_map(
        shards,
        mesh=mesh,
        in_specs=placed,
        out_specs=(
            P(("grp", "dev"), None, None),
            P(("grp", "dev"), None, None),
            P("dev", "grp", None),
        ),
        check_vma=False,
    )
```

time: 255 us -> 119 us (0.47)
  waiting for transfers between devices: 81 us -> 42.3 us
  local copies, waits for them, and re-layouts: 38.2 us -> 3.43 us
  matrix products: 56.4 us -> 21.8 us
  blocking collectives: 28.7 us -> 0 us
  other arithmetic: 27.2 us -> 1.86 us
  starting transfers between devices: 7.98 us -> 31.6 us
  Pallas kernels: 0 us -> 16.6 us
  between operations: 13.9 us -> 0.87 us
    ppermute x0 -> x29, waiting for transfers between devices: none -> 42.3 us  [partner(): return lax.ppermute(x, axis, [(i, i ^ k) for i in range(size)])]
    reduce_scatter x2 -> x0, waiting for transfers between devices: 36.4 us -> none  [the longest x1 24.9 us: shards(): lax.psum_scatter(jnp.einsum('ple,ek->lpk', caption_share, kv_weight, pref...]
    ppermute x0 -> x29, starting transfers between devices: none -> 31.6 us  [partner(): return lax.ppermute(x, axis, [(i, i ^ k) for i in range(size)])]
    dot_general x10 -> x3, matrix products: 44.4 us -> 13.9 us  [the longest x1 9.51 us: shards(): lax.dot_general(d_queries, q_weight, (((1,), (1,)), ((), ())), preferred_...]
    all_to_all x2 -> x0, waiting for transfers between devices: 25.5 us -> none  [the longest x1 25.5 us: shards(): lax.all_to_all(split_grad, 'grp', split_axis=1, concat_axis=1, tiled=True)]
    unnamed x1 -> x0, other arithmetic: 23.4 us -> none
    all_gather x1 -> x0, waiting for transfers between devices: 19 us -> none  [shards(): piece = lax.all_gather(whole_prompts, 'dev', axis=0, tiled=True)]
    all_gather x2 -> x0, blocking collectives: 18.7 us -> none  [the longest x1 9.75 us: shards(): whole_prompts = lax.all_gather(kv_block, 'grp', axis=1, tiled=True)]
  transfers between devices with their start and end apart: 5 -> 29, of which waited for: 4 -> 20; matrix products, arithmetic and copies ran while one was open for 15% -> 15% of each run, Pallas kernels for 0% -> 0%
where the time goes in v1:
time: 119 us; the launch traced here: 118 us
  waiting for transfers between devices  42.3 us (36%)
  starting transfers between devices  31.6 us (27%)
  matrix products  21.8 us (18%)
  Pallas kernels  16.6 us (14%)
  local copies, waits for them, and re-layouts  3.43 us (3%)
  other arithmetic  1.86 us (2%)
    ppermute x29, waiting for transfers between devices, partner(): return lax.ppermute(x, axis, [(i, i ^ k) for i in range(size)])  42.3 us
    ppermute x29, starting transfers between devices, partner(): return lax.ppermute(x, axis, [(i, i ^ k) for i in range(size)])  31.6 us
    pallas_call x1, Pallas kernels, attend(): pl.pallas_call(body, grid_spec=pltpu.PrefetchScalarGridSpec(num_scalar_pr...  14.2 us
    dot_general x1, matrix products, shards(): lax.dot_general(d_queries, q_weight, (((1,), (1,)), ((), ())), preferred_...  9.51 us
    dot_general x1, matrix products, shards(): jnp.dot(image_tokens.reshape(samp_dev * img_len, width_img), q_weight, pr...  7.83 us
    dot_general x1, matrix products, shards(): partial = jnp.dot(caption_share, kv_weight, preferred_element_type=F32)  3.02 us
  transfers between devices with their start and end apart: 29, of which 20 were waited for; matrix products, arithmetic and copies ran while one was open for 15% of the time, Pallas kernels for 0%

profile of v1, /device:TPU:0, one launch (start us, length us, event | category | flops | bytes accessed | tf_op | source)
XLA Modules:
  0.0 118.4 jit_solution(3655876132973292316)
XLA Ops:
  0.7 1.0 dynamic-slice_bitcast_fusion.3
  1.6 3.0 %collective-permute-start = (bf16[16,1024]{1,0:T(8,128)(2,1)S(1)}, bf16[16,1024]{1,0:T(8,128)(2,1)S(1)}, u32[]{:S(2)}, u32[]{:S(2)}) collective-permute-start(bf16[16,1024]{1,0:T(8,128)(2,1)S(1)} %get-tuple-element.31), channel_id=1, source_target_pairs={{0,8},{8,0},{16,24},{24,16},{1,9},{9,1},{17,25},{25,17},{2,10},{10... | collective-permute-start | bytes 98312 | tf_op jit(solution)/shard_map/ppermute | solution.py:19
  4.7 1.5 %collective-permute-start.1 = (bf16[16,1024]{1,0:T(8,128)(2,1)S(1)}, bf16[16,1024]{1,0:T(8,128)(2,1)S(1)}, u32[]{:S(2)}, u32[]{:S(2)}) collective-permute-start(bf16[16,1024]{1,0:T(8,128)(2,1)S(1)} %get-tuple-element.33), channel_id=1, source_target_pairs={{0,16},{8,24},{16,0},{24,8},{1,17},{9,25},{17,1},{25,9},{2,18},{10... | collective-permute-start | bytes 98312 | tf_op jit(solution)/shard_map/ppermute | solution.py:19
  6.2 0.0 collective-permute-start.2
  6.2 0.4 collective-permute-done
  6.6 2.0 %collective-permute-done.1 = bf16[16,1024]{1,0:T(8,128)(2,1)S(1)} collective-permute-done((bf16[16,1024]{1,0:T(8,128)(2,1)S(1)}, bf16[16,1024]{1,0:T(8,128)(2,1)S(1)}, u32[]{:S(2)}, u32[]{:S(2)}) %collective-permute-start.1) | collective-permute-done | bytes 32800 | tf_op jit(solution)/shard_map/ppermute | solution.py:19
  8.6 2.4 %collective-permute-done.2 = bf16[16,1024]{1,0:T(8,128)(2,1)S(1)} collective-permute-done((bf16[16,1024]{1,0:T(8,128)(2,1)S(1)}, bf16[16,1024]{1,0:T(8,128)(2,1)S(1)}, u32[]{:S(2)}, u32[]{:S(2)}) %collective-permute-start.2) | collective-permute-done | bytes 32800 | tf_op jit(solution)/shard_map/ppermute | solution.py:19
  11.0 3.0 %fusion.15 = f32[64,2048]{1,0:T(8,128)S(1)} fusion(bf16[1024,2048]{1,0:T(8,128)(2,1)} %param.8, bf16[16,1024]{1,0:T(8,128)(2,1)S(1)} %collective-permute-done.2, bf16[16,1024]{1,0:T(8,128)(2,1)S(1)} %collective-permute-done.1, bf16[16,1024]{1,0:T(8,128)(2,1)S(1)} %collective-permute-done, bf16[16,1024]{1,0:T(8,128)(2,1)S(1)} %get-tuple-element.30), kind=kOutput, calls=%fused_computation.21 | convolution fusion | flops 268959744 | bytes 4849664 | tf_op jit(solution)/shard_map/dot_general | solution.py:155
  14.1 0.6 collective-permute-start.3
  14.7 0.1 collective-permute-start.4
  14.7 2.9 %collective-permute-start.5 = (f32[16,2048]{1,0:T(8,128)S(1)}, f32[16,2048]{1,0:T(8,128)S(1)}, u32[]{:S(2)}, u32[]{:S(2)}) collective-permute-start(f32[16,2048]{1,0:T(8,128)S(1)} %get-tuple-element.22), channel_id=1, source_target_pairs={{0,24},{8,16},{16,8},{24,0},{1,25},{9,17},{17,9},{25,1},{2,26},{10... | collective-permute-start | bytes 393224 | tf_op jit(solution)/shard_map/ppermute | solution.py:19
  17.6 1.5 %collective-permute-done.3 = f32[16,2048]{1,0:T(8,128)S(1)} collective-permute-done((f32[16,2048]{1,0:T(8,128)S(1)}, f32[16,2048]{1,0:T(8,128)S(1)}, u32[]{:S(2)}, u32[]{:S(2)}) %collective-permute-start.3) | collective-permute-done | bytes 131104 | tf_op jit(solution)/shard_map/ppermute | solution.py:19
  19.2 1.9 %collective-permute-done.4 = f32[16,2048]{1,0:T(8,128)S(1)} collective-permute-done((f32[16,2048]{1,0:T(8,128)S(1)}, f32[16,2048]{1,0:T(8,128)S(1)}, u32[]{:S(2)}, u32[]{:S(2)}) %collective-permute-start.4) | collective-permute-done | bytes 131104 | tf_op jit(solution)/shard_map/ppermute | solution.py:19
  21.1 0.0 collective-permute-done.5
  21.1 2.7 %collective-permute-start.7 = (bf16[16,2048]{1,0:T(8,128)(2,1)S(1)}, bf16[16,2048]{1,0:T(8,128)(2,1)S(1)}, u32[]{:S(2)}, u32[]{:S(2)}) collective-permute-start(bf16[16,2048]{1,0:T(8,128)(2,1)S(1)} %fusion.14), channel_id=1, source_target_pairs={{0,4},{1,5},{2,6},{3,7},{4,0},{5,1},{6,2},{7,3},{8,12},{9,13},{10,... | collective-permute-start | bytes 196616 | tf_op jit(solution)/shard_map/ppermute | solution.py:19
  23.8 1.3 %collective-permute-start.8 = (bf16[16,2048]{1,0:T(8,128)(2,1)S(1)}, bf16[16,2048]{1,0:T(8,128)(2,1)S(1)}, u32[]{:S(2)}, u32[]{:S(2)}) collective-permute-start(bf16[16,2048]{1,0:T(8,128)(2,1)S(1)} %fusion.14), channel_id=1, source_target_pairs={{0,6},{1,7},{2,4},{3,5},{4,2},{5,3},{6,0},{7,1},{8,14},{9,15},{10,... | collective-permute-start | bytes 196616 | tf_op jit(solution)/shard_map/ppermute | solution.py:19
  25.1 0.2 collective-permute-start.6
  25.3 1.0 collective-permute-done.7
  26.3 3.6 %collective-permute-done.8 = bf16[16,2048]{1,0:T(8,128)(2,1)S(1)} collective-permute-done((bf16[16,2048]{1,0:T(8,128)(2,1)S(1)}, bf16[16,2048]{1,0:T(8,128)(2,1)S(1)}, u32[]{:S(2)}, u32[]{:S(2)}) %collective-permute-start.8) | collective-permute-done | bytes 65568 | tf_op jit(solution)/shard_map/ppermute | solution.py:19
  29.9 0.2 collective-permute-done.6
  30.1 0.0 copy-start.1
  30.1 1.7 %collective-permute-start.9 = (bf16[4,16,2048]{2,1,0:T(8,128)(2,1)S(1)}, bf16[4,16,2048]{2,1,0:T(8,128)(2,1)S(1)}, u32[]{:S(2)}, u32[]{:S(2)}) collective-permute-start(bf16[4,16,2048]{2,1,0:T(8,128)(2,1)S(1)} %pad_maximum_fusion.refs_0_), channel_id=1, source_target_pairs={{0,8},{8,0},{16,24},{24,16},{1,9},{9,1},{17,25},{25,17},{2,10},{10... | collective-permute-start | bytes 786440 | tf_op jit(solution)/shard_map/ppermute | solution.py:19
  31.9 1.3 %collective-permute-start.10 = (bf16[4,16,2048]{2,1,0:T(8,128)(2,1)S(1)}, bf16[4,16,2048]{2,1,0:T(8,128)(2,1)S(1)}, u32[]{:S(2)}, u32[]{:S(2)}) collective-permute-start(bf16[4,16,2048]{2,1,0:T(8,128)(2,1)S(1)} %pad_maximum_fusion.refs_0_), channel_id=1, source_target_pairs={{0,16},{8,24},{16,0},{24,8},{1,17},{9,25},{17,1},{25,9},{2,18},{10... | collective-permute-start | bytes 786440 | tf_op jit(solution)/shard_map/ppermute | solution.py:19
  33.2 0.5 collective-permute-start.11
  33.7 0.0 collective-permute-start.12
  33.7 3.0 %collective-permute-done.9.refs_1_ = bf16[4,16,2048]{2,1,0:T(8,128)(2,1)S(1)} collective-permute-done((bf16[4,16,2048]{2,1,0:T(8,128)(2,1)S(1)}, bf16[4,16,2048]{2,1,0:T(8,128)(2,1)S(1)}, u32[]{:S(2)}, u32[]{:S(2)}) %collective-permute-start.9) | collective-permute-done | bytes 262176 | tf_op jit(solution)/shard_map/ppermute | solution.py:19
  36.7 4.3 %collective-permute-done.10.refs_2_ = bf16[4,16,2048]{2,1,0:T(8,128)(2,1)S(1)} collective-permute-done((bf16[4,16,2048]{2,1,0:T(8,128)(2,1)S(1)}, bf16[4,16,2048]{2,1,0:T(8,128)(2,1)S(1)}, u32[]{:S(2)}, u32[]{:S(2)}) %collective-permute-start.10) | collective-permute-done | bytes 262176 | tf_op jit(solution)/shard_map/ppermute | solution.py:19
  41.1 0.5 collective-permute-start.15
  41.6 7.8 %convolution_convert_fusion.1.q_ref = bf16[1024,1024]{1,0:T(8,128)(2,1)} fusion(bf16[1024,2048]{1,0:T(8,128)(2,1)S(1)} %bitcast.55, bf16[2048,1024]{1,0:T(8,128)(2,1)} %param.10), kind=kOutput, calls=%fused_computation.1 | convolution fusion | flops 4296015872 | bytes 10485760 | tf_op jit(solution)/shard_map/dot_general | solution.py:165
  49.4 0.6 pad_add_fusion.ids_ref
  50.1 0.6 copy-done.5
  50.8 0.1 copy-done.6
  50.9 0.1 copy-done.7
  51.0 0.1 copy-done.8
  51.0 14.2 %attend.1 = (bf16[1024,1024]{1,0:T(8,128)(2,1)}, bf16[1024,1024]{1,0:T(8,128)(2,1)}, bf16[4,16,2048]{2,1,0:T(8,128)(2,1)}, bf16[4,16,2048]{2,1,0:T(8,128)(2,1)},...) custom-call(s32[2]{0:T(128)} %pad_add_fusion.ids_ref, s32[128]{0:T(128)} %prompt_ref.3, s32[8]{0:T(128)} %len_ref.1, ...), custom_call_target="tpu_custom_call" | custom-call | tf_op jit(solution)/shard_map/attend/pallas_call | solution.py:92
  65.2 0.8 collective-permute-start.16
  66.0 1.1 collective-permute-start.17
  67.2 1.6 %collective-permute-start.18 = (bf16[4,16,2048]{2,1,0:T(8,128)(2,1)}, bf16[4,16,2048]{2,1,0:T(8,128)(2,1)S(1)}, u32[]{:S(2)}, u32[]{:S(2)}) collective-permute-start(bf16[4,16,2048]{2,1,0:T(8,128)(2,1)} %get-tuple-element.16), channel_id=1, source_target_pairs={{0,24},{8,16},{16,8},{24,0},{1,25},{9,17},{17,9},{25,1},{2,26},{10... | collective-permute-start | bytes 786440 | tf_op jit(solution)/shard_map/ppermute | solution.py:19
  68.8 5.9 %collective-permute-done.16.refs_1_ = bf16[4,16,2048]{2,1,0:T(8,128)(2,1)S(1)} collective-permute-done((bf16[4,16,2048]{2,1,0:T(8,128)(2,1)}, bf16[4,16,2048]{2,1,0:T(8,128)(2,1)S(1)}, u32[]{:S(2)}, u32[]{:S(2)}) %collective-permute-start.16) | collective-permute-done | bytes 262176 | tf_op jit(solution)/shard_map/ppermute | solution.py:19
  74.7 0.6 collective-permute-done.17.refs_2_
  75.3 5.0 %collective-permute-done.18.refs_3_ = bf16[4,16,2048]{2,1,0:T(8,128)(2,1)S(1)} collective-permute-done((bf16[4,16,2048]{2,1,0:T(8,128)(2,1)}, bf16[4,16,2048]{2,1,0:T(8,128)(2,1)S(1)}, u32[]{:S(2)}, u32[]{:S(2)}) %collective-permute-start.18) | collective-permute-done | bytes 262176 | tf_op jit(solution)/shard_map/ppermute | solution.py:19
  80.3 0.7 copy-done.11
  81.0 2.4 %combine.1 = (f32[4,16,2048]{2,1,0:T(8,128)}, bf16[4,16,2048]{2,1,0:T(8,128)(2,1)}) custom-call(s32[2]{0:T(128)} %pad_add_fusion.ids_ref, s32[128]{0:T(128)} %prompt_ref.3, bf16[4,16,2048]{2,1,0:T(8,128)(2,1)} %get-tuple-element.13.refs_0_, bf16[4,16,2048]{2,1,0:T(8,128)(2,1)} %copy-done.9, bf16[4,16,2048]{2,1,0:T(8,128)(2,1)} %copy-done.10, ...), custom_call_target="tpu_custom_call" | custom-call | tf_op jit(solution)/shard_map/combine/pallas_call | solution.py:124
  83.4 1.7 %collective-permute-done.19 = bf16[4,16,2048]{2,1,0:T(8,128)(2,1)S(1)} collective-permute-done((bf16[4,16,2048]{2,1,0:T(8,128)(2,1)}, bf16[4,16,2048]{2,1,0:T(8,128)(2,1)S(1)}, u32[]{:S(2)}, u32[]{:S(2)}) %collective-permute-start.19) | collective-permute-done | bytes 262176 | tf_op jit(solution)/shard_map/ppermute | solution.py:19
  85.1 1.1 fusion.26
  86.3 0.3 collective-permute-start.20
  86.6 2.7 %collective-permute-start.21 = (bf16[16,2048]{1,0:T(8,128)(2,1)S(1)}, bf16[16,2048]{1,0:T(8,128)(2,1)S(1)}, u32[]{:S(2)}, u32[]{:S(2)}) collective-permute-start(bf16[16,2048]{1,0:T(8,128)(2,1)S(1)} %get-tuple-element.29), channel_id=1, source_target_pairs={{0,4},{1,5},{2,6},{3,7},{4,0},{5,1},{6,2},{7,3},{8,12},{9,13},{10,... | collective-permute-start | bytes 196616 | tf_op jit(solution)/shard_map/ppermute | solution.py:19
  89.2 1.5 %collective-permute-start.22 = (bf16[16,2048]{1,0:T(8,128)(2,1)S(1)}, bf16[16,2048]{1,0:T(8,128)(2,1)S(1)}, u32[]{:S(2)}, u32[]{:S(2)}) collective-permute-start(bf16[16,2048]{1,0:T(8,128)(2,1)S(1)} %get-tuple-element.28), channel_id=1, source_target_pairs={{0,6},{1,7},{2,4},{3,5},{4,2},{5,3},{6,0},{7,1},{8,14},{9,15},{10,... | collective-permute-start | bytes 196616 | tf_op jit(solution)/shard_map/ppermute | solution.py:19
  90.7 0.9 collective-permute-done.20
  91.6 2.7 %collective-permute-done.21 = bf16[16,2048]{1,0:T(8,128)(2,1)S(1)} collective-permute-done((bf16[16,2048]{1,0:T(8,128)(2,1)S(1)}, bf16[16,2048]{1,0:T(8,128)(2,1)S(1)}, u32[]{:S(2)}, u32[]{:S(2)}) %collective-permute-start.21) | collective-permute-done | bytes 65568 | tf_op jit(solution)/shard_map/ppermute | solution.py:19
  94.3 1.1 collective-permute-done.22
  95.4 1.0 collective-permute-start.23
  96.4 1.5 %collective-permute-start.24 = (bf16[16,2048]{1,0:T(8,128)(2,1)S(1)}, bf16[16,2048]{1,0:T(8,128)(2,1)S(1)}, u32[]{:S(2)}, u32[]{:S(2)}) collective-permute-start(bf16[16,2048]{1,0:T(8,128)(2,1)S(1)} %fusion.11), channel_id=1, source_target_pairs={{0,16},{8,24},{16,0},{24,8},{1,17},{9,25},{17,1},{25,9},{2,18},{10... | collective-permute-start | bytes 196616 | tf_op jit(solution)/shard_map/ppermute | solution.py:19
  97.9 1.1 collective-permute-start.25
  99.0 9.5 %convolution_convert_fusion = bf16[1024,2048]{1,0:T(8,128)(2,1)} fusion(bf16[1024,1024]{1,0:T(8,128)(2,1)} %get-tuple-element.12, bf16[2048,1024]{1,0:T(8,128)(2,1)} %param.10), kind=kOutput, calls=%fused_computation | convolution fusion | flops 4297064448 | bytes 10485760 | tf_op jit(solution)/shard_map/dot_general | solution.py:199
  108.5 1.4 %fusion = f32[64,1024]{1,0:T(8,128)S(1)} fusion(bf16[1024,2048]{1,0:T(8,128)(2,1)S(1)} %copy-done, bf16[16,2048]{1,0:T(8,128)(2,1)S(1)} %collective-permute-done.25, bf16[16,2048]{1,0:T(8,128)(2,1)S(1)} %collective-permute-done.24, bf16[16,2048]{1,0:T(8,128)(2,1)S(1)} %collective-permute-done.23, bf16[16,2048]{1,0:T(8,128)(2,1)S(1)} %fusion.11), kind=kOutput, calls=%fused_computation.4 | convolution fusion | flops 269484032 | bytes 4718592 | tf_op jit(solution)/shard_map/dot_general | solution.py:189
  110.0 1.0 collective-permute-start.26
  111.0 1.6 %collective-permute-start.27 = (f32[16,1024]{1,0:T(8,128)S(1)}, f32[16,1024]{1,0:T(8,128)S(1)}, u32[]{:S(2)}, u32[]{:S(2)}) collective-permute-start(f32[16,1024]{1,0:T(8,128)S(1)} %get-tuple-element.25), channel_id=1, source_target_pairs={{0,16},{8,24},{16,0},{24,8},{1,17},{9,25},{17,1},{25,9},{2,18},{10... | collective-permute-start | bytes 196616 | tf_op jit(solution)/shard_map/ppermute | solution.py:19
  112.5 1.1 collective-permute-start.28
  113.6 0.7 collective-permute-done.26
  114.3 1.0 collective-permute-done.27
  115.3 2.4 %collective-permute-done.28 = f32[16,1024]{1,0:T(8,128)S(1)} collective-permute-done((f32[16,1024]{1,0:T(8,128)S(1)}, f32[16,1024]{1,0:T(8,128)S(1)}, u32[]{:S(2)}, u32[]{:S(2)}) %collective-permute-start.28) | collective-permute-done | bytes 65568 | tf_op jit(solution)/shard_map/ppermute | solution.py:19
  117.7 0.0 copy-start.12
  117.7 0.7 copy-done.12
  (42 shorter events, 0.3 us)
Async XLA Ops:
  0.7 40.9 %copy-start.13 = (bf16[4,256,2048]{2,1,0:T(8,128)(2,1)S(1)}, bf16[4,256,2048]{2,1,0:T(8,128)(2,1)}, u32[]{:S(2)}) copy-start(bf16[4,256,2048]{2,1,0:T(8,128)(2,1)} %param.9) | copy-start | bytes 12582916
  1.6 4.9 %collective-permute-start = (bf16[16,1024]{1,0:T(8,128)(2,1)S(1)}, bf16[16,1024]{1,0:T(8,128)(2,1)S(1)}, u32[]{:S(2)}, u32[]{:S(2)}) collective-permute-start(bf16[16,1024]{1,0:T(8,128)(2,1)S(1)} %get-tuple-element.31), channel_id=1, source_target_pairs={{0,8},{8,0},{16,24},{24,16},{1,9},{9,1},{17,25},{25,17},{2,10},{10... | collective-permute-start | bytes 98312 | tf_op jit(solution)/shard_map/ppermute | solution.py:19
  4.7 3.9 %collective-permute-start.1 = (bf16[16,1024]{1,0:T(8,128)(2,1)S(1)}, bf16[16,1024]{1,0:T(8,128)(2,1)S(1)}, u32[]{:S(2)}, u32[]{:S(2)}) collective-permute-start(bf16[16,1024]{1,0:T(8,128)(2,1)S(1)} %get-tuple-element.33), channel_id=1, source_target_pairs={{0,16},{8,24},{16,0},{24,8},{1,17},{9,25},{17,1},{25,9},{2,18},{10... | collective-permute-start | bytes 98312 | tf_op jit(solution)/shard_map/ppermute | solution.py:19
  6.2 4.8 %collective-permute-start.2 = (bf16[16,1024]{1,0:T(8,128)(2,1)S(1)}, bf16[16,1024]{1,0:T(8,128)(2,1)S(1)}, u32[]{:S(2)}, u32[]{:S(2)}) collective-permute-start(bf16[16,1024]{1,0:T(8,128)(2,1)S(1)} %get-tuple-element.32), channel_id=1, source_target_pairs={{0,24},{8,16},{16,8},{24,0},{1,25},{9,17},{17,9},{25,1},{2,26},{10... | collective-permute-start | bytes 98312 | tf_op jit(solution)/shard_map/ppermute | solution.py:19
  14.1 5.1 %collective-permute-start.3 = (f32[16,2048]{1,0:T(8,128)S(1)}, f32[16,2048]{1,0:T(8,128)S(1)}, u32[]{:S(2)}, u32[]{:S(2)}) collective-permute-start(f32[16,2048]{1,0:T(8,128)S(1)} %get-tuple-element.21), channel_id=1, source_target_pairs={{0,8},{8,0},{16,24},{24,16},{1,9},{9,1},{17,25},{25,17},{2,10},{10... | collective-permute-start | bytes 393224 | tf_op jit(solution)/shard_map/ppermute | solution.py:19
  14.7 6.4 %collective-permute-start.4 = (f32[16,2048]{1,0:T(8,128)S(1)}, f32[16,2048]{1,0:T(8,128)S(1)}, u32[]{:S(2)}, u32[]{:S(2)}) collective-permute-start(f32[16,2048]{1,0:T(8,128)S(1)} %get-tuple-element.23), channel_id=1, source_target_pairs={{0,16},{8,24},{16,0},{24,8},{1,17},{9,25},{17,1},{25,9},{2,18},{10... | collective-permute-start | bytes 393224 | tf_op jit(solution)/shard_map/ppermute | solution.py:19
  14.7 6.3 %collective-permute-start.5 = (f32[16,2048]{1,0:T(8,128)S(1)}, f32[16,2048]{1,0:T(8,128)S(1)}, u32[]{:S(2)}, u32[]{:S(2)}) collective-permute-start(f32[16,2048]{1,0:T(8,128)S(1)} %get-tuple-element.22), channel_id=1, source_target_pairs={{0,24},{8,16},{16,8},{24,0},{1,25},{9,17},{17,9},{25,1},{2,26},{10... | collective-permute-start | bytes 393224 | tf_op jit(solution)/shard_map/ppermute | solution.py:19
  21.1 5.2 %collective-permute-start.7 = (bf16[16,2048]{1,0:T(8,128)(2,1)S(1)}, bf16[16,2048]{1,0:T(8,128)(2,1)S(1)}, u32[]{:S(2)}, u32[]{:S(2)}) collective-permute-start(bf16[16,2048]{1,0:T(8,128)(2,1)S(1)} %fusion.14), channel_id=1, source_target_pairs={{0,4},{1,5},{2,6},{3,7},{4,0},{5,1},{6,2},{7,3},{8,12},{9,13},{10,... | collective-permute-start | bytes 196616 | tf_op jit(solution)/shard_map/ppermute | solution.py:19
  23.8 6.2 %collective-permute-start.8 = (bf16[16,2048]{1,0:T(8,128)(2,1)S(1)}, bf16[16,2048]{1,0:T(8,128)(2,1)S(1)}, u32[]{:S(2)}, u32[]{:S(2)}) collective-permute-start(bf16[16,2048]{1,0:T(8,128)(2,1)S(1)} %fusion.14), channel_id=1, source_target_pairs={{0,6},{1,7},{2,4},{3,5},{4,2},{5,3},{6,0},{7,1},{8,14},{9,15},{10,... | collective-permute-start | bytes 196616 | tf_op jit(solution)/shard_map/ppermute | solution.py:19
  25.1 5.0 %collective-permute-start.6 = (bf16[16,2048]{1,0:T(8,128)(2,1)S(1)}, bf16[16,2048]{1,0:T(8,128)(2,1)S(1)}, u32[]{:S(2)}, u32[]{:S(2)}) collective-permute-start(bf16[16,2048]{1,0:T(8,128)(2,1)S(1)} %fusion.14), channel_id=1, source_target_pairs={{0,2},{1,3},{2,0},{3,1},{4,6},{5,7},{6,4},{7,5},{8,10},{9,11},{10,... | collective-permute-start | bytes 196616 | tf_op jit(solution)/shard_map/ppermute | solution.py:19
  30.1 19.3 %copy-start.1 = (bf16[4,16,2048]{2,1,0:T(8,128)(2,1)}, bf16[4,16,2048]{2,1,0:T(8,128)(2,1)S(1)}, u32[]{:S(2)}) copy-start(bf16[4,16,2048]{2,1,0:T(8,128)(2,1)S(1)} %pad_maximum_fusion.refs_0_) | copy-start | bytes 786436
  30.1 6.6 %collective-permute-start.9 = (bf16[4,16,2048]{2,1,0:T(8,128)(2,1)S(1)}, bf16[4,16,2048]{2,1,0:T(8,128)(2,1)S(1)}, u32[]{:S(2)}, u32[]{:S(2)}) collective-permute-start(bf16[4,16,2048]{2,1,0:T(8,128)(2,1)S(1)} %pad_maximum_fusion.refs_0_), channel_id=1, source_target_pairs={{0,8},{8,0},{16,24},{24,16},{1,9},{9,1},{17,25},{25,17},{2,10},{10... | collective-permute-start | bytes 786440 | tf_op jit(solution)/shard_map/ppermute | solution.py:19
  31.9 9.2 %collective-permute-start.10 = (bf16[4,16,2048]{2,1,0:T(8,128)(2,1)S(1)}, bf16[4,16,2048]{2,1,0:T(8,128)(2,1)S(1)}, u32[]{:S(2)}, u32[]{:S(2)}) collective-permute-start(bf16[4,16,2048]{2,1,0:T(8,128)(2,1)S(1)} %pad_maximum_fusion.refs_0_), channel_id=1, source_target_pairs={{0,16},{8,24},{16,0},{24,8},{1,17},{9,25},{17,1},{25,9},{2,18},{10... | collective-permute-start | bytes 786440 | tf_op jit(solution)/shard_map/ppermute | solution.py:19
  33.2 7.9 %collective-permute-start.11 = (bf16[4,16,2048]{2,1,0:T(8,128)(2,1)S(1)}, bf16[4,16,2048]{2,1,0:T(8,128)(2,1)S(1)}, u32[]{:S(2)}, u32[]{:S(2)}) collective-permute-start(bf16[4,16,2048]{2,1,0:T(8,128)(2,1)S(1)} %pad_maximum_fusion.refs_0_), channel_id=1, source_target_pairs={{0,24},{8,16},{16,8},{24,0},{1,25},{9,17},{17,9},{25,1},{2,26},{10... | collective-permute-start | bytes 786440 | tf_op jit(solution)/shard_map/ppermute | solution.py:19
  33.7 16.4 %collective-permute-start.12 = (bf16[4,16,2048]{2,1,0:T(8,128)(2,1)S(1)}, bf16[4,16,2048]{2,1,0:T(8,128)(2,1)S(1)}, u32[]{:S(2)}, u32[]{:S(2)}) collective-permute-start(bf16[4,16,2048]{2,1,0:T(8,128)(2,1)S(1)} %pad_maximum_fusion.refs_0_), channel_id=1, source_target_pairs={{0,1},{1,0},{2,3},{3,2},{4,5},{5,4},{6,7},{7,6},{8,9},{9,8},{10,11... | collective-permute-start | bytes 786440 | tf_op jit(solution)/shard_map/ppermute | solution.py:19
  36.7 12.7 %copy-start.2 = (bf16[4,16,2048]{2,1,0:T(8,128)(2,1)}, bf16[4,16,2048]{2,1,0:T(8,128)(2,1)S(1)}, u32[]{:S(2)}) copy-start(bf16[4,16,2048]{2,1,0:T(8,128)(2,1)S(1)} %collective-permute-done.9.refs_1_) | copy-start | bytes 786436
  36.7 13.4 %collective-permute-start.13 = (bf16[4,16,2048]{2,1,0:T(8,128)(2,1)S(1)}, bf16[4,16,2048]{2,1,0:T(8,128)(2,1)S(1)}, u32[]{:S(2)}, u32[]{:S(2)}) collective-permute-start(bf16[4,16,2048]{2,1,0:T(8,128)(2,1)S(1)} %collective-permute-done.9.refs_1_), channel_id=1, source_target_pairs={{0,1},{1,0},{2,3},{3,2},{4,5},{5,4},{6,7},{7,6},{8,9},{9,8},{10,11... | collective-permute-start | bytes 786440 | tf_op jit(solution)/shard_map/ppermute | solution.py:19
  41.0 8.4 %copy-start.3 = (bf16[4,16,2048]{2,1,0:T(8,128)(2,1)}, bf16[4,16,2048]{2,1,0:T(8,128)(2,1)S(1)}, u32[]{:S(2)}) copy-start(bf16[4,16,2048]{2,1,0:T(8,128)(2,1)S(1)} %collective-permute-done.10.refs_2_) | copy-start | bytes 786436
  41.0 9.0 %collective-permute-start.14 = (bf16[4,16,2048]{2,1,0:T(8,128)(2,1)S(1)}, bf16[4,16,2048]{2,1,0:T(8,128)(2,1)S(1)}, u32[]{:S(2)}, u32[]{:S(2)}) collective-permute-start(bf16[4,16,2048]{2,1,0:T(8,128)(2,1)S(1)} %collective-permute-done.10.refs_2_), channel_id=1, source_target_pairs={{0,1},{1,0},{2,3},{3,2},{4,5},{5,4},{6,7},{7,6},{8,9},{9,8},{10,11... | collective-permute-start | bytes 786440 | tf_op jit(solution)/shard_map/ppermute | solution.py:19
  41.1 8.4 %copy-start.4 = (bf16[4,16,2048]{2,1,0:T(8,128)(2,1)}, bf16[4,16,2048]{2,1,0:T(8,128)(2,1)S(1)}, u32[]{:S(2)}) copy-start(bf16[4,16,2048]{2,1,0:T(8,128)(2,1)S(1)} %collective-permute-done.11.refs_3_) | copy-start | bytes 786436
  41.1 9.0 %collective-permute-start.15 = (bf16[4,16,2048]{2,1,0:T(8,128)(2,1)S(1)}, bf16[4,16,2048]{2,1,0:T(8,128)(2,1)S(1)}, u32[]{:S(2)}, u32[]{:S(2)}) collective-permute-start(bf16[4,16,2048]{2,1,0:T(8,128)(2,1)S(1)} %collective-permute-done.11.refs_3_), channel_id=1, source_target_pairs={{0,1},{1,0},{2,3},{3,2},{4,5},{5,4},{6,7},{7,6},{8,9},{9,8},{10,11... | collective-permute-start | bytes 786440 | tf_op jit(solution)/shard_map/ppermute | solution.py:19
  50.1 0.7 copy-start.5
  50.1 0.8 copy-start.6
  50.1 0.9 copy-start.7
  50.1 0.9 copy-start.8
  65.2 9.5 %collective-permute-start.16 = (bf16[4,16,2048]{2,1,0:T(8,128)(2,1)}, bf16[4,16,2048]{2,1,0:T(8,128)(2,1)S(1)}, u32[]{:S(2)}, u32[]{:S(2)}) collective-permute-start(bf16[4,16,2048]{2,1,0:T(8,128)(2,1)} %get-tuple-element.14), channel_id=1, source_target_pairs={{0,8},{8,0},{16,24},{24,16},{1,9},{9,1},{17,25},{25,17},{2,10},{10... | collective-permute-start | bytes 786440 | tf_op jit(solution)/shard_map/ppermute | solution.py:19
  66.0 9.3 %collective-permute-start.17 = (bf16[4,16,2048]{2,1,0:T(8,128)(2,1)}, bf16[4,16,2048]{2,1,0:T(8,128)(2,1)S(1)}, u32[]{:S(2)}, u32[]{:S(2)}) collective-permute-start(bf16[4,16,2048]{2,1,0:T(8,128)(2,1)} %get-tuple-element.15), channel_id=1, source_target_pairs={{0,16},{8,24},{16,0},{24,8},{1,17},{9,25},{17,1},{25,9},{2,18},{10... | collective-permute-start | bytes 786440 | tf_op jit(solution)/shard_map/ppermute | solution.py:19
  67.2 13.1 %collective-permute-start.18 = (bf16[4,16,2048]{2,1,0:T(8,128)(2,1)}, bf16[4,16,2048]{2,1,0:T(8,128)(2,1)S(1)}, u32[]{:S(2)}, u32[]{:S(2)}) collective-permute-start(bf16[4,16,2048]{2,1,0:T(8,128)(2,1)} %get-tuple-element.16), channel_id=1, source_target_pairs={{0,24},{8,16},{16,8},{24,0},{1,25},{9,17},{17,9},{25,1},{2,26},{10... | collective-permute-start | bytes 786440 | tf_op jit(solution)/shard_map/ppermute | solution.py:19
  74.7 5.6 %copy-start.9 = (bf16[4,16,2048]{2,1,0:T(8,128)(2,1)}, bf16[4,16,2048]{2,1,0:T(8,128)(2,1)S(1)}, u32[]{:S(2)}) copy-start(bf16[4,16,2048]{2,1,0:T(8,128)(2,1)S(1)} %collective-permute-done.16.refs_1_) | copy-start | bytes 786436
  75.3 5.0 %copy-start.10 = (bf16[4,16,2048]{2,1,0:T(8,128)(2,1)}, bf16[4,16,2048]{2,1,0:T(8,128)(2,1)S(1)}, u32[]{:S(2)}) copy-start(bf16[4,16,2048]{2,1,0:T(8,128)(2,1)S(1)} %collective-permute-done.17.refs_2_) | copy-start | bytes 786436
  80.3 0.7 copy-start.11
  83.4 1.7 %collective-permute-start.19 = (bf16[4,16,2048]{2,1,0:T(8,128)(2,1)}, bf16[4,16,2048]{2,1,0:T(8,128)(2,1)S(1)}, u32[]{:S(2)}, u32[]{:S(2)}) collective-permute-start(bf16[4,16,2048]{2,1,0:T(8,128)(2,1)} %get-tuple-element.18), channel_id=1, source_target_pairs={{0,1},{1,0},{2,3},{3,2},{4,5},{5,4},{6,7},{7,6},{8,9},{9,8},{10,11... | collective-permute-start | bytes 786440 | tf_op jit(solution)/shard_map/ppermute | solution.py:19
  86.3 5.3 %collective-permute-start.20 = (bf16[16,2048]{1,0:T(8,128)(2,1)S(1)}, bf16[16,2048]{1,0:T(8,128)(2,1)S(1)}, u32[]{:S(2)}, u32[]{:S(2)}) collective-permute-start(bf16[16,2048]{1,0:T(8,128)(2,1)S(1)} %get-tuple-element.27), channel_id=1, source_target_pairs={{0,2},{1,3},{2,0},{3,1},{4,6},{5,7},{6,4},{7,5},{8,10},{9,11},{10,... | collective-permute-start | bytes 196616 | tf_op jit(solution)/shard_map/ppermute | solution.py:19
  86.6 7.7 %collective-permute-start.21 = (bf16[16,2048]{1,0:T(8,128)(2,1)S(1)}, bf16[16,2048]{1,0:T(8,128)(2,1)S(1)}, u32[]{:S(2)}, u32[]{:S(2)}) collective-permute-start(bf16[16,2048]{1,0:T(8,128)(2,1)S(1)} %get-tuple-element.29), channel_id=1, source_target_pairs={{0,4},{1,5},{2,6},{3,7},{4,0},{5,1},{6,2},{7,3},{8,12},{9,13},{10,... | collective-permute-start | bytes 196616 | tf_op jit(solution)/shard_map/ppermute | solution.py:19
  89.2 6.2 %collective-permute-start.22 = (bf16[16,2048]{1,0:T(8,128)(2,1)S(1)}, bf16[16,2048]{1,0:T(8,128)(2,1)S(1)}, u32[]{:S(2)}, u32[]{:S(2)}) collective-permute-start(bf16[16,2048]{1,0:T(8,128)(2,1)S(1)} %get-tuple-element.28), channel_id=1, source_target_pairs={{0,6},{1,7},{2,4},{3,5},{4,2},{5,3},{6,0},{7,1},{8,14},{9,15},{10,... | collective-permute-start | bytes 196616 | tf_op jit(solution)/shard_map/ppermute | solution.py:19
  95.4 13.1 %collective-permute-start.23 = (bf16[16,2048]{1,0:T(8,128)(2,1)S(1)}, bf16[16,2048]{1,0:T(8,128)(2,1)S(1)}, u32[]{:S(2)}, u32[]{:S(2)}) collective-permute-start(bf16[16,2048]{1,0:T(8,128)(2,1)S(1)} %fusion.11), channel_id=1, source_target_pairs={{0,8},{8,0},{16,24},{24,16},{1,9},{9,1},{17,25},{25,17},{2,10},{10... | collective-permute-start | bytes 196616 | tf_op jit(solution)/shard_map/ppermute | solution.py:19
  96.4 12.1 %collective-permute-start.24 = (bf16[16,2048]{1,0:T(8,128)(2,1)S(1)}, bf16[16,2048]{1,0:T(8,128)(2,1)S(1)}, u32[]{:S(2)}, u32[]{:S(2)}) collective-permute-start(bf16[16,2048]{1,0:T(8,128)(2,1)S(1)} %fusion.11), channel_id=1, source_target_pairs={{0,16},{8,24},{16,0},{24,8},{1,17},{9,25},{17,1},{25,9},{2,18},{10... | collective-permute-start | bytes 196616 | tf_op jit(solution)/shard_map/ppermute | solution.py:19
  97.9 10.6 %collective-permute-start.25 = (bf16[16,2048]{1,0:T(8,128)(2,1)S(1)}, bf16[16,2048]{1,0:T(8,128)(2,1)S(1)}, u32[]{:S(2)}, u32[]{:S(2)}) collective-permute-start(bf16[16,2048]{1,0:T(8,128)(2,1)S(1)} %fusion.11), channel_id=1, source_target_pairs={{0,24},{8,16},{16,8},{24,0},{1,25},{9,17},{17,9},{25,1},{2,26},{10... | collective-permute-start | bytes 196616 | tf_op jit(solution)/shard_map/ppermute | solution.py:19
  99.0 9.5 %copy-start = (bf16[1024,2048]{1,0:T(8,128)(2,1)S(1)}, bf16[1024,2048]{1,0:T(8,128)(2,1)}, u32[]{:S(2)}) copy-start(bf16[1024,2048]{1,0:T(8,128)(2,1)} %param.8) | copy-start | bytes 12582916
  110.0 4.3 %collective-permute-start.26 = (f32[16,1024]{1,0:T(8,128)S(1)}, f32[16,1024]{1,0:T(8,128)S(1)}, u32[]{:S(2)}, u32[]{:S(2)}) collective-permute-start(f32[16,1024]{1,0:T(8,128)S(1)} %get-tuple-element.26), channel_id=1, source_target_pairs={{0,8},{8,0},{16,24},{24,16},{1,9},{9,1},{17,25},{25,17},{2,10},{10... | collective-permute-start | bytes 196616 | tf_op jit(solution)/shard_map/ppermute | solution.py:19
  111.0 4.3 %collective-permute-start.27 = (f32[16,1024]{1,0:T(8,128)S(1)}, f32[16,1024]{1,0:T(8,128)S(1)}, u32[]{:S(2)}, u32[]{:S(2)}) collective-permute-start(f32[16,1024]{1,0:T(8,128)S(1)} %get-tuple-element.25), channel_id=1, source_target_pairs={{0,16},{8,24},{16,0},{24,8},{1,17},{9,25},{17,1},{25,9},{2,18},{10... | collective-permute-start | bytes 196616 | tf_op jit(solution)/shard_map/ppermute | solution.py:19
  112.5 5.2 %collective-permute-start.28 = (f32[16,1024]{1,0:T(8,128)S(1)}, f32[16,1024]{1,0:T(8,128)S(1)}, u32[]{:S(2)}, u32[]{:S(2)}) collective-permute-start(f32[16,1024]{1,0:T(8,128)S(1)} %get-tuple-element.24), channel_id=1, source_target_pairs={{0,24},{8,16},{16,8},{24,0},{1,25},{9,17},{17,9},{25,1},{2,26},{10... | collective-permute-start | bytes 196616 | tf_op jit(solution)/shard_map/ppermute | solution.py:19
  117.7 0.7 copy-start.12

commit v2 on v1

v2 whole, which is shorter than its diff:
```python
import math

import jax
import jax.numpy as jnp
from jax import lax
from jax.experimental import pallas as pl
from jax.experimental.pallas import tpu as pltpu
from jax.sharding import PartitionSpec as P

HEADS = 8
HD = 128
NEG_FILL = -1e30
HALVES = 2
F32 = jnp.float32
BF16 = jnp.bfloat16
MIB = 1 << 20
NN = (((1,), (0,)), ((), ()))
NT = (((1,), (1,)), ((), ()))
TN = (((0,), (0,)), ((), ()))
VMEM = pl.BlockSpec(memory_space=pltpu.VMEM)
SMEM = pl.BlockSpec(memory_space=pltpu.SMEM)
ANY = pl.BlockSpec(memory_space=pl.ANY)
HBM = pl.BlockSpec(memory_space=pltpu.HBM)


def dot(a, b, dims):
    return lax.dot_general(a, b, dims, preferred_element_type=F32)


def partner(x, axis, size, k):
    return lax.ppermute(x, axis, [(i, i ^ k) for i in range(size)])


def shape_of(*dims, dtype=BF16):
    return jax.ShapeDtypeStruct(dims, dtype)


def params(limit):
    return pltpu.CompilerParams(vmem_limit_bytes=limit * MIB)


def cost(flops, size):
    return pl.CostEstimate(flops=flops, bytes_accessed=size, transcendentals=0)


def project(blocks, weight, dims, width):
    n = len(blocks)
    rows = blocks[0].shape[0]
    step = min(width, 512)

    def body(*refs):
        w_ref = refs[n]
        left = jnp.concatenate([r[...] for r in refs[:n]], axis=0)
        for start in range(0, width, step):
            cols = slice(start, start + step)
            w = w_ref[:, cols] if dims is NN else w_ref[cols, :]
            out = dot(left, w, dims)
            for k in range(n):
                refs[n + 1 + k][:, cols] = out[k * rows : (k + 1) * rows]

    return pl.pallas_call(
        body,
        in_specs=[VMEM] * (n + 1),
        out_specs=[VMEM] * n,
        out_shape=[shape_of(rows, width, dtype=F32)] * n,
        compiler_params=params(16),
        cost_estimate=cost(2 * n * rows * weight.size, weight.size * 2),
        name="project",
    )(*blocks, weight)


def far(x):
    return pltpu.with_memory_space_constraint(x, pltpu.HBM)


def fetch(arrays):
    n = len(arrays)

    def body(*refs):
        sem = refs[-1]
        copies = [pltpu.make_async_copy(refs[i], refs[n + i], sem.at[i]) for i in range(n)]
        for c in copies:
            c.start()
        for c in copies:
            c.wait()

    return pl.pallas_call(
        body,
        in_specs=[HBM] * n,
        out_specs=[VMEM] * n,
        out_shape=[shape_of(*a.shape) for a in arrays],
        scratch_shapes=[pltpu.SemaphoreType.DMA((n,))],
        compiler_params=params(16),
        cost_estimate=cost(0, sum(a.size for a in arrays) * 4),
        name="fetch",
    )(*[far(a) for a in arrays])


def query_product(tokens, weight, row0, rows):
    depth, width = weight.shape
    step = 256
    steps = rows // step

    def body(x_ref, w_ref, o_ref, x_buf, o_buf, x_sem, o_sem):
        def get(i):
            at = pl.ds(row0 + i * step, step)
            return pltpu.make_async_copy(x_ref.at[at, :], x_buf.at[i], x_sem.at[i])

        def put(i):
            at = pl.ds(i * step, step)
            return pltpu.make_async_copy(o_buf.at[i], o_ref.at[at, :], o_sem.at[i])

        for i in range(steps):
            get(i).start()
        for i in range(steps):
            get(i).wait()
            o_buf[i] = dot(x_buf[i], w_ref[...], NN).astype(BF16)
            put(i).start()
        for i in range(steps):
            put(i).wait()

    return pl.pallas_call(
        body,
        in_specs=[HBM, VMEM],
        out_specs=HBM,
        out_shape=pltpu.HBM((rows, width), BF16),
        scratch_shapes=[
            pltpu.VMEM((steps, step, depth), BF16),
            pltpu.VMEM((steps, step, width), BF16),
            pltpu.SemaphoreType.DMA((steps,)),
            pltpu.SemaphoreType.DMA((steps,)),
        ],
        compiler_params=params(24),
        cost_estimate=cost(2 * rows * depth * width, 2 * (rows * depth + depth * width)),
        name="query_product",
    )(far(tokens), weight)


def image_product(d_queries, weight, held, row0, total):
    rows, depth = d_queries.shape
    width = weight.shape[0]
    step = 256
    steps = rows // step

    def body(x_ref, w_ref, *refs):
        o_ref, buf, sem = refs[-3:]

        def put(i):
            return pltpu.make_async_copy(
                buf.at[i], o_ref.at[pl.ds(row0 + i * step, step), :], sem.at[i]
            )

        for i in range(steps):
            buf[i] = dot(x_ref[i * step : (i + 1) * step, :], w_ref[...], NT).astype(BF16)
            put(i).start()
        for i in range(steps):
            put(i).wait()

    more = [] if held is None else [held]
    return pl.pallas_call(
        body,
        in_specs=[VMEM, VMEM] + [ANY] * len(more),
        out_specs=ANY,
        out_shape=shape_of(total, width),
        scratch_shapes=[pltpu.VMEM((steps, step, width), BF16), pltpu.SemaphoreType.DMA((steps,))],
        input_output_aliases={2: 0} if more else {},
        compiler_params=params(24),
        cost_estimate=cost(2 * rows * depth * width, 2 * (rows * depth + depth * width)),
        name="image_product",
    )(d_queries, weight, *more)


def select(ids, prompt_of, same, other, dims):
    samp_dev, n_grp, n_dev, halves = dims
    _, block_len, width = same.shape
    part = samp_dev // halves

    def body(ids_ref, prompt_ref, same_ref, other_ref, *outs):
        for k in range(n_grp):
            base = ((ids_ref[0] ^ k) * n_dev + ids_ref[1]) * samp_dev
            for s in range(samp_dev):
                rel = prompt_ref[base + s] ^ ids_ref[1]
                out = outs[k * halves + s // part]

                @pl.when(rel & 1 == 0)
                def _():
                    out[s % part] = same_ref[rel >> 1]

                @pl.when(rel & 1 == 1)
                def _():
                    out[s % part] = other_ref[rel >> 1]

    return pl.pallas_call(
        body,
        in_specs=[SMEM, SMEM, VMEM, VMEM],
        out_specs=[VMEM] * (n_grp * halves),
        out_shape=[shape_of(part, block_len, width)] * (n_grp * halves),
        compiler_params=params(16),
        name="select",
    )(ids, prompt_of, same, other)


def attend(ids, prompt_of, lens, queries, grads, slots, held, first, dims):
    samp_dev, img_len, inner, n_grp, n_dev = dims
    part, block_len, _ = slots[0].shape
    full_len = n_grp * block_len
    scale = 1.0 / math.sqrt(HD)

    def body(ids_ref, prompt_ref, len_ref, q_ref, g_ref, *refs):
        ins = refs[:n_grp]
        dq_ref, ctx_ref = refs[-(n_grp + 4)], refs[-(n_grp + 3)]
        outs = refs[-(n_grp + 2) : -2]
        buf, sem = refs[-2:]
        row = lax.broadcasted_iota(jnp.int32, (full_len, 1), 0)
        token = ((row // block_len) ^ ids_ref[0]) * block_len + row % block_len
        zero = jnp.zeros((full_len, HD), BF16)
        base = (ids_ref[0] * n_dev + ids_ref[1]) * samp_dev + first

        def put(s):
            return pltpu.make_async_copy(
                buf.at[s], ctx_ref.at[pl.ds((first + s) * img_len, img_len), :], sem.at[s]
            )

        def sample(s):
            at = slice(s * img_len, (s + 1) * img_len)
            all_at = slice((first + s) * img_len, (first + s + 1) * img_len)
            live = (token < len_ref[prompt_ref[base + s]])[None]
            kv = jnp.concatenate([r[s] for r in ins], axis=0)
            for h in range(0, HEADS, 2):
                one = slice(h * HD, (h + 1) * HD)
                two = slice((h + 1) * HD, (h + 2) * HD)
                pair = slice(h * HD, (h + 2) * HD)
                v_one = slice(inner + h * HD, inner + (h + 1) * HD)
                v_two = slice(inner + (h + 1) * HD, inner + (h + 2) * HD)
                k1, k2, v1, v2 = kv[:, one], kv[:, two], kv[:, v_one], kv[:, v_two]
                keys = jnp.concatenate(
                    [jnp.concatenate([k1, zero], 1), jnp.concatenate([zero, k2], 1)], 0
                )
                values = jnp.concatenate(
                    [jnp.concatenate([v1, zero], 1), jnp.concatenate([zero, v2], 1)], 0
                )
                scores = jnp.stack([dot(k1, q_ref[at, one], NT), dot(k2, q_ref[at, two], NT)])
                d_soft = jnp.stack(
                    [dot(v1, g_ref[all_at, one], NT), dot(v2, g_ref[all_at, two], NT)]
                )
                scores = jnp.where(live, scores * scale, NEG_FILL)
                expd = jnp.exp(scores - jnp.max(scores, axis=1, keepdims=True))
                soft = expd * (1.0 / jnp.sum(expd, axis=1, keepdims=True))
                soft_b = soft.astype(BF16).reshape(2 * full_len, img_len)
                mean = jnp.sum(d_soft * soft, axis=1, keepdims=True)
                d_scores = (
                    (soft * (d_soft - mean) * scale).astype(BF16).reshape(2 * full_len, img_len)
                )
                buf[s, :, pair] = dot(soft_b, values, TN).astype(BF16)
                dq_ref[at, pair] = dot(d_scores, keys, TN).astype(BF16)
                d_keys = dot(d_scores, q_ref[at, pair], NN).astype(BF16)
                d_values = dot(soft_b, g_ref[all_at, pair], NN).astype(BF16)
                for k in range(n_grp):
                    a = slice(k * block_len, (k + 1) * block_len)
                    b = slice(full_len + k * block_len, full_len + (k + 1) * block_len)
                    outs[k][s, :, one] = d_keys[a, :HD]
                    outs[k][s, :, two] = d_keys[b, HD:]
                    outs[k][s, :, v_one] = d_values[a, :HD]
                    outs[k][s, :, v_two] = d_values[b, HD:]
            put(s).start()

        for s in range(part):
            sample(s)
        for s in range(part):
            put(s).wait()

    more = [] if held is None else [held]
    rows = part * img_len
    return pl.pallas_call(
        body,
        in_specs=[SMEM, SMEM, SMEM, VMEM, VMEM] + [VMEM] * n_grp + [ANY] * len(more),
        out_specs=[VMEM, ANY] + [VMEM] * n_grp,
        out_shape=[shape_of(rows, inner), shape_of(samp_dev * img_len, inner)]
        + [shape_of(part, block_len, 2 * inner)] * n_grp,
        scratch_shapes=[pltpu.VMEM((part, img_len, inner), BF16), pltpu.SemaphoreType.DMA((part,))],
        input_output_aliases={5 + n_grp: 1} if more else {},
        compiler_params=params(24),
        cost_estimate=cost(20 * rows * full_len * inner, 8 * rows * inner),
        name="attend",
    )(ids, prompt_of, lens, queries, grads, *slots, *more)


def combine(ids, prompt_of, arrived, dims):
    samp_dev, n_grp, n_dev, halves = dims
    part, block_len, width = arrived[0][0].shape
    chips = n_dev // 2

    def body(ids_ref, prompt_ref, *refs):
        same_ref, other_ref, acc_ref = refs[-3:]
        acc_ref[...] = jnp.zeros_like(acc_ref)
        for k in range(n_grp):
            base = ((ids_ref[0] ^ k) * n_dev + ids_ref[1]) * samp_dev
            for s in range(samp_dev):
                rel = prompt_ref[base + s] ^ ids_ref[1]
                slot = (rel & 1) * chips + (rel >> 1)
                acc_ref[slot] += refs[k * halves + s // part][s % part].astype(F32)
        same_ref[...] = acc_ref[:chips]
        other_ref[...] = acc_ref[chips:].astype(BF16)

    return pl.pallas_call(
        body,
        in_specs=[SMEM, SMEM] + [VMEM] * (n_grp * halves),
        out_specs=[VMEM, VMEM],
        out_shape=[
            shape_of(chips, block_len, width, dtype=F32),
            shape_of(chips, block_len, width),
        ],
        scratch_shapes=[pltpu.VMEM((2 * chips, block_len, width), F32)],
        compiler_params=params(16),
        name="combine",
    )(ids, prompt_of, *[x for pair in arrived for x in pair])


def shards(captions, kv_weight, image_tokens, q_weight, context_grad, sample_prompt, caption_len):
    n_grp = lax.axis_size("grp")
    n_dev = lax.axis_size("dev")
    grp_at = lax.axis_index("grp")
    dev_at = lax.axis_index("dev")
    samp_dev, img_len, width_img = image_tokens.shape
    _, block_len, width_cap = captions.shape
    inner = q_weight.shape[1]
    share = width_cap // n_grp
    chips = n_dev // 2
    part = samp_dev // HALVES
    rows = samp_dev * img_len
    ids = jnp.stack([grp_at, dev_at]).astype(jnp.int32)
    tokens = image_tokens.reshape(rows, width_img)
    grads = context_grad.reshape(rows, inner)

    def over_grp(blocks):
        return [blocks[0]] + [partner(blocks[k], "grp", n_grp, k) for k in range(1, n_grp)]

    whole = captions.reshape(block_len, width_cap)
    pieces = [lax.dynamic_slice_in_dim(whole, (grp_at ^ k) * share, share, 1) for k in range(n_grp)]
    (kv_near,) = fetch([kv_weight])
    partial = project(over_grp(pieces), kv_near, NN, 2 * inner)
    queries = []
    for half in range(HALVES):
        queries.append(
            query_product(tokens, q_weight, half * part * img_len, part * img_len)
        )
    *queries, grads = fetch(queries + [grads])
    summed = over_grp(partial)
    kv_block = sum(summed[1:], summed[0]).astype(BF16)

    same = jnp.stack([kv_block] + [partner(kv_block, "dev", n_dev, 2 * k) for k in range(1, chips)])
    other = partner(same, "dev", n_dev, 1)
    dims = (samp_dev, n_grp, n_dev, HALVES)
    chosen = select(ids, sample_prompt, same, other, dims)
    slots = [over_grp(chosen[half::HALVES]) for half in range(HALVES)]

    context, arrived, d_queries = None, [], []
    for half in range(HALVES):
        d_q, context, *d_kv = attend(
            ids,
            sample_prompt,
            caption_len,
            queries[half],
            grads,
            slots[half],
            context,
            half * part,
            (samp_dev, img_len, inner, n_grp, n_dev),
        )
        d_queries.append(d_q)
        arrived.append(over_grp(d_kv))

    image_grad = None
    for half in range(HALVES):
        image_grad = image_product(
            d_queries[half], q_weight, image_grad, half * part * img_len, rows
        )

    mine, theirs = combine(ids, sample_prompt, list(zip(*arrived)), dims)
    both = mine + partner(theirs, "dev", n_dev, 1).astype(F32)
    kv_grad = both[0]
    for k in range(1, chips):
        sent = partner(both[k].astype(BF16), "dev", n_dev, 2 * k)
        kv_grad = kv_grad + sent.astype(F32)
    grad_blocks = over_grp([kv_grad.astype(BF16)] * n_grp)
    shares = over_grp(project(grad_blocks, kv_weight, NT, share))
    caption_grad = jnp.zeros((block_len, width_cap), F32)
    for k in range(n_grp):
        caption_grad = lax.dynamic_update_slice_in_dim(
            caption_grad, shares[k], (grp_at ^ k) * share, 1
        )
    return (
        context.reshape(samp_dev, img_len, inner),
        image_grad.reshape(samp_dev, img_len, width_img),
        caption_grad[None],
    )


def solution(mesh):
    placed = (
        P("dev", "grp", None),
        P("grp", None),
        P(("grp", "dev"), None, None),
        P(),
        P(("grp", "dev"), None, None),
        P(),
        P(),
    )

    return jax.shard_map(
        shards,
        mesh=mesh,
        in_specs=placed,
        out_specs=(
            P(("grp", "dev"), None, None),
            P(("grp", "dev"), None, None),
            P("dev", "grp", None),
        ),
        check_vma=False,
    )
```

time: 119 us -> 105 us (0.88)
  matrix products: 21.8 us -> 0 us
  Pallas kernels: 16.6 us -> 32.9 us
  waiting for transfers between devices: 42.3 us -> 30.7 us
  starting transfers between devices: 31.6 us -> 36 us
  other arithmetic: 1.86 us -> 0.43 us
    dot_general x4 -> x0, matrix products: 21.8 us -> none  [the longest x1 9.51 us: shards(): lax.dot_general(d_queries, q_weight, (((1,), (1,)), ((), ())), preferred_...]
    pallas_call x2 -> x12, Pallas kernels: 16.6 us -> 32.9 us  [the longest x2 9.1 us: query_product(): pl.pallas_call(body, in_specs=[HBM, VMEM], out_specs=HBM, out_shape=pltpu...]
    ppermute x29 -> x32, waiting for transfers between devices: 42.3 us -> 30.7 us  [partner(): return lax.ppermute(x, axis, [(i, i ^ k) for i in range(size)])]
    ppermute x29 -> x32, starting transfers between devices: 31.6 us -> 36 us  [partner(): return lax.ppermute(x, axis, [(i, i ^ k) for i in range(size)])]
    unnamed x28 -> x12, local copies, waits for them, and re-layouts: 2.34 us -> 2.91 us
  transfers between devices with their start and end apart: 29 -> 32, of which waited for: 20 -> 19; matrix products, arithmetic and copies ran while one was open for 15% -> 0% of each run, Pallas kernels for 0% -> 24%
where the time goes in v2:
time: 105 us
  starting transfers between devices  36 us (34%)
  Pallas kernels  32.9 us (31%)
  waiting for transfers between devices  30.7 us (29%)
  local copies, waits for them, and re-layouts  3.81 us (4%)
    ppermute x32, starting transfers between devices, partner(): return lax.ppermute(x, axis, [(i, i ^ k) for i in range(size)])  36 us
    ppermute x32, waiting for transfers between devices, partner(): return lax.ppermute(x, axis, [(i, i ^ k) for i in range(size)])  30.7 us
    pallas_call x2, Pallas kernels, query_product(): pl.pallas_call(body, in_specs=[HBM, VMEM], out_specs=HBM, out_shape=pltpu...  9.1 us
    pallas_call x2, Pallas kernels, attend(): pl.pallas_call(body, in_specs=[SMEM, SMEM, SMEM, VMEM, VMEM] + [VMEM] * n...  8.67 us
    pallas_call x2, Pallas kernels, image_product(): pl.pallas_call(body, in_specs=[VMEM, VMEM] + [ANY] * len(more), out_specs...  6.77 us
    pallas_call x2, Pallas kernels, fetch(): pl.pallas_call(body, in_specs=[HBM] * n, out_specs=[VMEM] * n, out_shape=...  4.46 us
    unnamed x12, local copies, waits for them, and re-layouts  2.91 us
    pallas_call x2, Pallas kernels, project(): pl.pallas_call(body, in_specs=[VMEM] * (n + 1), out_specs=[VMEM] * n, out...  2.22 us
  transfers between devices with their start and end apart: 32, of which 19 were waited for; matrix products, arithmetic and copies ran while one was open for 0% of the time, Pallas kernels for 24%

profile of v2, /device:TPU:0, one launch (start us, length us, event | category | flops | bytes accessed | tf_op | source)
XLA Modules:
  0.0 104.8 jit_solution(7421554262756851000)
XLA Ops:
  0.7 0.8 dynamic-slice_bitcast_fusion
  1.5 4.0 %collective-permute-start.2 = (bf16[16,1024]{1,0:T(8,128)(2,1)S(1)}, bf16[16,1024]{1,0:T(8,128)(2,1)S(1)}, u32[]{:S(2)}, u32[]{:S(2)}) collective-permute-start(bf16[16,1024]{1,0:T(8,128)(2,1)S(1)} %get-tuple-element.74), channel_id=1, source_target_pairs={{0,24},{8,16},{16,8},{24,0},{1,25},{9,17},{17,9},{25,1},{2,26},{10... | collective-permute-start | bytes 98312 | tf_op jit(solution)/shard_map/ppermute | solution.py:31
  5.5 0.5 collective-permute-start
  6.0 0.1 collective-permute-start.1
  6.1 2.2 %fetch.3.refs_4_ = bf16[1024,2048]{1,0:T(8,128)(2,1)S(1)} custom-call(bf16[1024,2048]{1,0:T(8,128)(2,1)} %refs_4_.1), custom_call_target="tpu_custom_call" | custom-call | bytes 8388608 | tf_op jit(solution)/shard_map/fetch/pallas_call | solution.py:87
  8.3 1.0 collective-permute-done.refs_1_
  9.4 0.5 collective-permute-done.1.refs_2_
  9.9 0.8 project.2
  10.8 1.6 %collective-permute-start.3 = (f32[16,2048]{1,0:T(8,128)S(1)}, f32[16,2048]{1,0:T(8,128)S(1)}, u32[]{:S(2)}, u32[]{:S(2)}) collective-permute-start(f32[16,2048]{1,0:T(8,128)S(1)} %get-tuple-element.39), channel_id=1, source_target_pairs={{0,8},{8,0},{16,24},{24,16},{1,9},{9,1},{17,25},{25,17},{2,10},{10... | collective-permute-start | bytes 393224 | tf_op jit(solution)/shard_map/ppermute | solution.py:31
  12.3 0.5 collective-permute-start.4
  12.8 1.5 %collective-permute-start.5 = (f32[16,2048]{1,0:T(8,128)S(1)}, f32[16,2048]{1,0:T(8,128)S(1)}, u32[]{:S(2)}, u32[]{:S(2)}) collective-permute-start(f32[16,2048]{1,0:T(8,128)S(1)} %get-tuple-element.41), channel_id=1, source_target_pairs={{0,24},{8,16},{16,8},{24,0},{1,25},{9,17},{17,9},{25,1},{2,26},{10... | collective-permute-start | bytes 393224 | tf_op jit(solution)/shard_map/ppermute | solution.py:31
  14.3 2.7 %collective-permute-done.3 = f32[16,2048]{1,0:T(8,128)S(1)} collective-permute-done((f32[16,2048]{1,0:T(8,128)S(1)}, f32[16,2048]{1,0:T(8,128)S(1)}, u32[]{:S(2)}, u32[]{:S(2)}) %collective-permute-start.3) | collective-permute-done | bytes 131104 | tf_op jit(solution)/shard_map/ppermute | solution.py:31
  17.0 2.4 %collective-permute-done.4 = f32[16,2048]{1,0:T(8,128)S(1)} collective-permute-done((f32[16,2048]{1,0:T(8,128)S(1)}, f32[16,2048]{1,0:T(8,128)S(1)}, u32[]{:S(2)}, u32[]{:S(2)}) %collective-permute-start.4) | collective-permute-done | bytes 131104 | tf_op jit(solution)/shard_map/ppermute | solution.py:31
  19.5 3.7 %collective-permute-start.8 = (bf16[16,2048]{1,0:T(8,128)(2,1)S(1)}, bf16[16,2048]{1,0:T(8,128)(2,1)S(1)}, u32[]{:S(2)}, u32[]{:S(2)}) collective-permute-start(bf16[16,2048]{1,0:T(8,128)(2,1)S(1)} %add_convert_fusion), channel_id=1, source_target_pairs={{0,6},{1,7},{2,4},{3,5},{4,2},{5,3},{6,0},{7,1},{8,14},{9,15},{10,... | collective-permute-start | bytes 196616 | tf_op jit(solution)/shard_map/ppermute | solution.py:31
  23.2 0.8 collective-permute-start.6
  24.0 2.1 %collective-permute-done.8 = bf16[16,2048]{1,0:T(8,128)(2,1)S(1)} collective-permute-done((bf16[16,2048]{1,0:T(8,128)(2,1)S(1)}, bf16[16,2048]{1,0:T(8,128)(2,1)S(1)}, u32[]{:S(2)}, u32[]{:S(2)}) %collective-permute-start.8) | collective-permute-done | bytes 65568 | tf_op jit(solution)/shard_map/ppermute | solution.py:31
  26.1 2.2 %collective-permute-done.7 = bf16[16,2048]{1,0:T(8,128)(2,1)S(1)} collective-permute-done((bf16[16,2048]{1,0:T(8,128)(2,1)S(1)}, bf16[16,2048]{1,0:T(8,128)(2,1)S(1)}, u32[]{:S(2)}, u32[]{:S(2)}) %collective-permute-start.7) | collective-permute-done | bytes 65568 | tf_op jit(solution)/shard_map/ppermute | solution.py:31
  28.5 0.1 pad_add_fusion.ids_ref
  28.5 1.4 %collective-permute-done.9.other_ref = bf16[4,16,2048]{2,1,0:T(8,128)(2,1)S(1)} collective-permute-done((bf16[4,16,2048]{2,1,0:T(8,128)(2,1)S(1)}, bf16[4,16,2048]{2,1,0:T(8,128)(2,1)S(1)}, u32[]{:S(2)}, u32[]{:S(2)}) %collective-permute-start.9) | collective-permute-done | bytes 262176 | tf_op jit(solution)/shard_map/ppermute | solution.py:31
  30.0 0.8 select.1
  30.8 0.3 collective-permute-start.13
  31.1 2.2 %copy-done = bf16[2048,1024]{1,0:T(8,128)(2,1)S(1)} copy-done((bf16[2048,1024]{1,0:T(8,128)(2,1)S(1)}, bf16[2048,1024]{1,0:T(8,128)(2,1)}, u32[]{:S(2)}) %copy-start) | copy-done | bytes 4194328
  33.3 4.5 %query_product.3.refs_1_ = bf16[512,1024]{1,0:T(8,128)(2,1)} custom-call(bf16[1024,2048]{1,0:T(8,128)(2,1)} %bitcast.42, bf16[2048,1024]{1,0:T(8,128)(2,1)S(1)} %copy-done), custom_call_target="tpu_custom_call" | custom-call | flops 2147483648 | bytes 6291456 | tf_op jit(solution)/shard_map/query_product/pallas_call | solution.py:122
  37.8 1.9 %collective-permute-start.10 = (bf16[2,16,2048]{2,1,0:T(8,128)(2,1)S(1)}, bf16[2,16,2048]{2,1,0:T(8,128)(2,1)S(1)}, u32[]{:S(2)}, u32[]{:S(2)}) collective-permute-start(bf16[2,16,2048]{2,1,0:T(8,128)(2,1)S(1)} %get-tuple-element.43), channel_id=1, source_target_pairs={{0,8},{8,0},{16,24},{24,16},{1,9},{9,1},{17,25},{25,17},{2,10},{10... | collective-permute-start | bytes 393224 | tf_op jit(solution)/shard_map/ppermute | solution.py:31
  39.7 0.8 collective-permute-start.11
  40.5 0.9 collective-permute-start.12
  41.4 1.1 %collective-permute-start.14 = (bf16[2,16,2048]{2,1,0:T(8,128)(2,1)S(1)}, bf16[2,16,2048]{2,1,0:T(8,128)(2,1)S(1)}, u32[]{:S(2)}, u32[]{:S(2)}) collective-permute-start(bf16[2,16,2048]{2,1,0:T(8,128)(2,1)S(1)} %get-tuple-element.49), channel_id=1, source_target_pairs={{0,16},{8,24},{16,0},{24,8},{1,17},{9,25},{17,1},{25,9},{2,18},{10... | collective-permute-start | bytes 393224 | tf_op jit(solution)/shard_map/ppermute | solution.py:31
  42.5 2.2 %collective-permute-start.15 = (bf16[2,16,2048]{2,1,0:T(8,128)(2,1)S(1)}, bf16[2,16,2048]{2,1,0:T(8,128)(2,1)S(1)}, u32[]{:S(2)}, u32[]{:S(2)}) collective-permute-start(bf16[2,16,2048]{2,1,0:T(8,128)(2,1)S(1)} %get-tuple-element.50), channel_id=1, source_target_pairs={{0,24},{8,16},{16,8},{24,0},{1,25},{9,17},{17,9},{25,1},{2,26},{10... | collective-permute-start | bytes 393224 | tf_op jit(solution)/shard_map/ppermute | solution.py:31
  44.7 4.5 %query_product.2.refs_0_ = bf16[512,1024]{1,0:T(8,128)(2,1)} custom-call(bf16[1024,2048]{1,0:T(8,128)(2,1)} %bitcast.43, bf16[2048,1024]{1,0:T(8,128)(2,1)S(1)} %copy-done), custom_call_target="tpu_custom_call" | custom-call | flops 2147483648 | bytes 6291456 | tf_op jit(solution)/shard_map/query_product/pallas_call | solution.py:122
  49.3 2.3 %fetch.2 = (bf16[512,1024]{1,0:T(8,128)(2,1)S(1)}, bf16[512,1024]{1,0:T(8,128)(2,1)S(1)}, bf16[1024,1024]{1,0:T(8,128)(2,1)S(1)}) custom-call(bf16[512,1024]{1,0:T(8,128)(2,1)} %query_product.2.refs_0_, bf16[512,1024]{1,0:T(8,128)(2,1)} %query_product.3.refs_1_, bf16[1024,1024]{1,0:T(8,128)(2,1)} %bitcast.46), custom_call_target="tpu_custom_call" | custom-call | bytes 8388608 | tf_op jit(solution)/shard_map/fetch/pallas_call | solution.py:87
  51.5 1.6 %collective-permute-done.14.refs_2_ = bf16[2,16,2048]{2,1,0:T(8,128)(2,1)S(1)} collective-permute-done((bf16[2,16,2048]{2,1,0:T(8,128)(2,1)S(1)}, bf16[2,16,2048]{2,1,0:T(8,128)(2,1)S(1)}, u32[]{:S(2)}, u32[]{:S(2)}) %collective-permute-start.14) | collective-permute-done | bytes 131104 | tf_op jit(solution)/shard_map/ppermute | solution.py:31
  53.1 4.3 %attend.2 = (bf16[512,1024]{1,0:T(8,128)(2,1)S(1)}, bf16[1024,1024]{1,0:T(8,128)(2,1)}, bf16[2,16,2048]{2,1,0:T(8,128)(2,1)S(1)}, bf16[2,16,2048]{2,1,0:T(8,128)...) custom-call(s32[2]{0:T(128)S(1)} %pad_add_fusion.ids_ref, s32[128]{0:T(128)S(1)} %copy-done.3, ...), custom_call_target="tpu_custom_call" | custom-call | flops 671088640 | bytes 4194304 | tf_op jit(solution)/shard_map/attend/pallas_call | solution.py:274
  57.5 4.3 %attend.3 = (bf16[512,1024]{1,0:T(8,128)(2,1)S(1)}, bf16[1024,1024]{1,0:T(8,128)(2,1)}, bf16[2,16,2048]{2,1,0:T(8,128)(2,1)S(1)}, bf16[2,16,2048]{2,1,0:T(8,128)...) custom-call(s32[2]{0:T(128)S(1)} %pad_add_fusion.ids_ref, ...), custom_call_target="tpu_custom_call", output_to_operand_aliasing={{1}: (9, {})} | custom-call | flops 671088640 | bytes 4194304 | tf_op jit(solution)/shard_map/attend/pallas_call | solution.py:274
  61.9 0.4 collective-permute-start.17
  62.3 0.9 collective-permute-start.19
  63.2 2.2 %collective-permute-start.21 = (bf16[2,16,2048]{2,1,0:T(8,128)(2,1)S(1)}, bf16[2,16,2048]{2,1,0:T(8,128)(2,1)S(1)}, u32[]{:S(2)}, u32[]{:S(2)}) collective-permute-start(bf16[2,16,2048]{2,1,0:T(8,128)(2,1)S(1)} %get-tuple-element.62), channel_id=1, source_target_pairs={{0,24},{8,16},{16,8},{24,0},{1,25},{9,17},{17,9},{25,1},{2,26},{10... | collective-permute-start | bytes 393224 | tf_op jit(solution)/shard_map/ppermute | solution.py:31
  65.4 0.4 collective-permute-start.16
  65.8 0.9 collective-permute-start.18
  66.7 1.6 %collective-permute-done.17.refs_3_ = bf16[2,16,2048]{2,1,0:T(8,128)(2,1)S(1)} collective-permute-done((bf16[2,16,2048]{2,1,0:T(8,128)(2,1)S(1)}, bf16[2,16,2048]{2,1,0:T(8,128)(2,1)S(1)}, u32[]{:S(2)}, u32[]{:S(2)}) %collective-permute-start.17) | collective-permute-done | bytes 131104 | tf_op jit(solution)/shard_map/ppermute | solution.py:31
  68.3 0.6 collective-permute-start.20
  68.9 1.8 %collective-permute-done.19.refs_5_ = bf16[2,16,2048]{2,1,0:T(8,128)(2,1)S(1)} collective-permute-done((bf16[2,16,2048]{2,1,0:T(8,128)(2,1)S(1)}, bf16[2,16,2048]{2,1,0:T(8,128)(2,1)S(1)}, u32[]{:S(2)}, u32[]{:S(2)}) %collective-permute-start.19) | collective-permute-done | bytes 131104 | tf_op jit(solution)/shard_map/ppermute | solution.py:31
  70.7 0.6 collective-permute-done.21.refs_7_
  71.3 2.5 %collective-permute-done.16.refs_2_ = bf16[2,16,2048]{2,1,0:T(8,128)(2,1)S(1)} collective-permute-done((bf16[2,16,2048]{2,1,0:T(8,128)(2,1)S(1)}, bf16[2,16,2048]{2,1,0:T(8,128)(2,1)S(1)}, u32[]{:S(2)}, u32[]{:S(2)}) %collective-permute-start.16) | collective-permute-done | bytes 131104 | tf_op jit(solution)/shard_map/ppermute | solution.py:31
  73.7 1.9 %collective-permute-done.18.refs_4_ = bf16[2,16,2048]{2,1,0:T(8,128)(2,1)S(1)} collective-permute-done((bf16[2,16,2048]{2,1,0:T(8,128)(2,1)S(1)}, bf16[2,16,2048]{2,1,0:T(8,128)(2,1)S(1)}, u32[]{:S(2)}, u32[]{:S(2)}) %collective-permute-start.18) | collective-permute-done | bytes 131104 | tf_op jit(solution)/shard_map/ppermute | solution.py:31
  75.6 0.9 combine.1
  76.6 1.5 %collective-permute-done.22 = bf16[4,16,2048]{2,1,0:T(8,128)(2,1)S(1)} collective-permute-done((bf16[4,16,2048]{2,1,0:T(8,128)(2,1)S(1)}, bf16[4,16,2048]{2,1,0:T(8,128)(2,1)S(1)}, u32[]{:S(2)}, u32[]{:S(2)}) %collective-permute-start.22) | collective-permute-done | bytes 262176 | tf_op jit(solution)/shard_map/ppermute | solution.py:31
  78.2 0.6 collective-permute-start.23
  78.8 3.0 %collective-permute-start.25 = (bf16[16,2048]{1,0:T(8,128)(2,1)S(1)}, bf16[16,2048]{1,0:T(8,128)(2,1)S(1)}, u32[]{:S(2)}, u32[]{:S(2)}) collective-permute-start(bf16[16,2048]{1,0:T(8,128)(2,1)S(1)} %get-tuple-element.72), channel_id=1, source_target_pairs={{0,6},{1,7},{2,4},{3,5},{4,2},{5,3},{6,0},{7,1},{8,14},{9,15},{10,... | collective-permute-start | bytes 196616 | tf_op jit(solution)/shard_map/ppermute | solution.py:31
  81.8 3.4 %image_product.2.refs_0_ = bf16[1024,2048]{1,0:T(8,128)(2,1)} custom-call(bf16[512,1024]{1,0:T(8,128)(2,1)S(1)} %get-tuple-element.54.x_ref, bf16[2048,1024]{1,0:T(8,128)(2,1)S(1)} %copy-done.1), custom_call_target="tpu_custom_call" | custom-call | flops 2147483648 | bytes 5242880 | tf_op jit(solution)/shard_map/image_product/pallas_call | solution.py:160
  85.2 0.9 collective-permute-done.25
  86.1 2.0 %collective-permute-done.24 = bf16[16,2048]{1,0:T(8,128)(2,1)S(1)} collective-permute-done((bf16[16,2048]{1,0:T(8,128)(2,1)S(1)}, bf16[16,2048]{1,0:T(8,128)(2,1)S(1)}, u32[]{:S(2)}, u32[]{:S(2)}) %collective-permute-start.24) | collective-permute-done | bytes 65568 | tf_op jit(solution)/shard_map/ppermute | solution.py:31
  88.1 0.2 fusion.3.refs_0_
  88.3 1.7 %collective-permute-start.28 = (bf16[16,2048]{1,0:T(8,128)(2,1)S(1)}, bf16[16,2048]{1,0:T(8,128)(2,1)S(1)}, u32[]{:S(2)}, u32[]{:S(2)}) collective-permute-start(bf16[16,2048]{1,0:T(8,128)(2,1)S(1)} %fusion.3.refs_0_), channel_id=1, source_target_pairs={{0,24},{8,16},{16,8},{24,0},{1,25},{9,17},{17,9},{25,1},{2,26},{10... | collective-permute-start | bytes 196616 | tf_op jit(solution)/shard_map/ppermute | solution.py:31
  90.0 1.0 collective-permute-start.27
  91.0 0.9 collective-permute-start.26
  91.9 3.4 %image_product.3 = bf16[1024,2048]{1,0:T(8,128)(2,1)} custom-call(bf16[512,1024]{1,0:T(8,128)(2,1)S(1)} %get-tuple-element.53.x_ref, bf16[2048,1024]{1,0:T(8,128)(2,1)S(1)} %copy-done.1, bf16[1024,2048]{1,0:T(8,128)(2,1)} %image_product.2.refs_0_), custom_call_target="tpu_custom_call", output_to_operand_aliasing={{}: (2, {})} | custom-call | flops 2147483648 | bytes 5242880 | tf_op jit(solution)/shard_map/image_product/pallas_call | solution.py:160
  95.3 1.4 %project.3 = (f32[16,1024]{1,0:T(8,128)S(1)}, f32[16,1024]{1,0:T(8,128)S(1)}, f32[16,1024]{1,0:T(8,128)S(1)}, f32[16,1024]{1,0:T(8,128)S(1)}) custom-call(bf16[16,2048]{1,0:T(8,128)(2,1)S(1)} %fusion.3.refs_0_, bf16[16,2048]{1,0:T(8,128)(2,1)S(1)} %collective-permute-done.26.refs_1_, bf16[16,2048]{1,0:T(8,128)(2,1)S(1)} %collective-permute-done.27.refs_2_, ...), custom_call_target="tpu_custom_call" | custom-call | flops 268435456 | bytes 4194304 | tf_op jit(solution)/shard_map/project/pallas_call | solution.py:61
  96.7 1.2 %collective-permute-start.29 = (f32[16,1024]{1,0:T(8,128)S(1)}, f32[16,1024]{1,0:T(8,128)S(1)}, u32[]{:S(2)}, u32[]{:S(2)}) collective-permute-start(f32[16,1024]{1,0:T(8,128)S(1)} %get-tuple-element.66), channel_id=1, source_target_pairs={{0,8},{8,0},{16,24},{24,16},{1,9},{9,1},{17,25},{25,17},{2,10},{10... | collective-permute-start | bytes 196616 | tf_op jit(solution)/shard_map/ppermute | solution.py:31
  97.9 1.0 collective-permute-start.30
  98.9 1.3 %collective-permute-start.31 = (f32[16,1024]{1,0:T(8,128)S(1)}, f32[16,1024]{1,0:T(8,128)S(1)}, u32[]{:S(2)}, u32[]{:S(2)}) collective-permute-start(f32[16,1024]{1,0:T(8,128)S(1)} %get-tuple-element.68), channel_id=1, source_target_pairs={{0,24},{8,16},{16,8},{24,0},{1,25},{9,17},{17,9},{25,1},{2,26},{10... | collective-permute-start | bytes 196616 | tf_op jit(solution)/shard_map/ppermute | solution.py:31
  100.3 1.1 %collective-permute-done.29 = f32[16,1024]{1,0:T(8,128)S(1)} collective-permute-done((f32[16,1024]{1,0:T(8,128)S(1)}, f32[16,1024]{1,0:T(8,128)S(1)}, u32[]{:S(2)}, u32[]{:S(2)}) %collective-permute-start.29) | collective-permute-done | bytes 65568 | tf_op jit(solution)/shard_map/ppermute | solution.py:31
  101.3 1.3 %collective-permute-done.30 = f32[16,1024]{1,0:T(8,128)S(1)} collective-permute-done((f32[16,1024]{1,0:T(8,128)S(1)}, f32[16,1024]{1,0:T(8,128)S(1)}, u32[]{:S(2)}, u32[]{:S(2)}) %collective-permute-start.30) | collective-permute-done | bytes 65568 | tf_op jit(solution)/shard_map/ppermute | solution.py:31
  102.7 1.4 %collective-permute-done.31 = f32[16,1024]{1,0:T(8,128)S(1)} collective-permute-done((f32[16,1024]{1,0:T(8,128)S(1)}, f32[16,1024]{1,0:T(8,128)S(1)}, u32[]{:S(2)}, u32[]{:S(2)}) %collective-permute-start.31) | collective-permute-done | bytes 65568 | tf_op jit(solution)/shard_map/ppermute | solution.py:31
  104.1 0.7 copy-done.5
  (36 shorter events, 0.4 us)
Async XLA Ops:
  1.5 6.8 %collective-permute-start.2 = (bf16[16,1024]{1,0:T(8,128)(2,1)S(1)}, bf16[16,1024]{1,0:T(8,128)(2,1)S(1)}, u32[]{:S(2)}, u32[]{:S(2)}) collective-permute-start(bf16[16,1024]{1,0:T(8,128)(2,1)S(1)} %get-tuple-element.74), channel_id=1, source_target_pairs={{0,24},{8,16},{16,8},{24,0},{1,25},{9,17},{17,9},{25,1},{2,26},{10... | collective-permute-start | bytes 98312 | tf_op jit(solution)/shard_map/ppermute | solution.py:31
  5.5 3.9 %collective-permute-start = (bf16[16,1024]{1,0:T(8,128)(2,1)S(1)}, bf16[16,1024]{1,0:T(8,128)(2,1)S(1)}, u32[]{:S(2)}, u32[]{:S(2)}) collective-permute-start(bf16[16,1024]{1,0:T(8,128)(2,1)S(1)} %get-tuple-element.75), channel_id=1, source_target_pairs={{0,8},{8,0},{16,24},{24,16},{1,9},{9,1},{17,25},{25,17},{2,10},{10... | collective-permute-start | bytes 98312 | tf_op jit(solution)/shard_map/ppermute | solution.py:31
  6.0 3.9 %collective-permute-start.1 = (bf16[16,1024]{1,0:T(8,128)(2,1)S(1)}, bf16[16,1024]{1,0:T(8,128)(2,1)S(1)}, u32[]{:S(2)}, u32[]{:S(2)}) collective-permute-start(bf16[16,1024]{1,0:T(8,128)(2,1)S(1)} %get-tuple-element.77), channel_id=1, source_target_pairs={{0,16},{8,24},{16,0},{24,8},{1,17},{9,25},{17,1},{25,9},{2,18},{10... | collective-permute-start | bytes 98312 | tf_op jit(solution)/shard_map/ppermute | solution.py:31
  8.3 21.7 %copy-start.3 = (s32[128]{0:T(128)S(1)}, s32[128]{0:T(128)}, u32[]{:S(2)}) copy-start(s32[128]{0:T(128)} %prompt_ref.7) | copy-start | bytes 1540
  10.8 6.3 %collective-permute-start.3 = (f32[16,2048]{1,0:T(8,128)S(1)}, f32[16,2048]{1,0:T(8,128)S(1)}, u32[]{:S(2)}, u32[]{:S(2)}) collective-permute-start(f32[16,2048]{1,0:T(8,128)S(1)} %get-tuple-element.39), channel_id=1, source_target_pairs={{0,8},{8,0},{16,24},{24,16},{1,9},{9,1},{17,25},{25,17},{2,10},{10... | collective-permute-start | bytes 393224 | tf_op jit(solution)/shard_map/ppermute | solution.py:31
  12.3 7.1 %collective-permute-start.4 = (f32[16,2048]{1,0:T(8,128)S(1)}, f32[16,2048]{1,0:T(8,128)S(1)}, u32[]{:S(2)}, u32[]{:S(2)}) collective-permute-start(f32[16,2048]{1,0:T(8,128)S(1)} %get-tuple-element.40), channel_id=1, source_target_pairs={{0,16},{8,24},{16,0},{24,8},{1,17},{9,25},{17,1},{25,9},{2,18},{10... | collective-permute-start | bytes 393224 | tf_op jit(solution)/shard_map/ppermute | solution.py:31
  12.8 6.6 %collective-permute-start.5 = (f32[16,2048]{1,0:T(8,128)S(1)}, f32[16,2048]{1,0:T(8,128)S(1)}, u32[]{:S(2)}, u32[]{:S(2)}) collective-permute-start(f32[16,2048]{1,0:T(8,128)S(1)} %get-tuple-element.41), channel_id=1, source_target_pairs={{0,24},{8,16},{16,8},{24,0},{1,25},{9,17},{17,9},{25,1},{2,26},{10... | collective-permute-start | bytes 393224 | tf_op jit(solution)/shard_map/ppermute | solution.py:31
  19.5 6.6 %collective-permute-start.8 = (bf16[16,2048]{1,0:T(8,128)(2,1)S(1)}, bf16[16,2048]{1,0:T(8,128)(2,1)S(1)}, u32[]{:S(2)}, u32[]{:S(2)}) collective-permute-start(bf16[16,2048]{1,0:T(8,128)(2,1)S(1)} %add_convert_fusion), channel_id=1, source_target_pairs={{0,6},{1,7},{2,4},{3,5},{4,2},{5,3},{6,0},{7,1},{8,14},{9,15},{10,... | collective-permute-start | bytes 196616 | tf_op jit(solution)/shard_map/ppermute | solution.py:31
  23.2 5.2 %collective-permute-start.7 = (bf16[16,2048]{1,0:T(8,128)(2,1)S(1)}, bf16[16,2048]{1,0:T(8,128)(2,1)S(1)}, u32[]{:S(2)}, u32[]{:S(2)}) collective-permute-start(bf16[16,2048]{1,0:T(8,128)(2,1)S(1)} %add_convert_fusion), channel_id=1, source_target_pairs={{0,4},{1,5},{2,6},{3,7},{4,0},{5,1},{6,2},{7,3},{8,12},{9,13},{10,... | collective-permute-start | bytes 196616 | tf_op jit(solution)/shard_map/ppermute | solution.py:31
  23.2 5.2 %collective-permute-start.6 = (bf16[16,2048]{1,0:T(8,128)(2,1)S(1)}, bf16[16,2048]{1,0:T(8,128)(2,1)S(1)}, u32[]{:S(2)}, u32[]{:S(2)}) collective-permute-start(bf16[16,2048]{1,0:T(8,128)(2,1)S(1)} %add_convert_fusion), channel_id=1, source_target_pairs={{0,2},{1,3},{2,0},{3,1},{4,6},{5,7},{6,4},{7,5},{8,10},{9,11},{10,... | collective-permute-start | bytes 196616 | tf_op jit(solution)/shard_map/ppermute | solution.py:31
  28.4 1.6 %collective-permute-start.9 = (bf16[4,16,2048]{2,1,0:T(8,128)(2,1)S(1)}, bf16[4,16,2048]{2,1,0:T(8,128)(2,1)S(1)}, u32[]{:S(2)}, u32[]{:S(2)}) collective-permute-start(bf16[4,16,2048]{2,1,0:T(8,128)(2,1)S(1)} %pad_maximum_fusion.same_ref), channel_id=1, source_target_pairs={{0,1},{1,0},{2,3},{3,2},{4,5},{5,4},{6,7},{7,6},{8,9},{9,8},{10,11... | collective-permute-start | bytes 786440 | tf_op jit(solution)/shard_map/ppermute | solution.py:31
  30.8 11.7 %collective-permute-start.13 = (bf16[2,16,2048]{2,1,0:T(8,128)(2,1)S(1)}, bf16[2,16,2048]{2,1,0:T(8,128)(2,1)S(1)}, u32[]{:S(2)}, u32[]{:S(2)}) collective-permute-start(bf16[2,16,2048]{2,1,0:T(8,128)(2,1)S(1)} %get-tuple-element.48), channel_id=1, source_target_pairs={{0,8},{8,0},{16,24},{24,16},{1,9},{9,1},{17,25},{25,17},{2,10},{10... | collective-permute-start | bytes 393224 | tf_op jit(solution)/shard_map/ppermute | solution.py:31
  31.1 2.2 %copy-start = (bf16[2048,1024]{1,0:T(8,128)(2,1)S(1)}, bf16[2048,1024]{1,0:T(8,128)(2,1)}, u32[]{:S(2)}) copy-start(bf16[2048,1024]{1,0:T(8,128)(2,1)} %w_ref.7) | copy-start | bytes 12582916
  37.8 19.7 %collective-permute-start.10 = (bf16[2,16,2048]{2,1,0:T(8,128)(2,1)S(1)}, bf16[2,16,2048]{2,1,0:T(8,128)(2,1)S(1)}, u32[]{:S(2)}, u32[]{:S(2)}) collective-permute-start(bf16[2,16,2048]{2,1,0:T(8,128)(2,1)S(1)} %get-tuple-element.43), channel_id=1, source_target_pairs={{0,8},{8,0},{16,24},{24,16},{1,9},{9,1},{17,25},{25,17},{2,10},{10... | collective-permute-start | bytes 393224 | tf_op jit(solution)/shard_map/ppermute | solution.py:31
  39.7 17.8 %collective-permute-start.11 = (bf16[2,16,2048]{2,1,0:T(8,128)(2,1)S(1)}, bf16[2,16,2048]{2,1,0:T(8,128)(2,1)S(1)}, u32[]{:S(2)}, u32[]{:S(2)}) collective-permute-start(bf16[2,16,2048]{2,1,0:T(8,128)(2,1)S(1)} %get-tuple-element.44), channel_id=1, source_target_pairs={{0,16},{8,24},{16,0},{24,8},{1,17},{9,25},{17,1},{25,9},{2,18},{10... | collective-permute-start | bytes 393224 | tf_op jit(solution)/shard_map/ppermute | solution.py:31
  40.5 17.0 %collective-permute-start.12 = (bf16[2,16,2048]{2,1,0:T(8,128)(2,1)S(1)}, bf16[2,16,2048]{2,1,0:T(8,128)(2,1)S(1)}, u32[]{:S(2)}, u32[]{:S(2)}) collective-permute-start(bf16[2,16,2048]{2,1,0:T(8,128)(2,1)S(1)} %get-tuple-element.45), channel_id=1, source_target_pairs={{0,24},{8,16},{16,8},{24,0},{1,25},{9,17},{17,9},{25,1},{2,26},{10... | collective-permute-start | bytes 393224 | tf_op jit(solution)/shard_map/ppermute | solution.py:31
  41.4 11.7 %collective-permute-start.14 = (bf16[2,16,2048]{2,1,0:T(8,128)(2,1)S(1)}, bf16[2,16,2048]{2,1,0:T(8,128)(2,1)S(1)}, u32[]{:S(2)}, u32[]{:S(2)}) collective-permute-start(bf16[2,16,2048]{2,1,0:T(8,128)(2,1)S(1)} %get-tuple-element.49), channel_id=1, source_target_pairs={{0,16},{8,24},{16,0},{24,8},{1,17},{9,25},{17,1},{25,9},{2,18},{10... | collective-permute-start | bytes 393224 | tf_op jit(solution)/shard_map/ppermute | solution.py:31
  42.5 10.7 %collective-permute-start.15 = (bf16[2,16,2048]{2,1,0:T(8,128)(2,1)S(1)}, bf16[2,16,2048]{2,1,0:T(8,128)(2,1)S(1)}, u32[]{:S(2)}, u32[]{:S(2)}) collective-permute-start(bf16[2,16,2048]{2,1,0:T(8,128)(2,1)S(1)} %get-tuple-element.50), channel_id=1, source_target_pairs={{0,24},{8,16},{16,8},{24,0},{1,25},{9,17},{17,9},{25,1},{2,26},{10... | collective-permute-start | bytes 393224 | tf_op jit(solution)/shard_map/ppermute | solution.py:31
  49.2 3.9 %copy-start.4 = (s32[8]{0:T(128)S(1)}, s32[8]{0:T(128)}, u32[]{:S(2)}) copy-start(s32[8]{0:T(128)} %len_ref.3) | copy-start | bytes 100
  57.5 24.3 %copy-start.1 = (bf16[2048,1024]{1,0:T(8,128)(2,1)S(1)}, bf16[2048,1024]{1,0:T(8,128)(2,1)}, u32[]{:S(2)}) copy-start(bf16[2048,1024]{1,0:T(8,128)(2,1)} %w_ref.7) | copy-start | bytes 12582916
  61.9 6.4 %collective-permute-start.17 = (bf16[2,16,2048]{2,1,0:T(8,128)(2,1)S(1)}, bf16[2,16,2048]{2,1,0:T(8,128)(2,1)S(1)}, u32[]{:S(2)}, u32[]{:S(2)}) collective-permute-start(bf16[2,16,2048]{2,1,0:T(8,128)(2,1)S(1)} %get-tuple-element.58), channel_id=1, source_target_pairs={{0,8},{8,0},{16,24},{24,16},{1,9},{9,1},{17,25},{25,17},{2,10},{10... | collective-permute-start | bytes 393224 | tf_op jit(solution)/shard_map/ppermute | solution.py:31
  62.3 8.4 %collective-permute-start.19 = (bf16[2,16,2048]{2,1,0:T(8,128)(2,1)S(1)}, bf16[2,16,2048]{2,1,0:T(8,128)(2,1)S(1)}, u32[]{:S(2)}, u32[]{:S(2)}) collective-permute-start(bf16[2,16,2048]{2,1,0:T(8,128)(2,1)S(1)} %get-tuple-element.60), channel_id=1, source_target_pairs={{0,16},{8,24},{16,0},{24,8},{1,17},{9,25},{17,1},{25,9},{2,18},{10... | collective-permute-start | bytes 393224 | tf_op jit(solution)/shard_map/ppermute | solution.py:31
  63.2 8.0 %collective-permute-start.21 = (bf16[2,16,2048]{2,1,0:T(8,128)(2,1)S(1)}, bf16[2,16,2048]{2,1,0:T(8,128)(2,1)S(1)}, u32[]{:S(2)}, u32[]{:S(2)}) collective-permute-start(bf16[2,16,2048]{2,1,0:T(8,128)(2,1)S(1)} %get-tuple-element.62), channel_id=1, source_target_pairs={{0,24},{8,16},{16,8},{24,0},{1,25},{9,17},{17,9},{25,1},{2,26},{10... | collective-permute-start | bytes 393224 | tf_op jit(solution)/shard_map/ppermute | solution.py:31
  65.4 8.3 %collective-permute-start.16 = (bf16[2,16,2048]{2,1,0:T(8,128)(2,1)S(1)}, bf16[2,16,2048]{2,1,0:T(8,128)(2,1)S(1)}, u32[]{:S(2)}, u32[]{:S(2)}) collective-permute-start(bf16[2,16,2048]{2,1,0:T(8,128)(2,1)S(1)} %get-tuple-element.57), channel_id=1, source_target_pairs={{0,8},{8,0},{16,24},{24,16},{1,9},{9,1},{17,25},{25,17},{2,10},{10... | collective-permute-start | bytes 393224 | tf_op jit(solution)/shard_map/ppermute | solution.py:31
  65.8 9.8 %collective-permute-start.18 = (bf16[2,16,2048]{2,1,0:T(8,128)(2,1)S(1)}, bf16[2,16,2048]{2,1,0:T(8,128)(2,1)S(1)}, u32[]{:S(2)}, u32[]{:S(2)}) collective-permute-start(bf16[2,16,2048]{2,1,0:T(8,128)(2,1)S(1)} %get-tuple-element.59), channel_id=1, source_target_pairs={{0,16},{8,24},{16,0},{24,8},{1,17},{9,25},{17,1},{25,9},{2,18},{10... | collective-permute-start | bytes 393224 | tf_op jit(solution)/shard_map/ppermute | solution.py:31
  68.3 7.3 %collective-permute-start.20 = (bf16[2,16,2048]{2,1,0:T(8,128)(2,1)S(1)}, bf16[2,16,2048]{2,1,0:T(8,128)(2,1)S(1)}, u32[]{:S(2)}, u32[]{:S(2)}) collective-permute-start(bf16[2,16,2048]{2,1,0:T(8,128)(2,1)S(1)} %get-tuple-element.61), channel_id=1, source_target_pairs={{0,24},{8,16},{16,8},{24,0},{1,25},{9,17},{17,9},{25,1},{2,26},{10... | collective-permute-start | bytes 393224 | tf_op jit(solution)/shard_map/ppermute | solution.py:31
  76.5 1.6 %collective-permute-start.22 = (bf16[4,16,2048]{2,1,0:T(8,128)(2,1)S(1)}, bf16[4,16,2048]{2,1,0:T(8,128)(2,1)S(1)}, u32[]{:S(2)}, u32[]{:S(2)}) collective-permute-start(bf16[4,16,2048]{2,1,0:T(8,128)(2,1)S(1)} %get-tuple-element.64), channel_id=1, source_target_pairs={{0,1},{1,0},{2,3},{3,2},{4,5},{5,4},{6,7},{7,6},{8,9},{9,8},{10,11... | collective-permute-start | bytes 786440 | tf_op jit(solution)/shard_map/ppermute | solution.py:31
  78.2 7.0 %collective-permute-start.23 = (bf16[16,2048]{1,0:T(8,128)(2,1)S(1)}, bf16[16,2048]{1,0:T(8,128)(2,1)S(1)}, u32[]{:S(2)}, u32[]{:S(2)}) collective-permute-start(bf16[16,2048]{1,0:T(8,128)(2,1)S(1)} %get-tuple-element.71), channel_id=1, source_target_pairs={{0,2},{1,3},{2,0},{3,1},{4,6},{5,7},{6,4},{7,5},{8,10},{9,11},{10,... | collective-permute-start | bytes 196616 | tf_op jit(solution)/shard_map/ppermute | solution.py:31
  78.8 7.3 %collective-permute-start.25 = (bf16[16,2048]{1,0:T(8,128)(2,1)S(1)}, bf16[16,2048]{1,0:T(8,128)(2,1)S(1)}, u32[]{:S(2)}, u32[]{:S(2)}) collective-permute-start(bf16[16,2048]{1,0:T(8,128)(2,1)S(1)} %get-tuple-element.72), channel_id=1, source_target_pairs={{0,6},{1,7},{2,4},{3,5},{4,2},{5,3},{6,0},{7,1},{8,14},{9,15},{10,... | collective-permute-start | bytes 196616 | tf_op jit(solution)/shard_map/ppermute | solution.py:31
  81.8 6.3 %collective-permute-start.24 = (bf16[16,2048]{1,0:T(8,128)(2,1)S(1)}, bf16[16,2048]{1,0:T(8,128)(2,1)S(1)}, u32[]{:S(2)}, u32[]{:S(2)}) collective-permute-start(bf16[16,2048]{1,0:T(8,128)(2,1)S(1)} %get-tuple-element.73), channel_id=1, source_target_pairs={{0,4},{1,5},{2,6},{3,7},{4,0},{5,1},{6,2},{7,3},{8,12},{9,13},{10,... | collective-permute-start | bytes 196616 | tf_op jit(solution)/shard_map/ppermute | solution.py:31
  88.3 6.9 %collective-permute-start.28 = (bf16[16,2048]{1,0:T(8,128)(2,1)S(1)}, bf16[16,2048]{1,0:T(8,128)(2,1)S(1)}, u32[]{:S(2)}, u32[]{:S(2)}) collective-permute-start(bf16[16,2048]{1,0:T(8,128)(2,1)S(1)} %fusion.3.refs_0_), channel_id=1, source_target_pairs={{0,24},{8,16},{16,8},{24,0},{1,25},{9,17},{17,9},{25,1},{2,26},{10... | collective-permute-start | bytes 196616 | tf_op jit(solution)/shard_map/ppermute | solution.py:31
  90.0 5.3 %collective-permute-start.27 = (bf16[16,2048]{1,0:T(8,128)(2,1)S(1)}, bf16[16,2048]{1,0:T(8,128)(2,1)S(1)}, u32[]{:S(2)}, u32[]{:S(2)}) collective-permute-start(bf16[16,2048]{1,0:T(8,128)(2,1)S(1)} %fusion.3.refs_0_), channel_id=1, source_target_pairs={{0,16},{8,24},{16,0},{24,8},{1,17},{9,25},{17,1},{25,9},{2,18},{10... | collective-permute-start | bytes 196616 | tf_op jit(solution)/shard_map/ppermute | solution.py:31
  91.0 4.3 %collective-permute-start.26 = (bf16[16,2048]{1,0:T(8,128)(2,1)S(1)}, bf16[16,2048]{1,0:T(8,128)(2,1)S(1)}, u32[]{:S(2)}, u32[]{:S(2)}) collective-permute-start(bf16[16,2048]{1,0:T(8,128)(2,1)S(1)} %fusion.3.refs_0_), channel_id=1, source_target_pairs={{0,8},{8,0},{16,24},{24,16},{1,9},{9,1},{17,25},{25,17},{2,10},{10... | collective-permute-start | bytes 196616 | tf_op jit(solution)/shard_map/ppermute | solution.py:31
  91.9 3.4 %copy-start.2 = (bf16[1024,2048]{1,0:T(8,128)(2,1)S(1)}, bf16[1024,2048]{1,0:T(8,128)(2,1)}, u32[]{:S(2)}) copy-start(bf16[1024,2048]{1,0:T(8,128)(2,1)} %refs_4_.1) | copy-start | bytes 12582916
  96.7 4.7 %collective-permute-start.29 = (f32[16,1024]{1,0:T(8,128)S(1)}, f32[16,1024]{1,0:T(8,128)S(1)}, u32[]{:S(2)}, u32[]{:S(2)}) collective-permute-start(f32[16,1024]{1,0:T(8,128)S(1)} %get-tuple-element.66), channel_id=1, source_target_pairs={{0,8},{8,0},{16,24},{24,16},{1,9},{9,1},{17,25},{25,17},{2,10},{10... | collective-permute-start | bytes 196616 | tf_op jit(solution)/shard_map/ppermute | solution.py:31
  97.9 4.8 %collective-permute-start.30 = (f32[16,1024]{1,0:T(8,128)S(1)}, f32[16,1024]{1,0:T(8,128)S(1)}, u32[]{:S(2)}, u32[]{:S(2)}) collective-permute-start(f32[16,1024]{1,0:T(8,128)S(1)} %get-tuple-element.67), channel_id=1, source_target_pairs={{0,16},{8,24},{16,0},{24,8},{1,17},{9,25},{17,1},{25,9},{2,18},{10... | collective-permute-start | bytes 196616 | tf_op jit(solution)/shard_map/ppermute | solution.py:31
  98.9 5.2 %collective-permute-start.31 = (f32[16,1024]{1,0:T(8,128)S(1)}, f32[16,1024]{1,0:T(8,128)S(1)}, u32[]{:S(2)}, u32[]{:S(2)}) collective-permute-start(f32[16,1024]{1,0:T(8,128)S(1)} %get-tuple-element.68), channel_id=1, source_target_pairs={{0,24},{8,16},{16,8},{24,0},{1,25},{9,17},{17,9},{25,1},{2,26},{10... | collective-permute-start | bytes 196616 | tf_op jit(solution)/shard_map/ppermute | solution.py:31
  104.1 0.7 copy-start.5

commit v3 on v2

--- a/solution.py
+++ b/solution.py
@@ -221,51 +221,76 @@
                 buf.at[s], ctx_ref.at[pl.ds((first + s) * img_len, img_len), :], sem.at[s]
             )
 
-        def sample(s):
+        items = [(s, h) for s in range(part) for h in range(0, HEADS, 2)]
+        kept = {}
+
+        def columns(h):
+            one = slice(h * HD, (h + 1) * HD)
+            two = slice((h + 1) * HD, (h + 2) * HD)
+            pair = slice(h * HD, (h + 2) * HD)
+            v_one = slice(inner + h * HD, inner + (h + 1) * HD)
+            v_two = slice(inner + (h + 1) * HD, inner + (h + 2) * HD)
+            return one, two, pair, v_one, v_two
+
+        def rows_of(s):
             at = slice(s * img_len, (s + 1) * img_len)
-            all_at = slice((first + s) * img_len, (first + s + 1) * img_len)
+            return at, slice((first + s) * img_len, (first + s + 1) * img_len)
+
+        def block(s, cols):
+            return jnp.concatenate([r[s, :, cols] for r in ins], axis=0)
+
+        def diagonal(s, one, two):
+            a, b = block(s, one), block(s, two)
+            return jnp.concatenate(
+                [jnp.concatenate([a, zero], 1), jnp.concatenate([zero, b], 1)], 0
+            )
+
+        def enter(n):
+            s, h = items[n]
+            at, all_at = rows_of(s)
+            one, two, pair, v_one, v_two = columns(h)
+            size = (2, full_len, img_len)
+            scores = dot(diagonal(s, one, two), q_ref[at, pair], NT).reshape(size)
+            d_soft = dot(diagonal(s, v_one, v_two), g_ref[all_at, pair], NT).reshape(size)
+            kept[n] = scores, d_soft
+
+        def weigh(n):
+            s, _ = items[n]
+            scores, d_soft = kept[n]
             live = (token < len_ref[prompt_ref[base + s]])[None]
-            kv = jnp.concatenate([r[s] for r in ins], axis=0)
-            for h in range(0, HEADS, 2):
-                one = slice(h * HD, (h + 1) * HD)
-                two = slice((h + 1) * HD, (h + 2) * HD)
-                pair = slice(h * HD, (h + 2) * HD)
-                v_one = slice(inner + h * HD, inner + (h + 1) * HD)
-                v_two = slice(inner + (h + 1) * HD, inner + (h + 2) * HD)
-                k1, k2, v1, v2 = kv[:, one], kv[:, two], kv[:, v_one], kv[:, v_two]
-                keys = jnp.concatenate(
-                    [jnp.concatenate([k1, zero], 1), jnp.concatenate([zero, k2], 1)], 0
-                )
-                values = jnp.concatenate(
-                    [jnp.concatenate([v1, zero], 1), jnp.concatenate([zero, v2], 1)], 0
-                )
-                scores = jnp.stack([dot(k1, q_ref[at, one], NT), dot(k2, q_ref[at, two], NT)])
-                d_soft = jnp.stack(
-                    [dot(v1, g_ref[all_at, one], NT), dot(v2, g_ref[all_at, two], NT)]
-                )
-                scores = jnp.where(live, scores * scale, NEG_FILL)
-                expd = jnp.exp(scores - jnp.max(scores, axis=1, keepdims=True))
-                soft = expd * (1.0 / jnp.sum(expd, axis=1, keepdims=True))
-                soft_b = soft.astype(BF16).reshape(2 * full_len, img_len)
-                mean = jnp.sum(d_soft * soft, axis=1, keepdims=True)
-                d_scores = (
-                    (soft * (d_soft - mean) * scale).astype(BF16).reshape(2 * full_len, img_len)
-                )
-                buf[s, :, pair] = dot(soft_b, values, TN).astype(BF16)
-                dq_ref[at, pair] = dot(d_scores, keys, TN).astype(BF16)
-                d_keys = dot(d_scores, q_ref[at, pair], NN).astype(BF16)
-                d_values = dot(soft_b, g_ref[all_at, pair], NN).astype(BF16)
-                for k in range(n_grp):
-                    a = slice(k * block_len, (k + 1) * block_len)
-                    b = slice(full_len + k * block_len, full_len + (k + 1) * block_len)
-                    outs[k][s, :, one] = d_keys[a, :HD]
-                    outs[k][s, :, two] = d_keys[b, HD:]
-                    outs[k][s, :, v_one] = d_values[a, :HD]
-                    outs[k][s, :, v_two] = d_values[b, HD:]
-            put(s).start()
-
-        for s in range(part):
-            sample(s)
+            scores = jnp.where(live, scores * scale, NEG_FILL)
+            expd = jnp.exp(scores - jnp.max(scores, axis=1, keepdims=True))
+            soft = expd * (1.0 / jnp.sum(expd, axis=1, keepdims=True))
+            mean = jnp.sum(d_soft * soft, axis=1, keepdims=True)
+            d_scores = (soft * (d_soft - mean) * scale).astype(BF16)
+            size = (2 * full_len, img_len)
+            kept[n] = soft.astype(BF16).reshape(size), d_scores.reshape(size)
+
+        def leave(n):
+            s, h = items[n]
+            at, all_at = rows_of(s)
+            one, two, pair, v_one, v_two = columns(h)
+            soft_b, d_scores = kept.pop(n)
+            d_keys = dot(d_scores, q_ref[at, pair], NN).astype(BF16)
+            d_values = dot(soft_b, g_ref[all_at, pair], NN).astype(BF16)
+            buf[s, :, pair] = dot(soft_b, diagonal(s, v_one, v_two), TN).astype(BF16)
+            dq_ref[at, pair] = dot(d_scores, diagonal(s, one, two), TN).astype(BF16)
+            for k in range(n_grp):
+                a = slice(k * block_len, (k + 1) * block_len)
+                b = slice(full_len + k * block_len, full_len + (k + 1) * block_len)
+                outs[k][s, :, one] = d_keys[a, :HD]
+                outs[k][s, :, two] = d_keys[b, HD:]
+                outs[k][s, :, v_one] = d_values[a, :HD]
+                outs[k][s, :, v_two] = d_values[b, HD:]
+            if h == HEADS - 2:
+                put(s).start()
+
+        enter(0)
+        for n in range(len(items)):
+            if n + 1 < len(items):
+                enter(n + 1)
+            weigh(n)
+            leave(n)
         for s in range(part):
             put(s).wait()
 

time: 105 us -> 103 us (0.981)
  Pallas kernels: 32.9 us -> 30.5 us
    pallas_call x2, Pallas kernels: 8.67 us -> 6.25 us  [attend(): pl.pallas_call(body, in_specs=[SMEM, SMEM, SMEM, VMEM, VMEM] + [VMEM] * n...]
  transfers between devices with their start and end apart: 32 -> 32, of which waited for: 19 -> 19; matrix products, arithmetic and copies ran while one was open for 0% -> 0% of each run, Pallas kernels for 24% -> 23%
where the time goes in v3:
time: 103 us; the launch traced here: 102 us
  starting transfers between devices  36 us (35%)
  waiting for transfers between devices  30.7 us (30%)
  Pallas kernels  30.5 us (30%)
  local copies, waits for them, and re-layouts  3.81 us (4%)
    ppermute x32, starting transfers between devices, partner(): return lax.ppermute(x, axis, [(i, i ^ k) for i in range(size)])  36 us
    ppermute x32, waiting for transfers between devices, partner(): return lax.ppermute(x, axis, [(i, i ^ k) for i in range(size)])  30.7 us
    pallas_call x2, Pallas kernels, query_product(): pl.pallas_call(body, in_specs=[HBM, VMEM], out_specs=HBM, out_shape=pltpu...  9.1 us
    pallas_call x2, Pallas kernels, image_product(): pl.pallas_call(body, in_specs=[VMEM, VMEM] + [ANY] * len(more), out_specs...  6.77 us
    pallas_call x2, Pallas kernels, attend(): pl.pallas_call(body, in_specs=[SMEM, SMEM, SMEM, VMEM, VMEM] + [VMEM] * n...  6.25 us
    pallas_call x2, Pallas kernels, fetch(): pl.pallas_call(body, in_specs=[HBM] * n, out_specs=[VMEM] * n, out_shape=...  4.46 us
    unnamed x12, local copies, waits for them, and re-layouts  2.91 us
    pallas_call x2, Pallas kernels, project(): pl.pallas_call(body, in_specs=[VMEM] * (n + 1), out_specs=[VMEM] * n, out...  2.22 us
  transfers between devices with their start and end apart: 32, of which 19 were waited for; matrix products, arithmetic and copies ran while one was open for 0% of the time, Pallas kernels for 23%

profile of v3, /device:TPU:0, one launch (start us, length us, event | category | flops | bytes accessed | tf_op | source)
XLA Modules:
  0.0 102.2 jit_solution(8126782783084224820)
XLA Ops:
  0.7 0.8 dynamic-slice_bitcast_fusion
  1.5 4.0 %collective-permute-start.2 = (bf16[16,1024]{1,0:T(8,128)(2,1)S(1)}, bf16[16,1024]{1,0:T(8,128)(2,1)S(1)}, u32[]{:S(2)}, u32[]{:S(2)}) collective-permute-start(bf16[16,1024]{1,0:T(8,128)(2,1)S(1)} %get-tuple-element.74), channel_id=1, source_target_pairs={{0,24},{8,16},{16,8},{24,0},{1,25},{9,17},{17,9},{25,1},{2,26},{10... | collective-permute-start | bytes 98312 | tf_op jit(solution)/shard_map/ppermute | solution.py:31
  5.5 0.5 collective-permute-start
  6.0 0.1 collective-permute-start.1
  6.1 2.2 %fetch.3.refs_4_ = bf16[1024,2048]{1,0:T(8,128)(2,1)S(1)} custom-call(bf16[1024,2048]{1,0:T(8,128)(2,1)} %refs_4_.1), custom_call_target="tpu_custom_call" | custom-call | bytes 8388608 | tf_op jit(solution)/shard_map/fetch/pallas_call | solution.py:87
  8.3 1.0 %collective-permute-done.refs_1_ = bf16[16,1024]{1,0:T(8,128)(2,1)S(1)} collective-permute-done((bf16[16,1024]{1,0:T(8,128)(2,1)S(1)}, bf16[16,1024]{1,0:T(8,128)(2,1)S(1)}, u32[]{:S(2)}, u32[]{:S(2)}) %collective-permute-start) | collective-permute-done | bytes 32800 | tf_op jit(solution)/shard_map/ppermute | solution.py:31
  9.4 0.5 collective-permute-done.1.refs_2_
  9.9 0.8 project.2
  10.8 1.6 %collective-permute-start.3 = (f32[16,2048]{1,0:T(8,128)S(1)}, f32[16,2048]{1,0:T(8,128)S(1)}, u32[]{:S(2)}, u32[]{:S(2)}) collective-permute-start(f32[16,2048]{1,0:T(8,128)S(1)} %get-tuple-element.39), channel_id=1, source_target_pairs={{0,8},{8,0},{16,24},{24,16},{1,9},{9,1},{17,25},{25,17},{2,10},{10... | collective-permute-start | bytes 393224 | tf_op jit(solution)/shard_map/ppermute | solution.py:31
  12.3 0.5 collective-permute-start.4
  12.8 1.5 %collective-permute-start.5 = (f32[16,2048]{1,0:T(8,128)S(1)}, f32[16,2048]{1,0:T(8,128)S(1)}, u32[]{:S(2)}, u32[]{:S(2)}) collective-permute-start(f32[16,2048]{1,0:T(8,128)S(1)} %get-tuple-element.41), channel_id=1, source_target_pairs={{0,24},{8,16},{16,8},{24,0},{1,25},{9,17},{17,9},{25,1},{2,26},{10... | collective-permute-start | bytes 393224 | tf_op jit(solution)/shard_map/ppermute | solution.py:31
  14.3 2.7 %collective-permute-done.3 = f32[16,2048]{1,0:T(8,128)S(1)} collective-permute-done((f32[16,2048]{1,0:T(8,128)S(1)}, f32[16,2048]{1,0:T(8,128)S(1)}, u32[]{:S(2)}, u32[]{:S(2)}) %collective-permute-start.3) | collective-permute-done | bytes 131104 | tf_op jit(solution)/shard_map/ppermute | solution.py:31
  17.0 2.4 %collective-permute-done.4 = f32[16,2048]{1,0:T(8,128)S(1)} collective-permute-done((f32[16,2048]{1,0:T(8,128)S(1)}, f32[16,2048]{1,0:T(8,128)S(1)}, u32[]{:S(2)}, u32[]{:S(2)}) %collective-permute-start.4) | collective-permute-done | bytes 131104 | tf_op jit(solution)/shard_map/ppermute | solution.py:31
  19.5 3.7 %collective-permute-start.8 = (bf16[16,2048]{1,0:T(8,128)(2,1)S(1)}, bf16[16,2048]{1,0:T(8,128)(2,1)S(1)}, u32[]{:S(2)}, u32[]{:S(2)}) collective-permute-start(bf16[16,2048]{1,0:T(8,128)(2,1)S(1)} %add_convert_fusion), channel_id=1, source_target_pairs={{0,6},{1,7},{2,4},{3,5},{4,2},{5,3},{6,0},{7,1},{8,14},{9,15},{10,... | collective-permute-start | bytes 196616 | tf_op jit(solution)/shard_map/ppermute | solution.py:31
  23.2 0.8 collective-permute-start.6
  24.0 2.1 %collective-permute-done.8 = bf16[16,2048]{1,0:T(8,128)(2,1)S(1)} collective-permute-done((bf16[16,2048]{1,0:T(8,128)(2,1)S(1)}, bf16[16,2048]{1,0:T(8,128)(2,1)S(1)}, u32[]{:S(2)}, u32[]{:S(2)}) %collective-permute-start.8) | collective-permute-done | bytes 65568 | tf_op jit(solution)/shard_map/ppermute | solution.py:31
  26.1 2.2 %collective-permute-done.7 = bf16[16,2048]{1,0:T(8,128)(2,1)S(1)} collective-permute-done((bf16[16,2048]{1,0:T(8,128)(2,1)S(1)}, bf16[16,2048]{1,0:T(8,128)(2,1)S(1)}, u32[]{:S(2)}, u32[]{:S(2)}) %collective-permute-start.7) | collective-permute-done | bytes 65568 | tf_op jit(solution)/shard_map/ppermute | solution.py:31
  28.4 0.1 collective-permute-start.9
  28.5 0.1 pad_add_fusion.ids_ref
  28.5 1.4 %collective-permute-done.9.other_ref = bf16[4,16,2048]{2,1,0:T(8,128)(2,1)S(1)} collective-permute-done((bf16[4,16,2048]{2,1,0:T(8,128)(2,1)S(1)}, bf16[4,16,2048]{2,1,0:T(8,128)(2,1)S(1)}, u32[]{:S(2)}, u32[]{:S(2)}) %collective-permute-start.9) | collective-permute-done | bytes 262176 | tf_op jit(solution)/shard_map/ppermute | solution.py:31
  30.0 0.8 select.1
  30.8 0.3 collective-permute-start.13
  31.1 2.2 %copy-done = bf16[2048,1024]{1,0:T(8,128)(2,1)S(1)} copy-done((bf16[2048,1024]{1,0:T(8,128)(2,1)S(1)}, bf16[2048,1024]{1,0:T(8,128)(2,1)}, u32[]{:S(2)}) %copy-start) | copy-done | bytes 4194328
  33.3 4.5 %query_product.3.refs_1_ = bf16[512,1024]{1,0:T(8,128)(2,1)} custom-call(bf16[1024,2048]{1,0:T(8,128)(2,1)} %bitcast.42, bf16[2048,1024]{1,0:T(8,128)(2,1)S(1)} %copy-done), custom_call_target="tpu_custom_call" | custom-call | flops 2147483648 | bytes 6291456 | tf_op jit(solution)/shard_map/query_product/pallas_call | solution.py:122
  37.8 1.9 %collective-permute-start.10 = (bf16[2,16,2048]{2,1,0:T(8,128)(2,1)S(1)}, bf16[2,16,2048]{2,1,0:T(8,128)(2,1)S(1)}, u32[]{:S(2)}, u32[]{:S(2)}) collective-permute-start(bf16[2,16,2048]{2,1,0:T(8,128)(2,1)S(1)} %get-tuple-element.43), channel_id=1, source_target_pairs={{0,8},{8,0},{16,24},{24,16},{1,9},{9,1},{17,25},{25,17},{2,10},{10... | collective-permute-start | bytes 393224 | tf_op jit(solution)/shard_map/ppermute | solution.py:31
  39.7 0.8 collective-permute-start.11
  40.5 0.9 collective-permute-start.12
  41.4 1.1 %collective-permute-start.14 = (bf16[2,16,2048]{2,1,0:T(8,128)(2,1)S(1)}, bf16[2,16,2048]{2,1,0:T(8,128)(2,1)S(1)}, u32[]{:S(2)}, u32[]{:S(2)}) collective-permute-start(bf16[2,16,2048]{2,1,0:T(8,128)(2,1)S(1)} %get-tuple-element.49), channel_id=1, source_target_pairs={{0,16},{8,24},{16,0},{24,8},{1,17},{9,25},{17,1},{25,9},{2,18},{10... | collective-permute-start | bytes 393224 | tf_op jit(solution)/shard_map/ppermute | solution.py:31
  42.5 2.2 %collective-permute-start.15 = (bf16[2,16,2048]{2,1,0:T(8,128)(2,1)S(1)}, bf16[2,16,2048]{2,1,0:T(8,128)(2,1)S(1)}, u32[]{:S(2)}, u32[]{:S(2)}) collective-permute-start(bf16[2,16,2048]{2,1,0:T(8,128)(2,1)S(1)} %get-tuple-element.50), channel_id=1, source_target_pairs={{0,24},{8,16},{16,8},{24,0},{1,25},{9,17},{17,9},{25,1},{2,26},{10... | collective-permute-start | bytes 393224 | tf_op jit(solution)/shard_map/ppermute | solution.py:31
  44.7 4.5 %query_product.2.refs_0_ = bf16[512,1024]{1,0:T(8,128)(2,1)} custom-call(bf16[1024,2048]{1,0:T(8,128)(2,1)} %bitcast.43, bf16[2048,1024]{1,0:T(8,128)(2,1)S(1)} %copy-done), custom_call_target="tpu_custom_call" | custom-call | flops 2147483648 | bytes 6291456 | tf_op jit(solution)/shard_map/query_product/pallas_call | solution.py:122
  49.3 2.3 %fetch.2 = (bf16[512,1024]{1,0:T(8,128)(2,1)S(1)}, bf16[512,1024]{1,0:T(8,128)(2,1)S(1)}, bf16[1024,1024]{1,0:T(8,128)(2,1)S(1)}) custom-call(bf16[512,1024]{1,0:T(8,128)(2,1)} %query_product.2.refs_0_, bf16[512,1024]{1,0:T(8,128)(2,1)} %query_product.3.refs_1_, bf16[1024,1024]{1,0:T(8,128)(2,1)} %bitcast.46), custom_call_target="tpu_custom_call" | custom-call | bytes 8388608 | tf_op jit(solution)/shard_map/fetch/pallas_call | solution.py:87
  51.5 1.6 %collective-permute-done.14.refs_2_ = bf16[2,16,2048]{2,1,0:T(8,128)(2,1)S(1)} collective-permute-done((bf16[2,16,2048]{2,1,0:T(8,128)(2,1)S(1)}, bf16[2,16,2048]{2,1,0:T(8,128)(2,1)S(1)}, u32[]{:S(2)}, u32[]{:S(2)}) %collective-permute-start.14) | collective-permute-done | bytes 131104 | tf_op jit(solution)/shard_map/ppermute | solution.py:31
  53.1 3.1 %attend.2 = (bf16[512,1024]{1,0:T(8,128)(2,1)S(1)}, bf16[1024,1024]{1,0:T(8,128)(2,1)}, bf16[2,16,2048]{2,1,0:T(8,128)(2,1)S(1)}, bf16[2,16,2048]{2,1,0:T(8,128)...) custom-call(s32[2]{0:T(128)S(1)} %pad_add_fusion.ids_ref, s32[128]{0:T(128)S(1)} %copy-done.3, ...), custom_call_target="tpu_custom_call" | custom-call | flops 671088640 | bytes 4194304 | tf_op jit(solution)/shard_map/attend/pallas_call | solution.py:299
  56.3 3.1 %attend.3 = (bf16[512,1024]{1,0:T(8,128)(2,1)S(1)}, bf16[1024,1024]{1,0:T(8,128)(2,1)}, bf16[2,16,2048]{2,1,0:T(8,128)(2,1)S(1)}, bf16[2,16,2048]{2,1,0:T(8,128)...) custom-call(s32[2]{0:T(128)S(1)} %pad_add_fusion.ids_ref, ...), custom_call_target="tpu_custom_call", output_to_operand_aliasing={{1}: (9, {})} | custom-call | flops 671088640 | bytes 4194304 | tf_op jit(solution)/shard_map/attend/pallas_call | solution.py:299
  59.5 0.4 collective-permute-start.17
  59.9 0.9 collective-permute-start.19
  60.8 2.2 %collective-permute-start.21 = (bf16[2,16,2048]{2,1,0:T(8,128)(2,1)S(1)}, bf16[2,16,2048]{2,1,0:T(8,128)(2,1)S(1)}, u32[]{:S(2)}, u32[]{:S(2)}) collective-permute-start(bf16[2,16,2048]{2,1,0:T(8,128)(2,1)S(1)} %get-tuple-element.62), channel_id=1, source_target_pairs={{0,24},{8,16},{16,8},{24,0},{1,25},{9,17},{17,9},{25,1},{2,26},{10... | collective-permute-start | bytes 393224 | tf_op jit(solution)/shard_map/ppermute | solution.py:31
  63.0 0.4 collective-permute-start.16
  63.4 0.9 collective-permute-start.18
  64.3 1.6 %collective-permute-done.17.refs_3_ = bf16[2,16,2048]{2,1,0:T(8,128)(2,1)S(1)} collective-permute-done((bf16[2,16,2048]{2,1,0:T(8,128)(2,1)S(1)}, bf16[2,16,2048]{2,1,0:T(8,128)(2,1)S(1)}, u32[]{:S(2)}, u32[]{:S(2)}) %collective-permute-start.17) | collective-permute-done | bytes 131104 | tf_op jit(solution)/shard_map/ppermute | solution.py:31
  65.9 0.6 collective-permute-start.20
  66.5 1.7 %collective-permute-done.19.refs_5_ = bf16[2,16,2048]{2,1,0:T(8,128)(2,1)S(1)} collective-permute-done((bf16[2,16,2048]{2,1,0:T(8,128)(2,1)S(1)}, bf16[2,16,2048]{2,1,0:T(8,128)(2,1)S(1)}, u32[]{:S(2)}, u32[]{:S(2)}) %collective-permute-start.19) | collective-permute-done | bytes 131104 | tf_op jit(solution)/shard_map/ppermute | solution.py:31
  68.2 0.6 collective-permute-done.21.refs_7_
  68.8 2.5 %collective-permute-done.16.refs_2_ = bf16[2,16,2048]{2,1,0:T(8,128)(2,1)S(1)} collective-permute-done((bf16[2,16,2048]{2,1,0:T(8,128)(2,1)S(1)}, bf16[2,16,2048]{2,1,0:T(8,128)(2,1)S(1)}, u32[]{:S(2)}, u32[]{:S(2)}) %collective-permute-start.16) | collective-permute-done | bytes 131104 | tf_op jit(solution)/shard_map/ppermute | solution.py:31
  71.3 1.9 %collective-permute-done.18.refs_4_ = bf16[2,16,2048]{2,1,0:T(8,128)(2,1)S(1)} collective-permute-done((bf16[2,16,2048]{2,1,0:T(8,128)(2,1)S(1)}, bf16[2,16,2048]{2,1,0:T(8,128)(2,1)S(1)}, u32[]{:S(2)}, u32[]{:S(2)}) %collective-permute-start.18) | collective-permute-done | bytes 131104 | tf_op jit(solution)/shard_map/ppermute | solution.py:31
  73.2 0.9 combine.1
  74.2 1.5 %collective-permute-done.22 = bf16[4,16,2048]{2,1,0:T(8,128)(2,1)S(1)} collective-permute-done((bf16[4,16,2048]{2,1,0:T(8,128)(2,1)S(1)}, bf16[4,16,2048]{2,1,0:T(8,128)(2,1)S(1)}, u32[]{:S(2)}, u32[]{:S(2)}) %collective-permute-start.22) | collective-permute-done | bytes 262176 | tf_op jit(solution)/shard_map/ppermute | solution.py:31
  75.8 0.6 collective-permute-start.23
  76.4 3.0 %collective-permute-start.25 = (bf16[16,2048]{1,0:T(8,128)(2,1)S(1)}, bf16[16,2048]{1,0:T(8,128)(2,1)S(1)}, u32[]{:S(2)}, u32[]{:S(2)}) collective-permute-start(bf16[16,2048]{1,0:T(8,128)(2,1)S(1)} %get-tuple-element.72), channel_id=1, source_target_pairs={{0,6},{1,7},{2,4},{3,5},{4,2},{5,3},{6,0},{7,1},{8,14},{9,15},{10,... | collective-permute-start | bytes 196616 | tf_op jit(solution)/shard_map/ppermute | solution.py:31
  79.4 3.4 %image_product.2.refs_0_ = bf16[1024,2048]{1,0:T(8,128)(2,1)} custom-call(bf16[512,1024]{1,0:T(8,128)(2,1)S(1)} %get-tuple-element.54.x_ref, bf16[2048,1024]{1,0:T(8,128)(2,1)S(1)} %copy-done.1), custom_call_target="tpu_custom_call" | custom-call | flops 2147483648 | bytes 5242880 | tf_op jit(solution)/shard_map/image_product/pallas_call | solution.py:160
  82.8 0.9 collective-permute-done.25
  83.7 2.0 %collective-permute-done.24 = bf16[16,2048]{1,0:T(8,128)(2,1)S(1)} collective-permute-done((bf16[16,2048]{1,0:T(8,128)(2,1)S(1)}, bf16[16,2048]{1,0:T(8,128)(2,1)S(1)}, u32[]{:S(2)}, u32[]{:S(2)}) %collective-permute-start.24) | collective-permute-done | bytes 65568 | tf_op jit(solution)/shard_map/ppermute | solution.py:31
  85.7 1.7 %collective-permute-start.28 = (bf16[16,2048]{1,0:T(8,128)(2,1)S(1)}, bf16[16,2048]{1,0:T(8,128)(2,1)S(1)}, u32[]{:S(2)}, u32[]{:S(2)}) collective-permute-start(bf16[16,2048]{1,0:T(8,128)(2,1)S(1)} %fusion.3.refs_0_), channel_id=1, source_target_pairs={{0,24},{8,16},{16,8},{24,0},{1,25},{9,17},{17,9},{25,1},{2,26},{10... | collective-permute-start | bytes 196616 | tf_op jit(solution)/shard_map/ppermute | solution.py:31
  87.4 1.0 %collective-permute-start.27 = (bf16[16,2048]{1,0:T(8,128)(2,1)S(1)}, bf16[16,2048]{1,0:T(8,128)(2,1)S(1)}, u32[]{:S(2)}, u32[]{:S(2)}) collective-permute-start(bf16[16,2048]{1,0:T(8,128)(2,1)S(1)} %fusion.3.refs_0_), channel_id=1, source_target_pairs={{0,16},{8,24},{16,0},{24,8},{1,17},{9,25},{17,1},{25,9},{2,18},{10... | collective-permute-start | bytes 196616 | tf_op jit(solution)/shard_map/ppermute | solution.py:31
  88.4 0.9 collective-permute-start.26
  89.3 3.4 %image_product.3 = bf16[1024,2048]{1,0:T(8,128)(2,1)} custom-call(bf16[512,1024]{1,0:T(8,128)(2,1)S(1)} %get-tuple-element.53.x_ref, bf16[2048,1024]{1,0:T(8,128)(2,1)S(1)} %copy-done.1, bf16[1024,2048]{1,0:T(8,128)(2,1)} %image_product.2.refs_0_), custom_call_target="tpu_custom_call", output_to_operand_aliasing={{}: (2, {})} | custom-call | flops 2147483648 | bytes 5242880 | tf_op jit(solution)/shard_map/image_product/pallas_call | solution.py:160
  92.7 1.4 %project.3 = (f32[16,1024]{1,0:T(8,128)S(1)}, f32[16,1024]{1,0:T(8,128)S(1)}, f32[16,1024]{1,0:T(8,128)S(1)}, f32[16,1024]{1,0:T(8,128)S(1)}) custom-call(bf16[16,2048]{1,0:T(8,128)(2,1)S(1)} %fusion.3.refs_0_, bf16[16,2048]{1,0:T(8,128)(2,1)S(1)} %collective-permute-done.26.refs_1_, bf16[16,2048]{1,0:T(8,128)(2,1)S(1)} %collective-permute-done.27.refs_2_, ...), custom_call_target="tpu_custom_call" | custom-call | flops 268435456 | bytes 4194304 | tf_op jit(solution)/shard_map/project/pallas_call | solution.py:61
  94.1 1.2 %collective-permute-start.29 = (f32[16,1024]{1,0:T(8,128)S(1)}, f32[16,1024]{1,0:T(8,128)S(1)}, u32[]{:S(2)}, u32[]{:S(2)}) collective-permute-start(f32[16,1024]{1,0:T(8,128)S(1)} %get-tuple-element.66), channel_id=1, source_target_pairs={{0,8},{8,0},{16,24},{24,16},{1,9},{9,1},{17,25},{25,17},{2,10},{10... | collective-permute-start | bytes 196616 | tf_op jit(solution)/shard_map/ppermute | solution.py:31
  95.3 1.0 collective-permute-start.30
  96.3 1.3 %collective-permute-start.31 = (f32[16,1024]{1,0:T(8,128)S(1)}, f32[16,1024]{1,0:T(8,128)S(1)}, u32[]{:S(2)}, u32[]{:S(2)}) collective-permute-start(f32[16,1024]{1,0:T(8,128)S(1)} %get-tuple-element.68), channel_id=1, source_target_pairs={{0,24},{8,16},{16,8},{24,0},{1,25},{9,17},{17,9},{25,1},{2,26},{10... | collective-permute-start | bytes 196616 | tf_op jit(solution)/shard_map/ppermute | solution.py:31
  97.7 1.1 %collective-permute-done.29 = f32[16,1024]{1,0:T(8,128)S(1)} collective-permute-done((f32[16,1024]{1,0:T(8,128)S(1)}, f32[16,1024]{1,0:T(8,128)S(1)}, u32[]{:S(2)}, u32[]{:S(2)}) %collective-permute-start.29) | collective-permute-done | bytes 65568 | tf_op jit(solution)/shard_map/ppermute | solution.py:31
  98.7 1.3 %collective-permute-done.30 = f32[16,1024]{1,0:T(8,128)S(1)} collective-permute-done((f32[16,1024]{1,0:T(8,128)S(1)}, f32[16,1024]{1,0:T(8,128)S(1)}, u32[]{:S(2)}, u32[]{:S(2)}) %collective-permute-start.30) | collective-permute-done | bytes 65568 | tf_op jit(solution)/shard_map/ppermute | solution.py:31
  100.1 1.4 %collective-permute-done.31 = f32[16,1024]{1,0:T(8,128)S(1)} collective-permute-done((f32[16,1024]{1,0:T(8,128)S(1)}, f32[16,1024]{1,0:T(8,128)S(1)}, u32[]{:S(2)}, u32[]{:S(2)}) %collective-permute-start.31) | collective-permute-done | bytes 65568 | tf_op jit(solution)/shard_map/ppermute | solution.py:31
  101.5 0.7 copy-done.5
  (36 shorter events, 0.4 us)
Async XLA Ops:
  1.5 6.8 %collective-permute-start.2 = (bf16[16,1024]{1,0:T(8,128)(2,1)S(1)}, bf16[16,1024]{1,0:T(8,128)(2,1)S(1)}, u32[]{:S(2)}, u32[]{:S(2)}) collective-permute-start(bf16[16,1024]{1,0:T(8,128)(2,1)S(1)} %get-tuple-element.74), channel_id=1, source_target_pairs={{0,24},{8,16},{16,8},{24,0},{1,25},{9,17},{17,9},{25,1},{2,26},{10... | collective-permute-start | bytes 98312 | tf_op jit(solution)/shard_map/ppermute | solution.py:31
  5.5 3.9 %collective-permute-start = (bf16[16,1024]{1,0:T(8,128)(2,1)S(1)}, bf16[16,1024]{1,0:T(8,128)(2,1)S(1)}, u32[]{:S(2)}, u32[]{:S(2)}) collective-permute-start(bf16[16,1024]{1,0:T(8,128)(2,1)S(1)} %get-tuple-element.75), channel_id=1, source_target_pairs={{0,8},{8,0},{16,24},{24,16},{1,9},{9,1},{17,25},{25,17},{2,10},{10... | collective-permute-start | bytes 98312 | tf_op jit(solution)/shard_map/ppermute | solution.py:31
  6.0 3.9 %collective-permute-start.1 = (bf16[16,1024]{1,0:T(8,128)(2,1)S(1)}, bf16[16,1024]{1,0:T(8,128)(2,1)S(1)}, u32[]{:S(2)}, u32[]{:S(2)}) collective-permute-start(bf16[16,1024]{1,0:T(8,128)(2,1)S(1)} %get-tuple-element.77), channel_id=1, source_target_pairs={{0,16},{8,24},{16,0},{24,8},{1,17},{9,25},{17,1},{25,9},{2,18},{10... | collective-permute-start | bytes 98312 | tf_op jit(solution)/shard_map/ppermute | solution.py:31
  8.3 21.7 %copy-start.3 = (s32[128]{0:T(128)S(1)}, s32[128]{0:T(128)}, u32[]{:S(2)}) copy-start(s32[128]{0:T(128)} %prompt_ref.7) | copy-start | bytes 1540
  10.8 6.3 %collective-permute-start.3 = (f32[16,2048]{1,0:T(8,128)S(1)}, f32[16,2048]{1,0:T(8,128)S(1)}, u32[]{:S(2)}, u32[]{:S(2)}) collective-permute-start(f32[16,2048]{1,0:T(8,128)S(1)} %get-tuple-element.39), channel_id=1, source_target_pairs={{0,8},{8,0},{16,24},{24,16},{1,9},{9,1},{17,25},{25,17},{2,10},{10... | collective-permute-start | bytes 393224 | tf_op jit(solution)/shard_map/ppermute | solution.py:31
  12.3 7.1 %collective-permute-start.4 = (f32[16,2048]{1,0:T(8,128)S(1)}, f32[16,2048]{1,0:T(8,128)S(1)}, u32[]{:S(2)}, u32[]{:S(2)}) collective-permute-start(f32[16,2048]{1,0:T(8,128)S(1)} %get-tuple-element.40), channel_id=1, source_target_pairs={{0,16},{8,24},{16,0},{24,8},{1,17},{9,25},{17,1},{25,9},{2,18},{10... | collective-permute-start | bytes 393224 | tf_op jit(solution)/shard_map/ppermute | solution.py:31
  12.8 6.6 %collective-permute-start.5 = (f32[16,2048]{1,0:T(8,128)S(1)}, f32[16,2048]{1,0:T(8,128)S(1)}, u32[]{:S(2)}, u32[]{:S(2)}) collective-permute-start(f32[16,2048]{1,0:T(8,128)S(1)} %get-tuple-element.41), channel_id=1, source_target_pairs={{0,24},{8,16},{16,8},{24,0},{1,25},{9,17},{17,9},{25,1},{2,26},{10... | collective-permute-start | bytes 393224 | tf_op jit(solution)/shard_map/ppermute | solution.py:31
  19.5 6.6 %collective-permute-start.8 = (bf16[16,2048]{1,0:T(8,128)(2,1)S(1)}, bf16[16,2048]{1,0:T(8,128)(2,1)S(1)}, u32[]{:S(2)}, u32[]{:S(2)}) collective-permute-start(bf16[16,2048]{1,0:T(8,128)(2,1)S(1)} %add_convert_fusion), channel_id=1, source_target_pairs={{0,6},{1,7},{2,4},{3,5},{4,2},{5,3},{6,0},{7,1},{8,14},{9,15},{10,... | collective-permute-start | bytes 196616 | tf_op jit(solution)/shard_map/ppermute | solution.py:31
  23.2 5.2 %collective-permute-start.7 = (bf16[16,2048]{1,0:T(8,128)(2,1)S(1)}, bf16[16,2048]{1,0:T(8,128)(2,1)S(1)}, u32[]{:S(2)}, u32[]{:S(2)}) collective-permute-start(bf16[16,2048]{1,0:T(8,128)(2,1)S(1)} %add_convert_fusion), channel_id=1, source_target_pairs={{0,4},{1,5},{2,6},{3,7},{4,0},{5,1},{6,2},{7,3},{8,12},{9,13},{10,... | collective-permute-start | bytes 196616 | tf_op jit(solution)/shard_map/ppermute | solution.py:31
  23.2 5.2 %collective-permute-start.6 = (bf16[16,2048]{1,0:T(8,128)(2,1)S(1)}, bf16[16,2048]{1,0:T(8,128)(2,1)S(1)}, u32[]{:S(2)}, u32[]{:S(2)}) collective-permute-start(bf16[16,2048]{1,0:T(8,128)(2,1)S(1)} %add_convert_fusion), channel_id=1, source_target_pairs={{0,2},{1,3},{2,0},{3,1},{4,6},{5,7},{6,4},{7,5},{8,10},{9,11},{10,... | collective-permute-start | bytes 196616 | tf_op jit(solution)/shard_map/ppermute | solution.py:31
  28.4 1.6 %collective-permute-start.9 = (bf16[4,16,2048]{2,1,0:T(8,128)(2,1)S(1)}, bf16[4,16,2048]{2,1,0:T(8,128)(2,1)S(1)}, u32[]{:S(2)}, u32[]{:S(2)}) collective-permute-start(bf16[4,16,2048]{2,1,0:T(8,128)(2,1)S(1)} %pad_maximum_fusion.same_ref), channel_id=1, source_target_pairs={{0,1},{1,0},{2,3},{3,2},{4,5},{5,4},{6,7},{7,6},{8,9},{9,8},{10,11... | collective-permute-start | bytes 786440 | tf_op jit(solution)/shard_map/ppermute | solution.py:31
  30.8 11.7 %collective-permute-start.13 = (bf16[2,16,2048]{2,1,0:T(8,128)(2,1)S(1)}, bf16[2,16,2048]{2,1,0:T(8,128)(2,1)S(1)}, u32[]{:S(2)}, u32[]{:S(2)}) collective-permute-start(bf16[2,16,2048]{2,1,0:T(8,128)(2,1)S(1)} %get-tuple-element.48), channel_id=1, source_target_pairs={{0,8},{8,0},{16,24},{24,16},{1,9},{9,1},{17,25},{25,17},{2,10},{10... | collective-permute-start | bytes 393224 | tf_op jit(solution)/shard_map/ppermute | solution.py:31
  31.1 2.2 %copy-start = (bf16[2048,1024]{1,0:T(8,128)(2,1)S(1)}, bf16[2048,1024]{1,0:T(8,128)(2,1)}, u32[]{:S(2)}) copy-start(bf16[2048,1024]{1,0:T(8,128)(2,1)} %w_ref.7) | copy-start | bytes 12582916
  37.8 18.5 %collective-permute-start.10 = (bf16[2,16,2048]{2,1,0:T(8,128)(2,1)S(1)}, bf16[2,16,2048]{2,1,0:T(8,128)(2,1)S(1)}, u32[]{:S(2)}, u32[]{:S(2)}) collective-permute-start(bf16[2,16,2048]{2,1,0:T(8,128)(2,1)S(1)} %get-tuple-element.43), channel_id=1, source_target_pairs={{0,8},{8,0},{16,24},{24,16},{1,9},{9,1},{17,25},{25,17},{2,10},{10... | collective-permute-start | bytes 393224 | tf_op jit(solution)/shard_map/ppermute | solution.py:31
  39.7 16.6 %collective-permute-start.11 = (bf16[2,16,2048]{2,1,0:T(8,128)(2,1)S(1)}, bf16[2,16,2048]{2,1,0:T(8,128)(2,1)S(1)}, u32[]{:S(2)}, u32[]{:S(2)}) collective-permute-start(bf16[2,16,2048]{2,1,0:T(8,128)(2,1)S(1)} %get-tuple-element.44), channel_id=1, source_target_pairs={{0,16},{8,24},{16,0},{24,8},{1,17},{9,25},{17,1},{25,9},{2,18},{10... | collective-permute-start | bytes 393224 | tf_op jit(solution)/shard_map/ppermute | solution.py:31
  40.5 15.8 %collective-permute-start.12 = (bf16[2,16,2048]{2,1,0:T(8,128)(2,1)S(1)}, bf16[2,16,2048]{2,1,0:T(8,128)(2,1)S(1)}, u32[]{:S(2)}, u32[]{:S(2)}) collective-permute-start(bf16[2,16,2048]{2,1,0:T(8,128)(2,1)S(1)} %get-tuple-element.45), channel_id=1, source_target_pairs={{0,24},{8,16},{16,8},{24,0},{1,25},{9,17},{17,9},{25,1},{2,26},{10... | collective-permute-start | bytes 393224 | tf_op jit(solution)/shard_map/ppermute | solution.py:31
  41.4 11.7 %collective-permute-start.14 = (bf16[2,16,2048]{2,1,0:T(8,128)(2,1)S(1)}, bf16[2,16,2048]{2,1,0:T(8,128)(2,1)S(1)}, u32[]{:S(2)}, u32[]{:S(2)}) collective-permute-start(bf16[2,16,2048]{2,1,0:T(8,128)(2,1)S(1)} %get-tuple-element.49), channel_id=1, source_target_pairs={{0,16},{8,24},{16,0},{24,8},{1,17},{9,25},{17,1},{25,9},{2,18},{10... | collective-permute-start | bytes 393224 | tf_op jit(solution)/shard_map/ppermute | solution.py:31
  42.5 10.7 %collective-permute-start.15 = (bf16[2,16,2048]{2,1,0:T(8,128)(2,1)S(1)}, bf16[2,16,2048]{2,1,0:T(8,128)(2,1)S(1)}, u32[]{:S(2)}, u32[]{:S(2)}) collective-permute-start(bf16[2,16,2048]{2,1,0:T(8,128)(2,1)S(1)} %get-tuple-element.50), channel_id=1, source_target_pairs={{0,24},{8,16},{16,8},{24,0},{1,25},{9,17},{17,9},{25,1},{2,26},{10... | collective-permute-start | bytes 393224 | tf_op jit(solution)/shard_map/ppermute | solution.py:31
  49.3 3.9 %copy-start.4 = (s32[8]{0:T(128)S(1)}, s32[8]{0:T(128)}, u32[]{:S(2)}) copy-start(s32[8]{0:T(128)} %len_ref.3) | copy-start | bytes 100
  56.3 23.0 %copy-start.1 = (bf16[2048,1024]{1,0:T(8,128)(2,1)S(1)}, bf16[2048,1024]{1,0:T(8,128)(2,1)}, u32[]{:S(2)}) copy-start(bf16[2048,1024]{1,0:T(8,128)(2,1)} %w_ref.7) | copy-start | bytes 12582916
  59.5 6.4 %collective-permute-start.17 = (bf16[2,16,2048]{2,1,0:T(8,128)(2,1)S(1)}, bf16[2,16,2048]{2,1,0:T(8,128)(2,1)S(1)}, u32[]{:S(2)}, u32[]{:S(2)}) collective-permute-start(bf16[2,16,2048]{2,1,0:T(8,128)(2,1)S(1)} %get-tuple-element.58), channel_id=1, source_target_pairs={{0,8},{8,0},{16,24},{24,16},{1,9},{9,1},{17,25},{25,17},{2,10},{10... | collective-permute-start | bytes 393224 | tf_op jit(solution)/shard_map/ppermute | solution.py:31
  59.9 8.4 %collective-permute-start.19 = (bf16[2,16,2048]{2,1,0:T(8,128)(2,1)S(1)}, bf16[2,16,2048]{2,1,0:T(8,128)(2,1)S(1)}, u32[]{:S(2)}, u32[]{:S(2)}) collective-permute-start(bf16[2,16,2048]{2,1,0:T(8,128)(2,1)S(1)} %get-tuple-element.60), channel_id=1, source_target_pairs={{0,16},{8,24},{16,0},{24,8},{1,17},{9,25},{17,1},{25,9},{2,18},{10... | collective-permute-start | bytes 393224 | tf_op jit(solution)/shard_map/ppermute | solution.py:31
  60.8 8.0 %collective-permute-start.21 = (bf16[2,16,2048]{2,1,0:T(8,128)(2,1)S(1)}, bf16[2,16,2048]{2,1,0:T(8,128)(2,1)S(1)}, u32[]{:S(2)}, u32[]{:S(2)}) collective-permute-start(bf16[2,16,2048]{2,1,0:T(8,128)(2,1)S(1)} %get-tuple-element.62), channel_id=1, source_target_pairs={{0,24},{8,16},{16,8},{24,0},{1,25},{9,17},{17,9},{25,1},{2,26},{10... | collective-permute-start | bytes 393224 | tf_op jit(solution)/shard_map/ppermute | solution.py:31
  63.0 8.3 %collective-permute-start.16 = (bf16[2,16,2048]{2,1,0:T(8,128)(2,1)S(1)}, bf16[2,16,2048]{2,1,0:T(8,128)(2,1)S(1)}, u32[]{:S(2)}, u32[]{:S(2)}) collective-permute-start(bf16[2,16,2048]{2,1,0:T(8,128)(2,1)S(1)} %get-tuple-element.57), channel_id=1, source_target_pairs={{0,8},{8,0},{16,24},{24,16},{1,9},{9,1},{17,25},{25,17},{2,10},{10... | collective-permute-start | bytes 393224 | tf_op jit(solution)/shard_map/ppermute | solution.py:31
  63.4 9.8 %collective-permute-start.18 = (bf16[2,16,2048]{2,1,0:T(8,128)(2,1)S(1)}, bf16[2,16,2048]{2,1,0:T(8,128)(2,1)S(1)}, u32[]{:S(2)}, u32[]{:S(2)}) collective-permute-start(bf16[2,16,2048]{2,1,0:T(8,128)(2,1)S(1)} %get-tuple-element.59), channel_id=1, source_target_pairs={{0,16},{8,24},{16,0},{24,8},{1,17},{9,25},{17,1},{25,9},{2,18},{10... | collective-permute-start | bytes 393224 | tf_op jit(solution)/shard_map/ppermute | solution.py:31
  65.9 7.3 %collective-permute-start.20 = (bf16[2,16,2048]{2,1,0:T(8,128)(2,1)S(1)}, bf16[2,16,2048]{2,1,0:T(8,128)(2,1)S(1)}, u32[]{:S(2)}, u32[]{:S(2)}) collective-permute-start(bf16[2,16,2048]{2,1,0:T(8,128)(2,1)S(1)} %get-tuple-element.61), channel_id=1, source_target_pairs={{0,24},{8,16},{16,8},{24,0},{1,25},{9,17},{17,9},{25,1},{2,26},{10... | collective-permute-start | bytes 393224 | tf_op jit(solution)/shard_map/ppermute | solution.py:31
  74.1 1.6 %collective-permute-start.22 = (bf16[4,16,2048]{2,1,0:T(8,128)(2,1)S(1)}, bf16[4,16,2048]{2,1,0:T(8,128)(2,1)S(1)}, u32[]{:S(2)}, u32[]{:S(2)}) collective-permute-start(bf16[4,16,2048]{2,1,0:T(8,128)(2,1)S(1)} %get-tuple-element.64), channel_id=1, source_target_pairs={{0,1},{1,0},{2,3},{3,2},{4,5},{5,4},{6,7},{7,6},{8,9},{9,8},{10,11... | collective-permute-start | bytes 786440 | tf_op jit(solution)/shard_map/ppermute | solution.py:31
  75.8 7.0 %collective-permute-start.23 = (bf16[16,2048]{1,0:T(8,128)(2,1)S(1)}, bf16[16,2048]{1,0:T(8,128)(2,1)S(1)}, u32[]{:S(2)}, u32[]{:S(2)}) collective-permute-start(bf16[16,2048]{1,0:T(8,128)(2,1)S(1)} %get-tuple-element.71), channel_id=1, source_target_pairs={{0,2},{1,3},{2,0},{3,1},{4,6},{5,7},{6,4},{7,5},{8,10},{9,11},{10,... | collective-permute-start | bytes 196616 | tf_op jit(solution)/shard_map/ppermute | solution.py:31
  76.4 7.3 %collective-permute-start.25 = (bf16[16,2048]{1,0:T(8,128)(2,1)S(1)}, bf16[16,2048]{1,0:T(8,128)(2,1)S(1)}, u32[]{:S(2)}, u32[]{:S(2)}) collective-permute-start(bf16[16,2048]{1,0:T(8,128)(2,1)S(1)} %get-tuple-element.72), channel_id=1, source_target_pairs={{0,6},{1,7},{2,4},{3,5},{4,2},{5,3},{6,0},{7,1},{8,14},{9,15},{10,... | collective-permute-start | bytes 196616 | tf_op jit(solution)/shard_map/ppermute | solution.py:31
  79.4 6.3 %collective-permute-start.24 = (bf16[16,2048]{1,0:T(8,128)(2,1)S(1)}, bf16[16,2048]{1,0:T(8,128)(2,1)S(1)}, u32[]{:S(2)}, u32[]{:S(2)}) collective-permute-start(bf16[16,2048]{1,0:T(8,128)(2,1)S(1)} %get-tuple-element.73), channel_id=1, source_target_pairs={{0,4},{1,5},{2,6},{3,7},{4,0},{5,1},{6,2},{7,3},{8,12},{9,13},{10,... | collective-permute-start | bytes 196616 | tf_op jit(solution)/shard_map/ppermute | solution.py:31
  85.7 6.9 %collective-permute-start.28 = (bf16[16,2048]{1,0:T(8,128)(2,1)S(1)}, bf16[16,2048]{1,0:T(8,128)(2,1)S(1)}, u32[]{:S(2)}, u32[]{:S(2)}) collective-permute-start(bf16[16,2048]{1,0:T(8,128)(2,1)S(1)} %fusion.3.refs_0_), channel_id=1, source_target_pairs={{0,24},{8,16},{16,8},{24,0},{1,25},{9,17},{17,9},{25,1},{2,26},{10... | collective-permute-start | bytes 196616 | tf_op jit(solution)/shard_map/ppermute | solution.py:31
  87.4 5.3 %collective-permute-start.27 = (bf16[16,2048]{1,0:T(8,128)(2,1)S(1)}, bf16[16,2048]{1,0:T(8,128)(2,1)S(1)}, u32[]{:S(2)}, u32[]{:S(2)}) collective-permute-start(bf16[16,2048]{1,0:T(8,128)(2,1)S(1)} %fusion.3.refs_0_), channel_id=1, source_target_pairs={{0,16},{8,24},{16,0},{24,8},{1,17},{9,25},{17,1},{25,9},{2,18},{10... | collective-permute-start | bytes 196616 | tf_op jit(solution)/shard_map/ppermute | solution.py:31
  88.4 4.3 %collective-permute-start.26 = (bf16[16,2048]{1,0:T(8,128)(2,1)S(1)}, bf16[16,2048]{1,0:T(8,128)(2,1)S(1)}, u32[]{:S(2)}, u32[]{:S(2)}) collective-permute-start(bf16[16,2048]{1,0:T(8,128)(2,1)S(1)} %fusion.3.refs_0_), channel_id=1, source_target_pairs={{0,8},{8,0},{16,24},{24,16},{1,9},{9,1},{17,25},{25,17},{2,10},{10... | collective-permute-start | bytes 196616 | tf_op jit(solution)/shard_map/ppermute | solution.py:31
  89.3 3.4 %copy-start.2 = (bf16[1024,2048]{1,0:T(8,128)(2,1)S(1)}, bf16[1024,2048]{1,0:T(8,128)(2,1)}, u32[]{:S(2)}) copy-start(bf16[1024,2048]{1,0:T(8,128)(2,1)} %refs_4_.1) | copy-start | bytes 12582916
  94.1 4.7 %collective-permute-start.29 = (f32[16,1024]{1,0:T(8,128)S(1)}, f32[16,1024]{1,0:T(8,128)S(1)}, u32[]{:S(2)}, u32[]{:S(2)}) collective-permute-start(f32[16,1024]{1,0:T(8,128)S(1)} %get-tuple-element.66), channel_id=1, source_target_pairs={{0,8},{8,0},{16,24},{24,16},{1,9},{9,1},{17,25},{25,17},{2,10},{10... | collective-permute-start | bytes 196616 | tf_op jit(solution)/shard_map/ppermute | solution.py:31
  95.3 4.8 %collective-permute-start.30 = (f32[16,1024]{1,0:T(8,128)S(1)}, f32[16,1024]{1,0:T(8,128)S(1)}, u32[]{:S(2)}, u32[]{:S(2)}) collective-permute-start(f32[16,1024]{1,0:T(8,128)S(1)} %get-tuple-element.67), channel_id=1, source_target_pairs={{0,16},{8,24},{16,0},{24,8},{1,17},{9,25},{17,1},{25,9},{2,18},{10... | collective-permute-start | bytes 196616 | tf_op jit(solution)/shard_map/ppermute | solution.py:31
  96.3 5.2 %collective-permute-start.31 = (f32[16,1024]{1,0:T(8,128)S(1)}, f32[16,1024]{1,0:T(8,128)S(1)}, u32[]{:S(2)}, u32[]{:S(2)}) collective-permute-start(f32[16,1024]{1,0:T(8,128)S(1)} %get-tuple-element.68), channel_id=1, source_target_pairs={{0,24},{8,16},{16,8},{24,0},{1,25},{9,17},{17,9},{25,1},{2,26},{10... | collective-permute-start | bytes 196616 | tf_op jit(solution)/shard_map/ppermute | solution.py:31
  101.5 0.7 copy-start.5

commit v4 on v3

--- a/solution.py
+++ b/solution.py
@@ -136,14 +136,16 @@
     )(far(tokens), weight)
 
 
-def image_product(d_queries, weight, held, row0, total):
+def image_product(d_queries, weight, context, held, row0, total):
     rows, depth = d_queries.shape
     width = weight.shape[0]
     step = 256
     steps = rows // step
 
-    def body(x_ref, w_ref, *refs):
-        o_ref, buf, sem = refs[-3:]
+    def body(x_ref, w_ref, c_ref, *refs):
+        o_ref, all_ref, buf, sem, c_sem = refs[-5:]
+        moved = pltpu.make_async_copy(c_ref, all_ref.at[pl.ds(row0, rows), :], c_sem)
+        moved.start()
 
         def put(i):
             return pltpu.make_async_copy(
@@ -155,22 +157,27 @@
             put(i).start()
         for i in range(steps):
             put(i).wait()
-
-    more = [] if held is None else [held]
-    return pl.pallas_call(
-        body,
-        in_specs=[VMEM, VMEM] + [ANY] * len(more),
-        out_specs=ANY,
-        out_shape=shape_of(total, width),
-        scratch_shapes=[pltpu.VMEM((steps, step, width), BF16), pltpu.SemaphoreType.DMA((steps,))],
-        input_output_aliases={2: 0} if more else {},
+        moved.wait()
+
+    more = [] if held is None else list(held)
+    return pl.pallas_call(
+        body,
+        in_specs=[VMEM, VMEM, VMEM] + [ANY] * len(more),
+        out_specs=[ANY, ANY],
+        out_shape=[shape_of(total, width), shape_of(total, depth)],
+        scratch_shapes=[
+            pltpu.VMEM((steps, step, width), BF16),
+            pltpu.SemaphoreType.DMA((steps,)),
+            pltpu.SemaphoreType.DMA,
+        ],
+        input_output_aliases={3: 0, 4: 1} if more else {},
         compiler_params=params(24),
         cost_estimate=cost(2 * rows * depth * width, 2 * (rows * depth + depth * width)),
         name="image_product",
-    )(d_queries, weight, *more)
-
-
-def select(ids, prompt_of, same, other, dims):
+    )(d_queries, weight, context, *more)
+
+
+def select(ids, prompt_of, same, other, half, dims):
     samp_dev, n_grp, n_dev, halves = dims
     _, block_len, width = same.shape
     part = samp_dev // halves
@@ -178,29 +185,28 @@
     def body(ids_ref, prompt_ref, same_ref, other_ref, *outs):
         for k in range(n_grp):
             base = ((ids_ref[0] ^ k) * n_dev + ids_ref[1]) * samp_dev
-            for s in range(samp_dev):
-                rel = prompt_ref[base + s] ^ ids_ref[1]
-                out = outs[k * halves + s // part]
+            for s in range(part):
+                rel = prompt_ref[base + half * part + s] ^ ids_ref[1]
 
                 @pl.when(rel & 1 == 0)
                 def _():
-                    out[s % part] = same_ref[rel >> 1]
+                    outs[k][s] = same_ref[rel >> 1]
 
                 @pl.when(rel & 1 == 1)
                 def _():
-                    out[s % part] = other_ref[rel >> 1]
+                    outs[k][s] = other_ref[rel >> 1]
 
     return pl.pallas_call(
         body,
         in_specs=[SMEM, SMEM, VMEM, VMEM],
-        out_specs=[VMEM] * (n_grp * halves),
-        out_shape=[shape_of(part, block_len, width)] * (n_grp * halves),
+        out_specs=[VMEM] * n_grp,
+        out_shape=[shape_of(part, block_len, width)] * n_grp,
         compiler_params=params(16),
         name="select",
     )(ids, prompt_of, same, other)
 
 
-def attend(ids, prompt_of, lens, queries, grads, slots, held, first, dims):
+def attend(ids, prompt_of, lens, queries, grads, slots, first, dims):
     samp_dev, img_len, inner, n_grp, n_dev = dims
     part, block_len, _ = slots[0].shape
     full_len = n_grp * block_len
@@ -208,18 +214,11 @@
 
     def body(ids_ref, prompt_ref, len_ref, q_ref, g_ref, *refs):
         ins = refs[:n_grp]
-        dq_ref, ctx_ref = refs[-(n_grp + 4)], refs[-(n_grp + 3)]
-        outs = refs[-(n_grp + 2) : -2]
-        buf, sem = refs[-2:]
+        dq_ref, ctx_ref, *outs = refs[n_grp:]
         row = lax.broadcasted_iota(jnp.int32, (full_len, 1), 0)
         token = ((row // block_len) ^ ids_ref[0]) * block_len + row % block_len
         zero = jnp.zeros((full_len, HD), BF16)
         base = (ids_ref[0] * n_dev + ids_ref[1]) * samp_dev + first
-
-        def put(s):
-            return pltpu.make_async_copy(
-                buf.at[s], ctx_ref.at[pl.ds((first + s) * img_len, img_len), :], sem.at[s]
-            )
 
         items = [(s, h) for s in range(part) for h in range(0, HEADS, 2)]
         kept = {}
@@ -273,7 +272,7 @@
             soft_b, d_scores = kept.pop(n)
             d_keys = dot(d_scores, q_ref[at, pair], NN).astype(BF16)
             d_values = dot(soft_b, g_ref[all_at, pair], NN).astype(BF16)
-            buf[s, :, pair] = dot(soft_b, diagonal(s, v_one, v_two), TN).astype(BF16)
+            ctx_ref[at, pair] = dot(soft_b, diagonal(s, v_one, v_two), TN).astype(BF16)
             dq_ref[at, pair] = dot(d_scores, diagonal(s, one, two), TN).astype(BF16)
             for k in range(n_grp):
                 a = slice(k * block_len, (k + 1) * block_len)
@@ -282,8 +281,6 @@
                 outs[k][s, :, two] = d_keys[b, HD:]
                 outs[k][s, :, v_one] = d_values[a, :HD]
                 outs[k][s, :, v_two] = d_values[b, HD:]
-            if h == HEADS - 2:
-                put(s).start()
 
         enter(0)
         for n in range(len(items)):
@@ -291,23 +288,17 @@
                 enter(n + 1)
             weigh(n)
             leave(n)
-        for s in range(part):
-            put(s).wait()
-
-    more = [] if held is None else [held]
+
     rows = part * img_len
     return pl.pallas_call(
         body,
-        in_specs=[SMEM, SMEM, SMEM, VMEM, VMEM] + [VMEM] * n_grp + [ANY] * len(more),
-        out_specs=[VMEM, ANY] + [VMEM] * n_grp,
-        out_shape=[shape_of(rows, inner), shape_of(samp_dev * img_len, inner)]
-        + [shape_of(part, block_len, 2 * inner)] * n_grp,
-        scratch_shapes=[pltpu.VMEM((part, img_len, inner), BF16), pltpu.SemaphoreType.DMA((part,))],
-        input_output_aliases={5 + n_grp: 1} if more else {},
+        in_specs=[SMEM, SMEM, SMEM, VMEM, VMEM] + [VMEM] * n_grp,
+        out_specs=[VMEM] * (n_grp + 2),
+        out_shape=[shape_of(rows, inner)] * 2 + [shape_of(part, block_len, 2 * inner)] * n_grp,
         compiler_params=params(24),
         cost_estimate=cost(20 * rows * full_len * inner, 8 * rows * inner),
         name="attend",
-    )(ids, prompt_of, lens, queries, grads, *slots, *more)
+    )(ids, prompt_of, lens, queries, grads, *slots)
 
 
 def combine(ids, prompt_of, arrived, dims):
@@ -376,30 +367,33 @@
     same = jnp.stack([kv_block] + [partner(kv_block, "dev", n_dev, 2 * k) for k in range(1, chips)])
     other = partner(same, "dev", n_dev, 1)
     dims = (samp_dev, n_grp, n_dev, HALVES)
-    chosen = select(ids, sample_prompt, same, other, dims)
-    slots = [over_grp(chosen[half::HALVES]) for half in range(HALVES)]
-
-    context, arrived, d_queries = None, [], []
+    slots = []
     for half in range(HALVES):
-        d_q, context, *d_kv = attend(
+        chosen = select(ids, sample_prompt, same, other, half, dims)
+        slots.append(over_grp(chosen))
+
+    contexts, arrived, d_queries = [], [], []
+    for half in range(HALVES):
+        d_q, ctx, *d_kv = attend(
             ids,
             sample_prompt,
             caption_len,
             queries[half],
             grads,
             slots[half],
-            context,
             half * part,
             (samp_dev, img_len, inner, n_grp, n_dev),
         )
         d_queries.append(d_q)
+        contexts.append(ctx)
         arrived.append(over_grp(d_kv))
 
-    image_grad = None
+    held = None
     for half in range(HALVES):
-        image_grad = image_product(
-            d_queries[half], q_weight, image_grad, half * part * img_len, rows
+        held = image_product(
+            d_queries[half], q_weight, contexts[half], held, half * part * img_len, rows
         )
+    image_grad, context = held
 
     mine, theirs = combine(ids, sample_prompt, list(zip(*arrived)), dims)
     both = mine + partner(theirs, "dev", n_dev, 1).astype(F32)

time: 103 us -> 96.3 us (0.935)
  waiting for transfers between devices: 30.7 us -> 23.8 us
  starting transfers between devices: 36 us -> 37.6 us
    ppermute x32, waiting for transfers between devices: 30.7 us -> 23.8 us  [partner(): return lax.ppermute(x, axis, [(i, i ^ k) for i in range(size)])]
    ppermute x32, starting transfers between devices: 36 us -> 37.6 us  [partner(): return lax.ppermute(x, axis, [(i, i ^ k) for i in range(size)])]
    pallas_call x2, Pallas kernels: 6.25 us -> 4.63 us  [attend(): pl.pallas_call(body, in_specs=[SMEM, SMEM, SMEM, VMEM, VMEM] + [VMEM] * n...]
  transfers between devices with their start and end apart: 32 -> 32, of which waited for: 19 -> 15; matrix products, arithmetic and copies ran while one was open for 0% -> 0% of each run, Pallas kernels for 23% -> 27%
where the time goes in v4:
time: 96.3 us; the launch traced here: 96 us
  starting transfers between devices  37.6 us (39%)
  Pallas kernels  29.6 us (31%)
  waiting for transfers between devices  23.8 us (25%)
  local copies, waits for them, and re-layouts  3.81 us (4%)
    ppermute x32, starting transfers between devices, partner(): return lax.ppermute(x, axis, [(i, i ^ k) for i in range(size)])  37.6 us
    ppermute x32, waiting for transfers between devices, partner(): return lax.ppermute(x, axis, [(i, i ^ k) for i in range(size)])  23.8 us
    pallas_call x2, Pallas kernels, query_product(): pl.pallas_call(body, in_specs=[HBM, VMEM], out_specs=HBM, out_shape=pltpu...  9.11 us
    pallas_call x2, Pallas kernels, image_product(): pl.pallas_call(body, in_specs=[VMEM, VMEM, VMEM] + [ANY] * len(more), out...  6.74 us
    pallas_call x2, Pallas kernels, attend(): pl.pallas_call(body, in_specs=[SMEM, SMEM, SMEM, VMEM, VMEM] + [VMEM] * n...  4.63 us
    pallas_call x2, Pallas kernels, fetch(): pl.pallas_call(body, in_specs=[HBM] * n, out_specs=[VMEM] * n, out_shape=...  4.46 us
    unnamed x12, local copies, waits for them, and re-layouts  2.91 us
    pallas_call x2, Pallas kernels, project(): pl.pallas_call(body, in_specs=[VMEM] * (n + 1), out_specs=[VMEM] * n, out...  2.22 us
  transfers between devices with their start and end apart: 32, of which 15 were waited for; matrix products, arithmetic and copies ran while one was open for 0% of the time, Pallas kernels for 27%

profile of v4, /device:TPU:0, one launch (start us, length us, event | category | flops | bytes accessed | tf_op | source)
XLA Modules:
  0.0 96.0 jit_solution(16018790940916704842)
XLA Ops:
  0.7 0.8 dynamic-slice_bitcast_fusion
  1.5 4.0 %collective-permute-start.2 = (bf16[16,1024]{1,0:T(8,128)(2,1)S(1)}, bf16[16,1024]{1,0:T(8,128)(2,1)S(1)}, u32[]{:S(2)}, u32[]{:S(2)}) collective-permute-start(bf16[16,1024]{1,0:T(8,128)(2,1)S(1)} %get-tuple-element.82), channel_id=1, source_target_pairs={{0,24},{8,16},{16,8},{24,0},{1,25},{9,17},{17,9},{25,1},{2,26},{10... | collective-permute-start | bytes 98312 | tf_op jit(solution)/shard_map/ppermute | solution.py:31
  5.5 0.5 collective-permute-start
  6.0 0.1 collective-permute-start.1
  6.1 2.2 %fetch.3.refs_4_ = bf16[1024,2048]{1,0:T(8,128)(2,1)S(1)} custom-call(bf16[1024,2048]{1,0:T(8,128)(2,1)} %refs_4_.1), custom_call_target="tpu_custom_call" | custom-call | bytes 8388608 | tf_op jit(solution)/shard_map/fetch/pallas_call | solution.py:87
  8.3 1.1 %collective-permute-done.refs_1_ = bf16[16,1024]{1,0:T(8,128)(2,1)S(1)} collective-permute-done((bf16[16,1024]{1,0:T(8,128)(2,1)S(1)}, bf16[16,1024]{1,0:T(8,128)(2,1)S(1)}, u32[]{:S(2)}, u32[]{:S(2)}) %collective-permute-start) | collective-permute-done | bytes 32800 | tf_op jit(solution)/shard_map/ppermute | solution.py:31
  9.4 0.5 collective-permute-done.1.refs_2_
  9.9 0.8 project.2
  10.8 1.6 %collective-permute-start.3 = (f32[16,2048]{1,0:T(8,128)S(1)}, f32[16,2048]{1,0:T(8,128)S(1)}, u32[]{:S(2)}, u32[]{:S(2)}) collective-permute-start(f32[16,2048]{1,0:T(8,128)S(1)} %get-tuple-element.43), channel_id=1, source_target_pairs={{0,8},{8,0},{16,24},{24,16},{1,9},{9,1},{17,25},{25,17},{2,10},{10... | collective-permute-start | bytes 393224 | tf_op jit(solution)/shard_map/ppermute | solution.py:31
  12.3 0.5 collective-permute-start.4
  12.8 1.5 %collective-permute-start.5 = (f32[16,2048]{1,0:T(8,128)S(1)}, f32[16,2048]{1,0:T(8,128)S(1)}, u32[]{:S(2)}, u32[]{:S(2)}) collective-permute-start(f32[16,2048]{1,0:T(8,128)S(1)} %get-tuple-element.45), channel_id=1, source_target_pairs={{0,24},{8,16},{16,8},{24,0},{1,25},{9,17},{17,9},{25,1},{2,26},{10... | collective-permute-start | bytes 393224 | tf_op jit(solution)/shard_map/ppermute | solution.py:31
  14.3 2.7 %collective-permute-done.3 = f32[16,2048]{1,0:T(8,128)S(1)} collective-permute-done((f32[16,2048]{1,0:T(8,128)S(1)}, f32[16,2048]{1,0:T(8,128)S(1)}, u32[]{:S(2)}, u32[]{:S(2)}) %collective-permute-start.3) | collective-permute-done | bytes 131104 | tf_op jit(solution)/shard_map/ppermute | solution.py:31
  17.0 2.4 %collective-permute-done.4 = f32[16,2048]{1,0:T(8,128)S(1)} collective-permute-done((f32[16,2048]{1,0:T(8,128)S(1)}, f32[16,2048]{1,0:T(8,128)S(1)}, u32[]{:S(2)}, u32[]{:S(2)}) %collective-permute-start.4) | collective-permute-done | bytes 131104 | tf_op jit(solution)/shard_map/ppermute | solution.py:31
  19.5 3.7 %collective-permute-start.8 = (bf16[16,2048]{1,0:T(8,128)(2,1)S(1)}, bf16[16,2048]{1,0:T(8,128)(2,1)S(1)}, u32[]{:S(2)}, u32[]{:S(2)}) collective-permute-start(bf16[16,2048]{1,0:T(8,128)(2,1)S(1)} %add_convert_fusion), channel_id=1, source_target_pairs={{0,6},{1,7},{2,4},{3,5},{4,2},{5,3},{6,0},{7,1},{8,14},{9,15},{10,... | collective-permute-start | bytes 196616 | tf_op jit(solution)/shard_map/ppermute | solution.py:31
  23.2 0.8 collective-permute-start.6
  24.0 2.1 %collective-permute-done.8 = bf16[16,2048]{1,0:T(8,128)(2,1)S(1)} collective-permute-done((bf16[16,2048]{1,0:T(8,128)(2,1)S(1)}, bf16[16,2048]{1,0:T(8,128)(2,1)S(1)}, u32[]{:S(2)}, u32[]{:S(2)}) %collective-permute-start.8) | collective-permute-done | bytes 65568 | tf_op jit(solution)/shard_map/ppermute | solution.py:31
  26.1 2.2 %collective-permute-done.7 = bf16[16,2048]{1,0:T(8,128)(2,1)S(1)} collective-permute-done((bf16[16,2048]{1,0:T(8,128)(2,1)S(1)}, bf16[16,2048]{1,0:T(8,128)(2,1)S(1)}, u32[]{:S(2)}, u32[]{:S(2)}) %collective-permute-start.7) | collective-permute-done | bytes 65568 | tf_op jit(solution)/shard_map/ppermute | solution.py:31
  28.4 0.1 collective-permute-start.9
  28.5 0.1 pad_add_fusion.ids_ref
  28.5 2.2 %copy-done = bf16[2048,1024]{1,0:T(8,128)(2,1)S(1)} copy-done((bf16[2048,1024]{1,0:T(8,128)(2,1)S(1)}, bf16[2048,1024]{1,0:T(8,128)(2,1)}, u32[]{:S(2)}) %copy-start) | copy-done | bytes 4194328
  30.7 4.6 %query_product.3.refs_1_ = bf16[512,1024]{1,0:T(8,128)(2,1)} custom-call(bf16[1024,2048]{1,0:T(8,128)(2,1)} %bitcast.42, bf16[2048,1024]{1,0:T(8,128)(2,1)S(1)} %copy-done), custom_call_target="tpu_custom_call" | custom-call | flops 2147483648 | bytes 6291456 | tf_op jit(solution)/shard_map/query_product/pallas_call | solution.py:122
  35.3 0.7 select.3
  36.0 0.3 collective-permute-start.13
  36.3 1.1 %collective-permute-start.14 = (bf16[2,16,2048]{2,1,0:T(8,128)(2,1)S(1)}, bf16[2,16,2048]{2,1,0:T(8,128)(2,1)S(1)}, u32[]{:S(2)}, u32[]{:S(2)}) collective-permute-start(bf16[2,16,2048]{2,1,0:T(8,128)(2,1)S(1)} %get-tuple-element.55), channel_id=1, source_target_pairs={{0,16},{8,24},{16,0},{24,8},{1,17},{9,25},{17,1},{25,9},{2,18},{10... | collective-permute-start | bytes 393224 | tf_op jit(solution)/shard_map/ppermute | solution.py:31
  37.4 2.2 %collective-permute-start.15 = (bf16[2,16,2048]{2,1,0:T(8,128)(2,1)S(1)}, bf16[2,16,2048]{2,1,0:T(8,128)(2,1)S(1)}, u32[]{:S(2)}, u32[]{:S(2)}) collective-permute-start(bf16[2,16,2048]{2,1,0:T(8,128)(2,1)S(1)} %get-tuple-element.56), channel_id=1, source_target_pairs={{0,24},{8,16},{16,8},{24,0},{1,25},{9,17},{17,9},{25,1},{2,26},{10... | collective-permute-start | bytes 393224 | tf_op jit(solution)/shard_map/ppermute | solution.py:31
  39.6 4.5 %query_product.2.refs_0_ = bf16[512,1024]{1,0:T(8,128)(2,1)} custom-call(bf16[1024,2048]{1,0:T(8,128)(2,1)} %bitcast.43, bf16[2048,1024]{1,0:T(8,128)(2,1)S(1)} %copy-done), custom_call_target="tpu_custom_call" | custom-call | flops 2147483648 | bytes 6291456 | tf_op jit(solution)/shard_map/query_product/pallas_call | solution.py:122
  44.1 2.3 %fetch.2 = (bf16[512,1024]{1,0:T(8,128)(2,1)S(1)}, bf16[512,1024]{1,0:T(8,128)(2,1)S(1)}, bf16[1024,1024]{1,0:T(8,128)(2,1)S(1)}) custom-call(bf16[512,1024]{1,0:T(8,128)(2,1)} %query_product.2.refs_0_, bf16[512,1024]{1,0:T(8,128)(2,1)} %query_product.3.refs_1_, bf16[1024,1024]{1,0:T(8,128)(2,1)} %bitcast.45), custom_call_target="tpu_custom_call" | custom-call | bytes 8388608 | tf_op jit(solution)/shard_map/fetch/pallas_call | solution.py:87
  46.4 0.9 select.2
  47.3 0.3 collective-permute-start.10
  47.6 1.1 %collective-permute-start.11 = (bf16[2,16,2048]{2,1,0:T(8,128)(2,1)S(1)}, bf16[2,16,2048]{2,1,0:T(8,128)(2,1)S(1)}, u32[]{:S(2)}, u32[]{:S(2)}) collective-permute-start(bf16[2,16,2048]{2,1,0:T(8,128)(2,1)S(1)} %get-tuple-element.48), channel_id=1, source_target_pairs={{0,16},{8,24},{16,0},{24,8},{1,17},{9,25},{17,1},{25,9},{2,18},{10... | collective-permute-start | bytes 393224 | tf_op jit(solution)/shard_map/ppermute | solution.py:31
  48.7 2.2 %collective-permute-start.12 = (bf16[2,16,2048]{2,1,0:T(8,128)(2,1)S(1)}, bf16[2,16,2048]{2,1,0:T(8,128)(2,1)S(1)}, u32[]{:S(2)}, u32[]{:S(2)}) collective-permute-start(bf16[2,16,2048]{2,1,0:T(8,128)(2,1)S(1)} %get-tuple-element.49), channel_id=1, source_target_pairs={{0,24},{8,16},{16,8},{24,0},{1,25},{9,17},{17,9},{25,1},{2,26},{10... | collective-permute-start | bytes 393224 | tf_op jit(solution)/shard_map/ppermute | solution.py:31
  50.9 2.3 %attend.3 = (bf16[512,1024]{1,0:T(8,128)(2,1)S(1)}, bf16[512,1024]{1,0:T(8,128)(2,1)S(1)}, bf16[2,16,2048]{2,1,0:T(8,128)(2,1)S(1)}, bf16[2,16,2048]{2,1,0:T(8,1...) custom-call(s32[2]{0:T(128)S(1)} %pad_add_fusion.ids_ref, s32[128]{0:T(128)S(1)} %copy-done.3, ...), custom_call_target="tpu_custom_call" | custom-call | flops 671088640 | bytes 4194304 | tf_op jit(solution)/shard_map/attend/pallas_call | solution.py:293
  53.2 0.2 collective-permute-start.16
  53.5 1.1 %collective-permute-start.18 = (bf16[2,16,2048]{2,1,0:T(8,128)(2,1)S(1)}, bf16[2,16,2048]{2,1,0:T(8,128)(2,1)S(1)}, u32[]{:S(2)}, u32[]{:S(2)}) collective-permute-start(bf16[2,16,2048]{2,1,0:T(8,128)(2,1)S(1)} %get-tuple-element.67), channel_id=1, source_target_pairs={{0,16},{8,24},{16,0},{24,8},{1,17},{9,25},{17,1},{25,9},{2,18},{10... | collective-permute-start | bytes 393224 | tf_op jit(solution)/shard_map/ppermute | solution.py:31
  54.6 2.2 %collective-permute-start.20 = (bf16[2,16,2048]{2,1,0:T(8,128)(2,1)S(1)}, bf16[2,16,2048]{2,1,0:T(8,128)(2,1)S(1)}, u32[]{:S(2)}, u32[]{:S(2)}) collective-permute-start(bf16[2,16,2048]{2,1,0:T(8,128)(2,1)S(1)} %get-tuple-element.69), channel_id=1, source_target_pairs={{0,24},{8,16},{16,8},{24,0},{1,25},{9,17},{17,9},{25,1},{2,26},{10... | collective-permute-start | bytes 393224 | tf_op jit(solution)/shard_map/ppermute | solution.py:31
  56.8 2.3 %attend.2 = (bf16[512,1024]{1,0:T(8,128)(2,1)S(1)}, bf16[512,1024]{1,0:T(8,128)(2,1)S(1)}, bf16[2,16,2048]{2,1,0:T(8,128)(2,1)S(1)}, bf16[2,16,2048]{2,1,0:T(8,1...) custom-call(s32[2]{0:T(128)S(1)} %pad_add_fusion.ids_ref, s32[128]{0:T(128)S(1)} %copy-done.3, ...), custom_call_target="tpu_custom_call" | custom-call | flops 671088640 | bytes 4194304 | tf_op jit(solution)/shard_map/attend/pallas_call | solution.py:293
  59.1 0.9 collective-permute-start.17
  60.0 0.6 collective-permute-start.19
  60.6 2.1 %collective-permute-start.21 = (bf16[2,16,2048]{2,1,0:T(8,128)(2,1)S(1)}, bf16[2,16,2048]{2,1,0:T(8,128)(2,1)S(1)}, u32[]{:S(2)}, u32[]{:S(2)}) collective-permute-start(bf16[2,16,2048]{2,1,0:T(8,128)(2,1)S(1)} %get-tuple-element.70), channel_id=1, source_target_pairs={{0,24},{8,16},{16,8},{24,0},{1,25},{9,17},{17,9},{25,1},{2,26},{10... | collective-permute-start | bytes 393224 | tf_op jit(solution)/shard_map/ppermute | solution.py:31
  62.7 2.4 %collective-permute-done.17.refs_3_ = bf16[2,16,2048]{2,1,0:T(8,128)(2,1)S(1)} collective-permute-done((bf16[2,16,2048]{2,1,0:T(8,128)(2,1)S(1)}, bf16[2,16,2048]{2,1,0:T(8,128)(2,1)S(1)}, u32[]{:S(2)}, u32[]{:S(2)}) %collective-permute-start.17) | collective-permute-done | bytes 131104 | tf_op jit(solution)/shard_map/ppermute | solution.py:31
  65.1 1.9 %collective-permute-done.19.refs_5_ = bf16[2,16,2048]{2,1,0:T(8,128)(2,1)S(1)} collective-permute-done((bf16[2,16,2048]{2,1,0:T(8,128)(2,1)S(1)}, bf16[2,16,2048]{2,1,0:T(8,128)(2,1)S(1)}, u32[]{:S(2)}, u32[]{:S(2)}) %collective-permute-start.19) | collective-permute-done | bytes 131104 | tf_op jit(solution)/shard_map/ppermute | solution.py:31
  67.0 0.9 combine.1
  67.9 0.1 collective-permute-start.22
  68.0 1.5 %collective-permute-done.22 = bf16[4,16,2048]{2,1,0:T(8,128)(2,1)S(1)} collective-permute-done((bf16[4,16,2048]{2,1,0:T(8,128)(2,1)S(1)}, bf16[4,16,2048]{2,1,0:T(8,128)(2,1)S(1)}, u32[]{:S(2)}, u32[]{:S(2)}) %collective-permute-start.22) | collective-permute-done | bytes 262176 | tf_op jit(solution)/shard_map/ppermute | solution.py:31
  69.5 0.1 fusion.4
  69.6 0.6 collective-permute-start.23
  70.1 3.0 %collective-permute-start.25 = (bf16[16,2048]{1,0:T(8,128)(2,1)S(1)}, bf16[16,2048]{1,0:T(8,128)(2,1)S(1)}, u32[]{:S(2)}, u32[]{:S(2)}) collective-permute-start(bf16[16,2048]{1,0:T(8,128)(2,1)S(1)} %get-tuple-element.80), channel_id=1, source_target_pairs={{0,6},{1,7},{2,4},{3,5},{4,2},{5,3},{6,0},{7,1},{8,14},{9,15},{10,... | collective-permute-start | bytes 196616 | tf_op jit(solution)/shard_map/ppermute | solution.py:31
  73.1 0.0 collective-permute-start.24
  73.1 3.4 %image_product.2 = (bf16[1024,2048]{1,0:T(8,128)(2,1)}, bf16[1024,1024]{1,0:T(8,128)(2,1)}) custom-call(bf16[512,1024]{1,0:T(8,128)(2,1)S(1)} %get-tuple-element.57.x_ref, bf16[2048,1024]{1,0:T(8,128)(2,1)S(1)} %copy-done.1, bf16[512,1024]{1,0:T(8,128)(2,1)S(1)} %get-tuple-element.58.c_ref), custom_call_target="tpu_custom_call" | custom-call | flops 2147483648 | bytes 5242880 | tf_op jit(solution)/shard_map/image_product/pallas_call | solution.py:163
  76.5 0.9 collective-permute-done.25
  77.4 2.0 %collective-permute-done.24 = bf16[16,2048]{1,0:T(8,128)(2,1)S(1)} collective-permute-done((bf16[16,2048]{1,0:T(8,128)(2,1)S(1)}, bf16[16,2048]{1,0:T(8,128)(2,1)S(1)}, u32[]{:S(2)}, u32[]{:S(2)}) %collective-permute-start.24) | collective-permute-done | bytes 65568 | tf_op jit(solution)/shard_map/ppermute | solution.py:31
  79.5 1.7 %collective-permute-start.28 = (bf16[16,2048]{1,0:T(8,128)(2,1)S(1)}, bf16[16,2048]{1,0:T(8,128)(2,1)S(1)}, u32[]{:S(2)}, u32[]{:S(2)}) collective-permute-start(bf16[16,2048]{1,0:T(8,128)(2,1)S(1)} %fusion.3.refs_0_), channel_id=1, source_target_pairs={{0,24},{8,16},{16,8},{24,0},{1,25},{9,17},{17,9},{25,1},{2,26},{10... | collective-permute-start | bytes 196616 | tf_op jit(solution)/shard_map/ppermute | solution.py:31
  81.2 1.1 %collective-permute-start.27 = (bf16[16,2048]{1,0:T(8,128)(2,1)S(1)}, bf16[16,2048]{1,0:T(8,128)(2,1)S(1)}, u32[]{:S(2)}, u32[]{:S(2)}) collective-permute-start(bf16[16,2048]{1,0:T(8,128)(2,1)S(1)} %fusion.3.refs_0_), channel_id=1, source_target_pairs={{0,16},{8,24},{16,0},{24,8},{1,17},{9,25},{17,1},{25,9},{2,18},{10... | collective-permute-start | bytes 196616 | tf_op jit(solution)/shard_map/ppermute | solution.py:31
  82.3 0.7 collective-permute-start.26
  83.0 3.4 %image_product.3 = (bf16[1024,2048]{1,0:T(8,128)(2,1)}, bf16[1024,1024]{1,0:T(8,128)(2,1)}) custom-call(bf16[512,1024]{1,0:T(8,128)(2,1)S(1)} %get-tuple-element.50.x_ref, bf16[2048,1024]{1,0:T(8,128)(2,1)S(1)} %copy-done.1, bf16[512,1024]{1,0:T(8,128)(2,1)S(1)} %get-tuple-element.51.c_ref, ...), custom_call_target="tpu_custom_call", output_to_operand_aliasing={{0}: (3, {}), {1}: (4, {})} | custom-call | flops 2147483648 | bytes 5242880 | tf_op jit(solution)/shard_map/image_product/pallas_call | solution.py:163
  86.4 0.2 collective-permute-done.26.refs_1_
  86.6 1.4 %project.3 = (f32[16,1024]{1,0:T(8,128)S(1)}, f32[16,1024]{1,0:T(8,128)S(1)}, f32[16,1024]{1,0:T(8,128)S(1)}, f32[16,1024]{1,0:T(8,128)S(1)}) custom-call(bf16[16,2048]{1,0:T(8,128)(2,1)S(1)} %fusion.3.refs_0_, bf16[16,2048]{1,0:T(8,128)(2,1)S(1)} %collective-permute-done.26.refs_1_, bf16[16,2048]{1,0:T(8,128)(2,1)S(1)} %collective-permute-done.27.refs_2_, ...), custom_call_target="tpu_custom_call" | custom-call | flops 268435456 | bytes 4194304 | tf_op jit(solution)/shard_map/project/pallas_call | solution.py:61
  88.0 1.2 %collective-permute-start.29 = (f32[16,1024]{1,0:T(8,128)S(1)}, f32[16,1024]{1,0:T(8,128)S(1)}, u32[]{:S(2)}, u32[]{:S(2)}) collective-permute-start(f32[16,1024]{1,0:T(8,128)S(1)} %get-tuple-element.74), channel_id=1, source_target_pairs={{0,8},{8,0},{16,24},{24,16},{1,9},{9,1},{17,25},{25,17},{2,10},{10... | collective-permute-start | bytes 196616 | tf_op jit(solution)/shard_map/ppermute | solution.py:31
  89.2 0.9 collective-permute-start.30
  90.1 1.4 %collective-permute-start.31 = (f32[16,1024]{1,0:T(8,128)S(1)}, f32[16,1024]{1,0:T(8,128)S(1)}, u32[]{:S(2)}, u32[]{:S(2)}) collective-permute-start(f32[16,1024]{1,0:T(8,128)S(1)} %get-tuple-element.76), channel_id=1, source_target_pairs={{0,24},{8,16},{16,8},{24,0},{1,25},{9,17},{17,9},{25,1},{2,26},{10... | collective-permute-start | bytes 196616 | tf_op jit(solution)/shard_map/ppermute | solution.py:31
  91.6 1.1 %collective-permute-done.29 = f32[16,1024]{1,0:T(8,128)S(1)} collective-permute-done((f32[16,1024]{1,0:T(8,128)S(1)}, f32[16,1024]{1,0:T(8,128)S(1)}, u32[]{:S(2)}, u32[]{:S(2)}) %collective-permute-start.29) | collective-permute-done | bytes 65568 | tf_op jit(solution)/shard_map/ppermute | solution.py:31
  92.7 1.2 %collective-permute-done.30 = f32[16,1024]{1,0:T(8,128)S(1)} collective-permute-done((f32[16,1024]{1,0:T(8,128)S(1)}, f32[16,1024]{1,0:T(8,128)S(1)}, u32[]{:S(2)}, u32[]{:S(2)}) %collective-permute-start.30) | collective-permute-done | bytes 65568 | tf_op jit(solution)/shard_map/ppermute | solution.py:31
  94.0 1.3 %collective-permute-done.31 = f32[16,1024]{1,0:T(8,128)S(1)} collective-permute-done((f32[16,1024]{1,0:T(8,128)S(1)}, f32[16,1024]{1,0:T(8,128)S(1)}, u32[]{:S(2)}, u32[]{:S(2)}) %collective-permute-start.31) | collective-permute-done | bytes 65568 | tf_op jit(solution)/shard_map/ppermute | solution.py:31
  95.3 0.7 copy-done.5
  (37 shorter events, 0.3 us)
Async XLA Ops:
  1.5 6.8 %collective-permute-start.2 = (bf16[16,1024]{1,0:T(8,128)(2,1)S(1)}, bf16[16,1024]{1,0:T(8,128)(2,1)S(1)}, u32[]{:S(2)}, u32[]{:S(2)}) collective-permute-start(bf16[16,1024]{1,0:T(8,128)(2,1)S(1)} %get-tuple-element.82), channel_id=1, source_target_pairs={{0,24},{8,16},{16,8},{24,0},{1,25},{9,17},{17,9},{25,1},{2,26},{10... | collective-permute-start | bytes 98312 | tf_op jit(solution)/shard_map/ppermute | solution.py:31
  5.5 3.9 %collective-permute-start = (bf16[16,1024]{1,0:T(8,128)(2,1)S(1)}, bf16[16,1024]{1,0:T(8,128)(2,1)S(1)}, u32[]{:S(2)}, u32[]{:S(2)}) collective-permute-start(bf16[16,1024]{1,0:T(8,128)(2,1)S(1)} %get-tuple-element.83), channel_id=1, source_target_pairs={{0,8},{8,0},{16,24},{24,16},{1,9},{9,1},{17,25},{25,17},{2,10},{10... | collective-permute-start | bytes 98312 | tf_op jit(solution)/shard_map/ppermute | solution.py:31
  6.0 3.9 %collective-permute-start.1 = (bf16[16,1024]{1,0:T(8,128)(2,1)S(1)}, bf16[16,1024]{1,0:T(8,128)(2,1)S(1)}, u32[]{:S(2)}, u32[]{:S(2)}) collective-permute-start(bf16[16,1024]{1,0:T(8,128)(2,1)S(1)} %get-tuple-element.85), channel_id=1, source_target_pairs={{0,16},{8,24},{16,0},{24,8},{1,17},{9,25},{17,1},{25,9},{2,18},{10... | collective-permute-start | bytes 98312 | tf_op jit(solution)/shard_map/ppermute | solution.py:31
  10.8 6.3 %collective-permute-start.3 = (f32[16,2048]{1,0:T(8,128)S(1)}, f32[16,2048]{1,0:T(8,128)S(1)}, u32[]{:S(2)}, u32[]{:S(2)}) collective-permute-start(f32[16,2048]{1,0:T(8,128)S(1)} %get-tuple-element.43), channel_id=1, source_target_pairs={{0,8},{8,0},{16,24},{24,16},{1,9},{9,1},{17,25},{25,17},{2,10},{10... | collective-permute-start | bytes 393224 | tf_op jit(solution)/shard_map/ppermute | solution.py:31
  12.3 7.1 %collective-permute-start.4 = (f32[16,2048]{1,0:T(8,128)S(1)}, f32[16,2048]{1,0:T(8,128)S(1)}, u32[]{:S(2)}, u32[]{:S(2)}) collective-permute-start(f32[16,2048]{1,0:T(8,128)S(1)} %get-tuple-element.44), channel_id=1, source_target_pairs={{0,16},{8,24},{16,0},{24,8},{1,17},{9,25},{17,1},{25,9},{2,18},{10... | collective-permute-start | bytes 393224 | tf_op jit(solution)/shard_map/ppermute | solution.py:31
  12.8 6.6 %collective-permute-start.5 = (f32[16,2048]{1,0:T(8,128)S(1)}, f32[16,2048]{1,0:T(8,128)S(1)}, u32[]{:S(2)}, u32[]{:S(2)}) collective-permute-start(f32[16,2048]{1,0:T(8,128)S(1)} %get-tuple-element.45), channel_id=1, source_target_pairs={{0,24},{8,16},{16,8},{24,0},{1,25},{9,17},{17,9},{25,1},{2,26},{10... | collective-permute-start | bytes 393224 | tf_op jit(solution)/shard_map/ppermute | solution.py:31
  19.5 6.6 %collective-permute-start.8 = (bf16[16,2048]{1,0:T(8,128)(2,1)S(1)}, bf16[16,2048]{1,0:T(8,128)(2,1)S(1)}, u32[]{:S(2)}, u32[]{:S(2)}) collective-permute-start(bf16[16,2048]{1,0:T(8,128)(2,1)S(1)} %add_convert_fusion), channel_id=1, source_target_pairs={{0,6},{1,7},{2,4},{3,5},{4,2},{5,3},{6,0},{7,1},{8,14},{9,15},{10,... | collective-permute-start | bytes 196616 | tf_op jit(solution)/shard_map/ppermute | solution.py:31
  23.2 5.2 %collective-permute-start.7 = (bf16[16,2048]{1,0:T(8,128)(2,1)S(1)}, bf16[16,2048]{1,0:T(8,128)(2,1)S(1)}, u32[]{:S(2)}, u32[]{:S(2)}) collective-permute-start(bf16[16,2048]{1,0:T(8,128)(2,1)S(1)} %add_convert_fusion), channel_id=1, source_target_pairs={{0,4},{1,5},{2,6},{3,7},{4,0},{5,1},{6,2},{7,3},{8,12},{9,13},{10,... | collective-permute-start | bytes 196616 | tf_op jit(solution)/shard_map/ppermute | solution.py:31
  23.2 5.2 %collective-permute-start.6 = (bf16[16,2048]{1,0:T(8,128)(2,1)S(1)}, bf16[16,2048]{1,0:T(8,128)(2,1)S(1)}, u32[]{:S(2)}, u32[]{:S(2)}) collective-permute-start(bf16[16,2048]{1,0:T(8,128)(2,1)S(1)} %add_convert_fusion), channel_id=1, source_target_pairs={{0,2},{1,3},{2,0},{3,1},{4,6},{5,7},{6,4},{7,5},{8,10},{9,11},{10,... | collective-permute-start | bytes 196616 | tf_op jit(solution)/shard_map/ppermute | solution.py:31
  28.4 6.9 %collective-permute-start.9 = (bf16[4,16,2048]{2,1,0:T(8,128)(2,1)S(1)}, bf16[4,16,2048]{2,1,0:T(8,128)(2,1)S(1)}, u32[]{:S(2)}, u32[]{:S(2)}) collective-permute-start(bf16[4,16,2048]{2,1,0:T(8,128)(2,1)S(1)} %pad_maximum_fusion.same_ref), channel_id=1, source_target_pairs={{0,1},{1,0},{2,3},{3,2},{4,5},{5,4},{6,7},{7,6},{8,9},{9,8},{10,11... | collective-permute-start | bytes 786440 | tf_op jit(solution)/shard_map/ppermute | solution.py:31
  28.5 2.2 %copy-start = (bf16[2048,1024]{1,0:T(8,128)(2,1)S(1)}, bf16[2048,1024]{1,0:T(8,128)(2,1)}, u32[]{:S(2)}) copy-start(bf16[2048,1024]{1,0:T(8,128)(2,1)} %w_ref.7) | copy-start | bytes 12582916
  30.7 4.6 %copy-start.3 = (s32[128]{0:T(128)S(1)}, s32[128]{0:T(128)}, u32[]{:S(2)}) copy-start(s32[128]{0:T(128)} %prompt_ref.9) | copy-start | bytes 1540
  36.0 12.7 %collective-permute-start.13 = (bf16[2,16,2048]{2,1,0:T(8,128)(2,1)S(1)}, bf16[2,16,2048]{2,1,0:T(8,128)(2,1)S(1)}, u32[]{:S(2)}, u32[]{:S(2)}) collective-permute-start(bf16[2,16,2048]{2,1,0:T(8,128)(2,1)S(1)} %get-tuple-element.54), channel_id=1, source_target_pairs={{0,8},{8,0},{16,24},{24,16},{1,9},{9,1},{17,25},{25,17},{2,10},{10... | collective-permute-start | bytes 393224 | tf_op jit(solution)/shard_map/ppermute | solution.py:31
  36.3 14.6 %collective-permute-start.14 = (bf16[2,16,2048]{2,1,0:T(8,128)(2,1)S(1)}, bf16[2,16,2048]{2,1,0:T(8,128)(2,1)S(1)}, u32[]{:S(2)}, u32[]{:S(2)}) collective-permute-start(bf16[2,16,2048]{2,1,0:T(8,128)(2,1)S(1)} %get-tuple-element.55), channel_id=1, source_target_pairs={{0,16},{8,24},{16,0},{24,8},{1,17},{9,25},{17,1},{25,9},{2,18},{10... | collective-permute-start | bytes 393224 | tf_op jit(solution)/shard_map/ppermute | solution.py:31
  37.4 13.5 %collective-permute-start.15 = (bf16[2,16,2048]{2,1,0:T(8,128)(2,1)S(1)}, bf16[2,16,2048]{2,1,0:T(8,128)(2,1)S(1)}, u32[]{:S(2)}, u32[]{:S(2)}) collective-permute-start(bf16[2,16,2048]{2,1,0:T(8,128)(2,1)S(1)} %get-tuple-element.56), channel_id=1, source_target_pairs={{0,24},{8,16},{16,8},{24,0},{1,25},{9,17},{17,9},{25,1},{2,26},{10... | collective-permute-start | bytes 393224 | tf_op jit(solution)/shard_map/ppermute | solution.py:31
  44.1 6.7 %copy-start.4 = (s32[8]{0:T(128)S(1)}, s32[8]{0:T(128)}, u32[]{:S(2)}) copy-start(s32[8]{0:T(128)} %len_ref.3) | copy-start | bytes 100
  47.3 7.3 %collective-permute-start.10 = (bf16[2,16,2048]{2,1,0:T(8,128)(2,1)S(1)}, bf16[2,16,2048]{2,1,0:T(8,128)(2,1)S(1)}, u32[]{:S(2)}, u32[]{:S(2)}) collective-permute-start(bf16[2,16,2048]{2,1,0:T(8,128)(2,1)S(1)} %get-tuple-element.47), channel_id=1, source_target_pairs={{0,8},{8,0},{16,24},{24,16},{1,9},{9,1},{17,25},{25,17},{2,10},{10... | collective-permute-start | bytes 393224 | tf_op jit(solution)/shard_map/ppermute | solution.py:31
  47.6 9.2 %collective-permute-start.11 = (bf16[2,16,2048]{2,1,0:T(8,128)(2,1)S(1)}, bf16[2,16,2048]{2,1,0:T(8,128)(2,1)S(1)}, u32[]{:S(2)}, u32[]{:S(2)}) collective-permute-start(bf16[2,16,2048]{2,1,0:T(8,128)(2,1)S(1)} %get-tuple-element.48), channel_id=1, source_target_pairs={{0,16},{8,24},{16,0},{24,8},{1,17},{9,25},{17,1},{25,9},{2,18},{10... | collective-permute-start | bytes 393224 | tf_op jit(solution)/shard_map/ppermute | solution.py:31
  48.7 8.1 %collective-permute-start.12 = (bf16[2,16,2048]{2,1,0:T(8,128)(2,1)S(1)}, bf16[2,16,2048]{2,1,0:T(8,128)(2,1)S(1)}, u32[]{:S(2)}, u32[]{:S(2)}) collective-permute-start(bf16[2,16,2048]{2,1,0:T(8,128)(2,1)S(1)} %get-tuple-element.49), channel_id=1, source_target_pairs={{0,24},{8,16},{16,8},{24,0},{1,25},{9,17},{17,9},{25,1},{2,26},{10... | collective-permute-start | bytes 393224 | tf_op jit(solution)/shard_map/ppermute | solution.py:31
  53.2 19.9 %copy-start.1 = (bf16[2048,1024]{1,0:T(8,128)(2,1)S(1)}, bf16[2048,1024]{1,0:T(8,128)(2,1)}, u32[]{:S(2)}) copy-start(bf16[2048,1024]{1,0:T(8,128)(2,1)} %w_ref.7) | copy-start | bytes 12582916
  53.2 7.4 %collective-permute-start.16 = (bf16[2,16,2048]{2,1,0:T(8,128)(2,1)S(1)}, bf16[2,16,2048]{2,1,0:T(8,128)(2,1)S(1)}, u32[]{:S(2)}, u32[]{:S(2)}) collective-permute-start(bf16[2,16,2048]{2,1,0:T(8,128)(2,1)S(1)} %get-tuple-element.65), channel_id=1, source_target_pairs={{0,8},{8,0},{16,24},{24,16},{1,9},{9,1},{17,25},{25,17},{2,10},{10... | collective-permute-start | bytes 393224 | tf_op jit(solution)/shard_map/ppermute | solution.py:31
  53.5 9.2 %collective-permute-start.18 = (bf16[2,16,2048]{2,1,0:T(8,128)(2,1)S(1)}, bf16[2,16,2048]{2,1,0:T(8,128)(2,1)S(1)}, u32[]{:S(2)}, u32[]{:S(2)}) collective-permute-start(bf16[2,16,2048]{2,1,0:T(8,128)(2,1)S(1)} %get-tuple-element.67), channel_id=1, source_target_pairs={{0,16},{8,24},{16,0},{24,8},{1,17},{9,25},{17,1},{25,9},{2,18},{10... | collective-permute-start | bytes 393224 | tf_op jit(solution)/shard_map/ppermute | solution.py:31
  54.6 8.1 %collective-permute-start.20 = (bf16[2,16,2048]{2,1,0:T(8,128)(2,1)S(1)}, bf16[2,16,2048]{2,1,0:T(8,128)(2,1)S(1)}, u32[]{:S(2)}, u32[]{:S(2)}) collective-permute-start(bf16[2,16,2048]{2,1,0:T(8,128)(2,1)S(1)} %get-tuple-element.69), channel_id=1, source_target_pairs={{0,24},{8,16},{16,8},{24,0},{1,25},{9,17},{17,9},{25,1},{2,26},{10... | collective-permute-start | bytes 393224 | tf_op jit(solution)/shard_map/ppermute | solution.py:31
  59.1 6.0 %collective-permute-start.17 = (bf16[2,16,2048]{2,1,0:T(8,128)(2,1)S(1)}, bf16[2,16,2048]{2,1,0:T(8,128)(2,1)S(1)}, u32[]{:S(2)}, u32[]{:S(2)}) collective-permute-start(bf16[2,16,2048]{2,1,0:T(8,128)(2,1)S(1)} %get-tuple-element.66), channel_id=1, source_target_pairs={{0,8},{8,0},{16,24},{24,16},{1,9},{9,1},{17,25},{25,17},{2,10},{10... | collective-permute-start | bytes 393224 | tf_op jit(solution)/shard_map/ppermute | solution.py:31
  60.0 7.0 %collective-permute-start.19 = (bf16[2,16,2048]{2,1,0:T(8,128)(2,1)S(1)}, bf16[2,16,2048]{2,1,0:T(8,128)(2,1)S(1)}, u32[]{:S(2)}, u32[]{:S(2)}) collective-permute-start(bf16[2,16,2048]{2,1,0:T(8,128)(2,1)S(1)} %get-tuple-element.68), channel_id=1, source_target_pairs={{0,16},{8,24},{16,0},{24,8},{1,17},{9,25},{17,1},{25,9},{2,18},{10... | collective-permute-start | bytes 393224 | tf_op jit(solution)/shard_map/ppermute | solution.py:31
  60.6 6.4 %collective-permute-start.21 = (bf16[2,16,2048]{2,1,0:T(8,128)(2,1)S(1)}, bf16[2,16,2048]{2,1,0:T(8,128)(2,1)S(1)}, u32[]{:S(2)}, u32[]{:S(2)}) collective-permute-start(bf16[2,16,2048]{2,1,0:T(8,128)(2,1)S(1)} %get-tuple-element.70), channel_id=1, source_target_pairs={{0,24},{8,16},{16,8},{24,0},{1,25},{9,17},{17,9},{25,1},{2,26},{10... | collective-permute-start | bytes 393224 | tf_op jit(solution)/shard_map/ppermute | solution.py:31
  67.9 1.6 %collective-permute-start.22 = (bf16[4,16,2048]{2,1,0:T(8,128)(2,1)S(1)}, bf16[4,16,2048]{2,1,0:T(8,128)(2,1)S(1)}, u32[]{:S(2)}, u32[]{:S(2)}) collective-permute-start(bf16[4,16,2048]{2,1,0:T(8,128)(2,1)S(1)} %get-tuple-element.72), channel_id=1, source_target_pairs={{0,1},{1,0},{2,3},{3,2},{4,5},{5,4},{6,7},{7,6},{8,9},{9,8},{10,11... | collective-permute-start | bytes 786440 | tf_op jit(solution)/shard_map/ppermute | solution.py:31
  69.6 6.9 %collective-permute-start.23 = (bf16[16,2048]{1,0:T(8,128)(2,1)S(1)}, bf16[16,2048]{1,0:T(8,128)(2,1)S(1)}, u32[]{:S(2)}, u32[]{:S(2)}) collective-permute-start(bf16[16,2048]{1,0:T(8,128)(2,1)S(1)} %get-tuple-element.79), channel_id=1, source_target_pairs={{0,2},{1,3},{2,0},{3,1},{4,6},{5,7},{6,4},{7,5},{8,10},{9,11},{10,... | collective-permute-start | bytes 196616 | tf_op jit(solution)/shard_map/ppermute | solution.py:31
  70.1 7.3 %collective-permute-start.25 = (bf16[16,2048]{1,0:T(8,128)(2,1)S(1)}, bf16[16,2048]{1,0:T(8,128)(2,1)S(1)}, u32[]{:S(2)}, u32[]{:S(2)}) collective-permute-start(bf16[16,2048]{1,0:T(8,128)(2,1)S(1)} %get-tuple-element.80), channel_id=1, source_target_pairs={{0,6},{1,7},{2,4},{3,5},{4,2},{5,3},{6,0},{7,1},{8,14},{9,15},{10,... | collective-permute-start | bytes 196616 | tf_op jit(solution)/shard_map/ppermute | solution.py:31
  73.1 6.3 %collective-permute-start.24 = (bf16[16,2048]{1,0:T(8,128)(2,1)S(1)}, bf16[16,2048]{1,0:T(8,128)(2,1)S(1)}, u32[]{:S(2)}, u32[]{:S(2)}) collective-permute-start(bf16[16,2048]{1,0:T(8,128)(2,1)S(1)} %get-tuple-element.81), channel_id=1, source_target_pairs={{0,4},{1,5},{2,6},{3,7},{4,0},{5,1},{6,2},{7,3},{8,12},{9,13},{10,... | collective-permute-start | bytes 196616 | tf_op jit(solution)/shard_map/ppermute | solution.py:31
  79.5 6.9 %collective-permute-start.28 = (bf16[16,2048]{1,0:T(8,128)(2,1)S(1)}, bf16[16,2048]{1,0:T(8,128)(2,1)S(1)}, u32[]{:S(2)}, u32[]{:S(2)}) collective-permute-start(bf16[16,2048]{1,0:T(8,128)(2,1)S(1)} %fusion.3.refs_0_), channel_id=1, source_target_pairs={{0,24},{8,16},{16,8},{24,0},{1,25},{9,17},{17,9},{25,1},{2,26},{10... | collective-permute-start | bytes 196616 | tf_op jit(solution)/shard_map/ppermute | solution.py:31
  81.2 5.2 %collective-permute-start.27 = (bf16[16,2048]{1,0:T(8,128)(2,1)S(1)}, bf16[16,2048]{1,0:T(8,128)(2,1)S(1)}, u32[]{:S(2)}, u32[]{:S(2)}) collective-permute-start(bf16[16,2048]{1,0:T(8,128)(2,1)S(1)} %fusion.3.refs_0_), channel_id=1, source_target_pairs={{0,16},{8,24},{16,0},{24,8},{1,17},{9,25},{17,1},{25,9},{2,18},{10... | collective-permute-start | bytes 196616 | tf_op jit(solution)/shard_map/ppermute | solution.py:31
  82.3 4.3 %collective-permute-start.26 = (bf16[16,2048]{1,0:T(8,128)(2,1)S(1)}, bf16[16,2048]{1,0:T(8,128)(2,1)S(1)}, u32[]{:S(2)}, u32[]{:S(2)}) collective-permute-start(bf16[16,2048]{1,0:T(8,128)(2,1)S(1)} %fusion.3.refs_0_), channel_id=1, source_target_pairs={{0,8},{8,0},{16,24},{24,16},{1,9},{9,1},{17,25},{25,17},{2,10},{10... | collective-permute-start | bytes 196616 | tf_op jit(solution)/shard_map/ppermute | solution.py:31
  83.0 3.6 %copy-start.2 = (bf16[1024,2048]{1,0:T(8,128)(2,1)S(1)}, bf16[1024,2048]{1,0:T(8,128)(2,1)}, u32[]{:S(2)}) copy-start(bf16[1024,2048]{1,0:T(8,128)(2,1)} %refs_4_.1) | copy-start | bytes 12582916
  88.0 4.7 %collective-permute-start.29 = (f32[16,1024]{1,0:T(8,128)S(1)}, f32[16,1024]{1,0:T(8,128)S(1)}, u32[]{:S(2)}, u32[]{:S(2)}) collective-permute-start(f32[16,1024]{1,0:T(8,128)S(1)} %get-tuple-element.74), channel_id=1, source_target_pairs={{0,8},{8,0},{16,24},{24,16},{1,9},{9,1},{17,25},{25,17},{2,10},{10... | collective-permute-start | bytes 196616 | tf_op jit(solution)/shard_map/ppermute | solution.py:31
  89.2 4.7 %collective-permute-start.30 = (f32[16,1024]{1,0:T(8,128)S(1)}, f32[16,1024]{1,0:T(8,128)S(1)}, u32[]{:S(2)}, u32[]{:S(2)}) collective-permute-start(f32[16,1024]{1,0:T(8,128)S(1)} %get-tuple-element.75), channel_id=1, source_target_pairs={{0,16},{8,24},{16,0},{24,8},{1,17},{9,25},{17,1},{25,9},{2,18},{10... | collective-permute-start | bytes 196616 | tf_op jit(solution)/shard_map/ppermute | solution.py:31
  90.1 5.2 %collective-permute-start.31 = (f32[16,1024]{1,0:T(8,128)S(1)}, f32[16,1024]{1,0:T(8,128)S(1)}, u32[]{:S(2)}, u32[]{:S(2)}) collective-permute-start(f32[16,1024]{1,0:T(8,128)S(1)} %get-tuple-element.76), channel_id=1, source_target_pairs={{0,24},{8,16},{16,8},{24,0},{1,25},{9,17},{17,9},{25,1},{2,26},{10... | collective-permute-start | bytes 196616 | tf_op jit(solution)/shard_map/ppermute | solution.py:31
  95.3 0.7 copy-start.5
